TPU v7x, 256 devices: a whole 4x4x8 slice. The times are simulated.
256 devices in a mesh: dp: 4 (over y), segment: 8 (over z_hi, x), chan: 8 (over z_lo, core).
Axes of the slice: x: 4, y: 4, z: 8 (z_hi: 2, z_lo: 4; z = z_hi * 4 + z_lo), core: 2. Of those that a mesh axis runs over, the one named last changes fastest.
Arguments:
- x_input: bfloat16 [4, 4, 256, 1024], P(None, 'dp', None, 'chan'), may hold values from -48 to 48
- d_output: bfloat16 [4, 4, 256, 1024], P(None, 'dp', None, 'chan'), may hold values from -6 to 6
- weights: bfloat16 [8, 9, 1024, 1024], P('segment', None, None, 'chan'), may hold values from -0.0625 to 0.0625
- gains: float32 [8, 1024], P('segment', 'chan'), may hold values from 0.5 to 1.5
- biases: float32 [8, 1024], P('segment', 'chan'), may hold values from -3 to 3
Outputs:
- d_weights: float32 [8, 9, 1024, 1024], P('segment', None, None, 'chan')
- d_gains: float32 [8, 1024], P('segment', 'chan')
- d_biases: float32 [8, 1024], P('segment', 'chan')
All inputs are finite; a program needn't handle non-finite values.
Results may differ from a plain program's by a relative error of at most 0.025.
Values may be sent and summed in bfloat16 or wider, within the bound.
No kernel may reach another device: no remote copies, remote signals or barrier semaphores. Data moves between devices by JAX's collectives and lax.ppermute only.
A program may use at most 64 MiB of HBM per device.

v0:
```python
import jax
import jax.numpy as jnp
from jax import lax
from jax.sharding import PartitionSpec as P

GROUPS = 32
SIDE = 16


EPSILON = 1e-05


def shifted(shard, axis, by):
    length = lax.axis_size(axis)
    pairs = [(i, i + by) for i in range(length) if 0 <= i + by < length]
    return lax.ppermute(shard, axis, pairs)


def expand_groups(statistic, group_width):
    return jnp.repeat(statistic, group_width, axis=1)[:, None, :]


def group_sums(values, group_width):
    batch_count, pixel_count, channels = values.shape
    grouped = values.reshape(batch_count, pixel_count, channels // group_width, group_width)
    return jnp.sum(grouped, axis=(1, 3))


def shifted_stack(images, forward_taps):
    batch_count, pixel_count, channels = images.shape
    square = images.reshape(batch_count, SIDE, SIDE, channels)
    padded = jnp.pad(square, ((0, 0), (1, 1), (1, 1), (0, 0)))
    tap_list = []
    for tap_y in range(3):
        for tap_x in range(3):
            start_y = tap_y if forward_taps else 2 - tap_y
            start_x = tap_x if forward_taps else 2 - tap_x
            window = padded[:, start_y : start_y + SIDE, start_x : start_x + SIDE, :]
            tap_list.append(window.reshape(batch_count * pixel_count, channels))
    return jnp.stack(tap_list)


def take_slot(buffer, slot_index):
    return lax.dynamic_index_in_dim(buffer, slot_index, 0, keepdims=False)


def put_slot(buffer, value, slot_index, allowed):
    current = take_slot(buffer, slot_index)
    return lax.dynamic_update_index_in_dim(
        buffer, jnp.where(allowed, value, current), slot_index, 0
    )


def local(x_input, d_output, weights, gains, biases):
    segments = lax.axis_size("segment")
    half_way = segments // 2
    position = lax.axis_index("segment")
    is_down = position < half_way
    level = jnp.where(is_down, position, 2 * half_way - 1 - position)
    weight = weights[0]
    gain_row = gains[0]
    bias_row = biases[0]
    micro_count, images, pixels, local_width = x_input.shape
    full_width = weight.shape[1]
    group_width = full_width // GROUPS
    local_groups = local_width // group_width
    row_count = images * pixels
    group_count = pixels * group_width
    tick_count = micro_count + segments - 1
    bwd_place = 2 * half_way - 1 - position
    act_shape = (images, pixels, local_width)
    below_slot = jnp.clip(position - 1, 0, half_way - 1)
    above_slot = jnp.clip(level + 1, 0, half_way - 1)
    has_above = level < half_way - 1
    before_slot = jnp.clip(level - 1, 0, half_way - 1)

    def normalize(values, group_mean, group_rstd):
        normed = (values - expand_groups(group_mean, group_width)) * expand_groups(
            group_rstd, group_width
        )
        return (normed, normed * gain_row + bias_row)

    def forward_tick(tick_index, loop_state):
        stack_recv, saved_inputs, saved_mean, saved_rstd, saved_full = loop_state
        micro_index = tick_index - position
        active = (micro_index >= 0) & (micro_index < micro_count)
        slot_index = jnp.clip(micro_index, 0, micro_count - 1)
        first_in = jnp.where(
            position == 0, take_slot(x_input, slot_index), take_slot(stack_recv, below_slot)
        )
        skip_part = take_slot(stack_recv, level).astype(jnp.float32)
        upper_part = jnp.where(
            has_above, take_slot(stack_recv, above_slot).astype(jnp.float32), 0.0
        )
        joined = (upper_part + skip_part).astype(jnp.bfloat16)
        inputs = jnp.where(is_down, first_in, joined)
        values = inputs.astype(jnp.float32)
        group_mean = group_sums(values, group_width) / group_count
        centred = values - expand_groups(group_mean, group_width)
        variance = group_sums(centred * centred, group_width) / group_count
        group_rstd = lax.rsqrt(variance + EPSILON)
        normed, pre_act = normalize(values, group_mean, group_rstd)
        hidden = (pre_act * jax.nn.sigmoid(pre_act)).astype(jnp.bfloat16)
        empty_sum = jnp.zeros((row_count, local_width), jnp.float32)
        shard_piece = lax.all_gather(hidden, "chan", axis=2, tiled=True)
        conv_out = lax.cond(
            active,
            lambda: empty_sum
            + jnp.einsum(
                "trc,tco->ro",
                shifted_stack(shard_piece, True),
                weight,
                preferred_element_type=jnp.float32,
            ),
            lambda: empty_sum,
        )
        output = (values + conv_out.reshape(act_shape)).astype(jnp.bfloat16)
        saved_inputs = put_slot(saved_inputs, inputs, slot_index, active)
        saved_mean = put_slot(saved_mean, group_mean, slot_index, active)
        saved_rstd = put_slot(saved_rstd, group_rstd, slot_index, active)
        outgoing = put_slot(stack_recv, output, level, True)
        next_stack = shifted(outgoing, "segment", 1)
        return (next_stack, saved_inputs, saved_mean, saved_rstd, saved_full)

    zero_stack = jnp.zeros((half_way,) + act_shape, jnp.bfloat16)
    zero_buffer = jnp.zeros((micro_count,) + act_shape, jnp.bfloat16)
    zero_stats = jnp.zeros((micro_count, images, local_groups), jnp.float32)
    full_init = jnp.zeros((1,), jnp.bfloat16)
    forward_state = lax.fori_loop(
        0, tick_count, forward_tick, (zero_stack, zero_buffer, zero_stats, zero_stats, full_init)
    )
    saved_inputs, saved_mean, saved_rstd, saved_full = (
        forward_state[1],
        forward_state[2],
        forward_state[3],
        forward_state[4],
    )

    def backward_tick(tick_index, loop_state):
        grad_stack, grad_weight, grad_gain, grad_bias = loop_state
        micro_index = tick_index - bwd_place
        active = (micro_index >= 0) & (micro_index < micro_count)
        slot_index = jnp.clip(micro_index, 0, micro_count - 1)
        own_part = take_slot(grad_stack, level).astype(jnp.float32)
        later_part = jnp.where(
            has_above, take_slot(grad_stack, above_slot).astype(jnp.float32), 0.0
        )
        down_grad = (own_part + later_part).astype(jnp.bfloat16)
        up_grad = jnp.where(
            level == 0, take_slot(d_output, slot_index), take_slot(grad_stack, before_slot)
        )
        grad_out = jnp.where(is_down, down_grad, up_grad)
        values = take_slot(saved_inputs, slot_index).astype(jnp.float32)
        group_mean = take_slot(saved_mean, slot_index)
        group_rstd = take_slot(saved_rstd, slot_index)
        normed, pre_act = normalize(values, group_mean, group_rstd)
        sigma = jax.nn.sigmoid(pre_act)
        grad_rows = grad_out.reshape(row_count, local_width)
        hidden = (pre_act * sigma).astype(jnp.bfloat16)
        shard_piece = lax.all_gather(hidden, "chan", axis=2, tiled=True)
        grad_weight = grad_weight + lax.cond(
            active,
            lambda: jnp.einsum(
                "trc,ro->tco",
                shifted_stack(shard_piece, True),
                grad_rows,
                preferred_element_type=jnp.float32,
            ),
            lambda: jnp.zeros((9, shard_piece.shape[2], local_width), jnp.float32),
        )
        partial_grad = lax.cond(
            active,
            lambda: jnp.einsum(
                "tro,tco->rc",
                shifted_stack(grad_out, False),
                weight,
                preferred_element_type=jnp.float32,
            ),
            lambda: jnp.zeros((row_count, full_width), jnp.float32),
        )
        grad_hidden = lax.psum_scatter(
            partial_grad.reshape(images, pixels, full_width).astype(jnp.bfloat16),
            "chan",
            scatter_dimension=2,
            tiled=True,
        ).astype(jnp.float32)
        grad_pre = grad_hidden * sigma * (1.0 + pre_act * (1.0 - sigma))
        grad_gain = grad_gain + jnp.where(active, jnp.sum(grad_pre * normed, axis=(0, 1)), 0.0)
        grad_bias = grad_bias + jnp.where(active, jnp.sum(grad_pre, axis=(0, 1)), 0.0)
        grad_normed = grad_pre * gain_row
        first_mean = expand_groups(group_sums(grad_normed, group_width) / group_count, group_width)
        second_mean = expand_groups(
            group_sums(grad_normed * normed, group_width) / group_count, group_width
        )
        grad_in = (
            grad_out.astype(jnp.float32)
            + expand_groups(group_rstd, group_width)
            * (grad_normed - first_mean - normed * second_mean)
        ).astype(jnp.bfloat16)
        outgoing = put_slot(grad_stack, grad_in, level, True)
        next_stack = shifted(outgoing, "segment", -1)
        return (next_stack, grad_weight, grad_gain, grad_bias)

    backward_init = (
        zero_stack,
        jnp.zeros(weight.shape, jnp.float32),
        jnp.zeros((local_width,), jnp.float32),
        jnp.zeros((local_width,), jnp.float32),
    )
    backward_state = lax.fori_loop(0, tick_count, backward_tick, backward_init)
    grad_weight, grad_gain, grad_bias = (
        lax.psum(backward_state[1].astype(jnp.bfloat16), "dp").astype(jnp.float32),
        lax.psum(backward_state[2].astype(jnp.bfloat16), "dp").astype(jnp.float32),
        lax.psum(backward_state[3].astype(jnp.bfloat16), "dp").astype(jnp.float32),
    )
    return (grad_weight[None], grad_gain[None], grad_bias[None])


def solution(mesh):
    in_specs = (
        P(None, "dp", None, "chan"),
        P(None, "dp", None, "chan"),
        P("segment", None, None, "chan"),
        P("segment", "chan"),
        P("segment", "chan"),
    )
    out_specs = (P("segment", None, None, "chan"), P("segment", "chan"), P("segment", "chan"))
    return jax.shard_map(local, mesh=mesh, in_specs=in_specs, out_specs=out_specs, check_vma=False)
```

profile of v0, /device:TPU:1, one launch (start us, length us, event | category | flops | bytes accessed | tf_op | source)
XLA Modules:
  0.0 1573.2 jit_solution(6133271358537587081)
XLA Ops:
  8.2 388.7 %while.47 = (s32[]{:T(128)}, bf16[4,1,256,128]{3,2,1,0:T(8,128)(2,1)S(1)}, bf16[4,1,256,128]{3,2,1,0:T(8,128)(2,1)S(1)}, f32[4,1,4]{2,1,0:T(1,128)S(1)}, f32[4,1...) while((s32[]{:T(128)}, ...), condition=%wide.region_7.8_spmd, body=%wide.region_0.7_spmd.sunk | while | flops 604864512 | bytes 33960956 | solution.py:129
  10.7 16.7 %all_gather.25 = bf16[1,256,1024]{2,1,0:T(8,128)(2,1)S(1)} all-gather(bf16[1,256,128]{2,1,0:T(8,128)(2,1)S(1)} %fusion.67), channel_id=1, replica_groups=mesh['dp'=4,'segment'=8,'chan'=8] {'chan'}, dimensions={2}, use_global_device_ids=true | all-gather | bytes 589824 | tf_op jit(solution)/shard_map/while/body/eval_jaxpr/all_gather | solution.py:105
  32.5 5.7 collective-permute-done
  40.8 14.4 all_gather.25
  63.2 5.4 collective-permute-done
  71.2 14.9 all_gather.25
  102.1 14.9 all_gather.25
  132.9 14.9 all_gather.25
  147.8 13.5 collective-permute-start
  169.4 14.9 all_gather.25
  184.3 14.2 collective-permute-start
  206.6 14.9 all_gather.25
  221.5 14.1 collective-permute-start
  243.7 14.9 all_gather.25
  258.6 14.1 collective-permute-start
  280.7 14.9 all_gather.25
  295.7 17.8 %collective-permute-start = (bf16[4,1,256,128]{3,2,1,0:T(8,128)(2,1)S(1)}, bf16[4,1,256,128]{3,2,1,0:T(8,128)(2,1)S(1)}, u32[]{:S(2)}, u32[]{:S(2)}) collective-permute-start(bf16[4,1,256,128]{3,2,1,0:T(8,128)(2,1)S(1)} %fusion.68), channel_id=1, source_target_pairs={{0,8},{8,16},{16,24},{24,32},{32,40},{40,48},{48,56},{1,9},{9,17},... | collective-permute-start | bytes 786440 | tf_op jit(solution)/shard_map/while/body/eval_jaxpr/ppermute | solution.py:16
  321.5 14.9 all_gather.25
  336.5 14.1 collective-permute-start
  358.6 14.9 all_gather.25
  373.6 17.8 %collective-permute-start = (bf16[4,1,256,128]{3,2,1,0:T(8,128)(2,1)S(1)}, bf16[4,1,256,128]{3,2,1,0:T(8,128)(2,1)S(1)}, u32[]{:S(2)}, u32[]{:S(2)}) collective-permute-start(bf16[4,1,256,128]{3,2,1,0:T(8,128)(2,1)S(1)} %fusion.68), channel_id=1, source_target_pairs={{0,8},{8,16},{16,24},{24,32},{32,40},{40,48},{48,56},{1,9},{9,17},... | collective-permute-start | bytes 786440 | tf_op jit(solution)/shard_map/while/body/eval_jaxpr/ppermute | solution.py:16
  397.6 1098.8 %while.48 = (s32[]{:T(128)}, bf16[4,1,256,128]{3,2,1,0:T(8,128)(2,1)}, f32[9,1024,128]{2,1,0:T(8,128)}, f32[128]{0:T(128)S(1)}, f32[128]{0:T(128)S(1)}, /*index=...) while((s32[]{:T(128)}, ...), condition=%wide.region_20.21_spmd.clone, body=%wide.region_8.20_spmd.clone.sunk | while | flops 1211728384 | bytes 62218040 | solution.py:210
  400.9 69.3 %reduce-scatter.6.cloned.1.call-done = bf16[128,256]{1,0:T(8,128)(2,1)} async-done(((bf16[1024,256]{1,0:T(8,128)(2,1)}), bf16[128,256]{1,0:T(8,128)(2,1)}) %reduce-scatter.6.cloned.1.call-update) | async-done | bytes 65552 | tf_op jit(solution)/shard_map/while
  474.1 19.5 %all_gather.26 = bf16[1,256,1024]{2,1,0:T(8,128)(2,1)S(1)} all-gather(bf16[1,256,128]{2,1,0:T(8,128)(2,1)S(1)} %get-tuple-element.1489), channel_id=1, replica_groups=mesh['dp'=4,'segment'=8,'chan'=8] {'chan'}, dimensions={2}, use_global_device_ids=true | all-gather | bytes 589824 | tf_op jit(solution)/shard_map/while/body/eval_jaxpr/all_gather | solution.py:160
  506.2 58.9 %reduce-scatter.6.cloned.1.call-done = bf16[128,256]{1,0:T(8,128)(2,1)} async-done(((bf16[1024,256]{1,0:T(8,128)(2,1)}), bf16[128,256]{1,0:T(8,128)(2,1)}) %reduce-scatter.6.cloned.1.call-update) | async-done | bytes 65552 | tf_op jit(solution)/shard_map/while
  569.0 19.5 %all_gather.26 = bf16[1,256,1024]{2,1,0:T(8,128)(2,1)S(1)} all-gather(bf16[1,256,128]{2,1,0:T(8,128)(2,1)S(1)} %get-tuple-element.1489), channel_id=1, replica_groups=mesh['dp'=4,'segment'=8,'chan'=8] {'chan'}, dimensions={2}, use_global_device_ids=true | all-gather | bytes 589824 | tf_op jit(solution)/shard_map/while/body/eval_jaxpr/all_gather | solution.py:160
  591.0 6.5 select_add_fusion.2
  602.5 58.7 %reduce-scatter.6.cloned.1.call-done = bf16[128,256]{1,0:T(8,128)(2,1)} async-done(((bf16[1024,256]{1,0:T(8,128)(2,1)}), bf16[128,256]{1,0:T(8,128)(2,1)}) %reduce-scatter.6.cloned.1.call-update) | async-done | bytes 65552 | tf_op jit(solution)/shard_map/while
  665.1 19.6 %all_gather.26 = bf16[1,256,1024]{2,1,0:T(8,128)(2,1)S(1)} all-gather(bf16[1,256,128]{2,1,0:T(8,128)(2,1)S(1)} %get-tuple-element.1489), channel_id=1, replica_groups=mesh['dp'=4,'segment'=8,'chan'=8] {'chan'}, dimensions={2}, use_global_device_ids=true | all-gather | bytes 589824 | tf_op jit(solution)/shard_map/while/body/eval_jaxpr/all_gather | solution.py:160
  687.3 6.5 select_add_fusion.2
  698.7 58.8 %reduce-scatter.6.cloned.1.call-done = bf16[128,256]{1,0:T(8,128)(2,1)} async-done(((bf16[1024,256]{1,0:T(8,128)(2,1)}), bf16[128,256]{1,0:T(8,128)(2,1)}) %reduce-scatter.6.cloned.1.call-update) | async-done | bytes 65552 | tf_op jit(solution)/shard_map/while
  761.4 19.6 %all_gather.26 = bf16[1,256,1024]{2,1,0:T(8,128)(2,1)S(1)} all-gather(bf16[1,256,128]{2,1,0:T(8,128)(2,1)S(1)} %get-tuple-element.1489), channel_id=1, replica_groups=mesh['dp'=4,'segment'=8,'chan'=8] {'chan'}, dimensions={2}, use_global_device_ids=true | all-gather | bytes 589824 | tf_op jit(solution)/shard_map/while/body/eval_jaxpr/all_gather | solution.py:160
  783.6 6.5 select_add_fusion.2
  795.1 63.4 %reduce-scatter.6.cloned.1.call-done = bf16[128,256]{1,0:T(8,128)(2,1)} async-done(((bf16[1024,256]{1,0:T(8,128)(2,1)}), bf16[128,256]{1,0:T(8,128)(2,1)}) %reduce-scatter.6.cloned.1.call-update) | async-done | bytes 65552 | tf_op jit(solution)/shard_map/while
  862.4 19.8 %all_gather.26 = bf16[1,256,1024]{2,1,0:T(8,128)(2,1)S(1)} all-gather(bf16[1,256,128]{2,1,0:T(8,128)(2,1)S(1)} %get-tuple-element.1489), channel_id=1, replica_groups=mesh['dp'=4,'segment'=8,'chan'=8] {'chan'}, dimensions={2}, use_global_device_ids=true | all-gather | bytes 589824 | tf_op jit(solution)/shard_map/while/body/eval_jaxpr/all_gather | solution.py:160
  884.7 6.5 select_add_fusion.2
  896.1 63.4 %reduce-scatter.6.cloned.1.call-done = bf16[128,256]{1,0:T(8,128)(2,1)} async-done(((bf16[1024,256]{1,0:T(8,128)(2,1)}), bf16[128,256]{1,0:T(8,128)(2,1)}) %reduce-scatter.6.cloned.1.call-update) | async-done | bytes 65552 | tf_op jit(solution)/shard_map/while
  963.5 19.5 %all_gather.26 = bf16[1,256,1024]{2,1,0:T(8,128)(2,1)S(1)} all-gather(bf16[1,256,128]{2,1,0:T(8,128)(2,1)S(1)} %get-tuple-element.1489), channel_id=1, replica_groups=mesh['dp'=4,'segment'=8,'chan'=8] {'chan'}, dimensions={2}, use_global_device_ids=true | all-gather | bytes 589824 | tf_op jit(solution)/shard_map/while/body/eval_jaxpr/all_gather | solution.py:160
  985.5 6.5 select_add_fusion.2
  997.0 63.4 %reduce-scatter.6.cloned.1.call-done = bf16[128,256]{1,0:T(8,128)(2,1)} async-done(((bf16[1024,256]{1,0:T(8,128)(2,1)}), bf16[128,256]{1,0:T(8,128)(2,1)}) %reduce-scatter.6.cloned.1.call-update) | async-done | bytes 65552 | tf_op jit(solution)/shard_map/while
  1064.3 19.6 %all_gather.26 = bf16[1,256,1024]{2,1,0:T(8,128)(2,1)S(1)} all-gather(bf16[1,256,128]{2,1,0:T(8,128)(2,1)S(1)} %get-tuple-element.1489), channel_id=1, replica_groups=mesh['dp'=4,'segment'=8,'chan'=8] {'chan'}, dimensions={2}, use_global_device_ids=true | all-gather | bytes 589824 | tf_op jit(solution)/shard_map/while/body/eval_jaxpr/all_gather | solution.py:160
  1086.5 6.5 select_add_fusion.2
  1100.7 58.3 %reduce-scatter.6.cloned.1.call-done = bf16[128,256]{1,0:T(8,128)(2,1)} async-done(((bf16[1024,256]{1,0:T(8,128)(2,1)}), bf16[128,256]{1,0:T(8,128)(2,1)}) %reduce-scatter.6.cloned.1.call-update) | async-done | bytes 65552 | tf_op jit(solution)/shard_map/while
  1162.9 19.5 %all_gather.26 = bf16[1,256,1024]{2,1,0:T(8,128)(2,1)S(1)} all-gather(bf16[1,256,128]{2,1,0:T(8,128)(2,1)S(1)} %get-tuple-element.1489), channel_id=1, replica_groups=mesh['dp'=4,'segment'=8,'chan'=8] {'chan'}, dimensions={2}, use_global_device_ids=true | all-gather | bytes 589824 | tf_op jit(solution)/shard_map/while/body/eval_jaxpr/all_gather | solution.py:160
  1182.4 27.5 %conditional.10 = (f32[9,1024,128]{2,1,0:T(8,128)}) conditional(s32[]{:T(128)} %convert_element_type.631, () %tuple.163, (bf16[1,256,1024]{2,1,0:T(8,128)(2,1)S(1)}, pred[]{:T(512)}, pred[]{:T(512)}, bf16[1,1,256,128]{3,2,1,0:T(8,128)(2,1)S(1)}, bf16[1,1,256,128]{3,2,1,0:T(8,128)(2,1)S(1)}, ...), branch_computations={%region_16.16_spmd, %region_17.17_spmd} | conditional | flops 604045312 | bytes 33226762 | solution.py:161
  1204.0 5.9 fusion.18
  1209.9 6.5 select_add_fusion.2
  1224.1 28.5 %reduce-scatter.6.cloned.1.call-done = bf16[128,256]{1,0:T(8,128)(2,1)} async-done(((bf16[1024,256]{1,0:T(8,128)(2,1)}), bf16[128,256]{1,0:T(8,128)(2,1)}) %reduce-scatter.6.cloned.1.call-update) | async-done | bytes 65552 | tf_op jit(solution)/shard_map/while
  1256.4 19.6 %all_gather.26 = bf16[1,256,1024]{2,1,0:T(8,128)(2,1)S(1)} all-gather(bf16[1,256,128]{2,1,0:T(8,128)(2,1)S(1)} %get-tuple-element.1489), channel_id=1, replica_groups=mesh['dp'=4,'segment'=8,'chan'=8] {'chan'}, dimensions={2}, use_global_device_ids=true | all-gather | bytes 589824 | tf_op jit(solution)/shard_map/while/body/eval_jaxpr/all_gather | solution.py:160
  1276.1 27.5 %conditional.10 = (f32[9,1024,128]{2,1,0:T(8,128)}) conditional(s32[]{:T(128)} %convert_element_type.631, () %tuple.163, (bf16[1,256,1024]{2,1,0:T(8,128)(2,1)S(1)}, pred[]{:T(512)}, pred[]{:T(512)}, bf16[1,1,256,128]{3,2,1,0:T(8,128)(2,1)S(1)}, bf16[1,1,256,128]{3,2,1,0:T(8,128)(2,1)S(1)}, ...), branch_computations={%region_16.16_spmd, %region_17.17_spmd} | conditional | flops 604045312 | bytes 33226762 | solution.py:161
  1297.6 5.9 fusion.18
  1303.5 6.5 select_add_fusion.2
  1317.8 27.1 %reduce-scatter.6.cloned.1.call-done = bf16[128,256]{1,0:T(8,128)(2,1)} async-done(((bf16[1024,256]{1,0:T(8,128)(2,1)}), bf16[128,256]{1,0:T(8,128)(2,1)}) %reduce-scatter.6.cloned.1.call-update) | async-done | bytes 65552 | tf_op jit(solution)/shard_map/while
  1348.7 19.6 %all_gather.26 = bf16[1,256,1024]{2,1,0:T(8,128)(2,1)S(1)} all-gather(bf16[1,256,128]{2,1,0:T(8,128)(2,1)S(1)} %get-tuple-element.1489), channel_id=1, replica_groups=mesh['dp'=4,'segment'=8,'chan'=8] {'chan'}, dimensions={2}, use_global_device_ids=true | all-gather | bytes 589824 | tf_op jit(solution)/shard_map/while/body/eval_jaxpr/all_gather | solution.py:160
  1368.4 27.5 %conditional.10 = (f32[9,1024,128]{2,1,0:T(8,128)}) conditional(s32[]{:T(128)} %convert_element_type.631, () %tuple.163, (bf16[1,256,1024]{2,1,0:T(8,128)(2,1)S(1)}, pred[]{:T(512)}, pred[]{:T(512)}, bf16[1,1,256,128]{3,2,1,0:T(8,128)(2,1)S(1)}, bf16[1,1,256,128]{3,2,1,0:T(8,128)(2,1)S(1)}, ...), branch_computations={%region_16.16_spmd, %region_17.17_spmd} | conditional | flops 604045312 | bytes 33226762 | solution.py:161
  1390.0 5.9 fusion.18
  1395.9 6.5 select_add_fusion.2
  1410.1 27.1 %reduce-scatter.6.cloned.1.call-done = bf16[128,256]{1,0:T(8,128)(2,1)} async-done(((bf16[1024,256]{1,0:T(8,128)(2,1)}), bf16[128,256]{1,0:T(8,128)(2,1)}) %reduce-scatter.6.cloned.1.call-update) | async-done | bytes 65552 | tf_op jit(solution)/shard_map/while
  1441.0 19.8 %all_gather.26 = bf16[1,256,1024]{2,1,0:T(8,128)(2,1)S(1)} all-gather(bf16[1,256,128]{2,1,0:T(8,128)(2,1)S(1)} %get-tuple-element.1489), channel_id=1, replica_groups=mesh['dp'=4,'segment'=8,'chan'=8] {'chan'}, dimensions={2}, use_global_device_ids=true | all-gather | bytes 589824 | tf_op jit(solution)/shard_map/while/body/eval_jaxpr/all_gather | solution.py:160
  1460.8 27.5 %conditional.10 = (f32[9,1024,128]{2,1,0:T(8,128)}) conditional(s32[]{:T(128)} %convert_element_type.631, () %tuple.163, (bf16[1,256,1024]{2,1,0:T(8,128)(2,1)S(1)}, pred[]{:T(512)}, pred[]{:T(512)}, bf16[1,1,256,128]{3,2,1,0:T(8,128)(2,1)S(1)}, bf16[1,1,256,128]{3,2,1,0:T(8,128)(2,1)S(1)}, ...), branch_computations={%region_16.16_spmd, %region_17.17_spmd} | conditional | flops 604045312 | bytes 33226762 | solution.py:161
  1482.4 5.9 fusion.18
  1488.3 6.5 select_add_fusion.2
  1500.6 8.8 all-reduce.3
  1510.4 51.4 %all-reduce.6.cloned.1.call-done = bf16[1,9,1024,128]{3,2,1,0:T(8,128)(2,1)} async-done(((bf16[1,9,1024,128]{3,2,1,0:T(8,128)(2,1)}), bf16[1,9,1024,128]{3,2,1,0:T(8,128)(2,1)}) %all-reduce.6.cloned.1.call-update) | async-done | bytes 2359312 | tf_op jit(solution)/shard_map/psum | solution.py:212
  (845 shorter events, 377.2 us)
Async XLA Ops:
  31.2 7.1 collective-permute-start
  59.0 9.6 collective-permute-start
  89.9 9.6 collective-permute-start
  120.7 9.6 collective-permute-start
  147.8 19.0 %collective-permute-start = (bf16[4,1,256,128]{3,2,1,0:T(8,128)(2,1)S(1)}, bf16[4,1,256,128]{3,2,1,0:T(8,128)(2,1)S(1)}, u32[]{:S(2)}, u32[]{:S(2)}) collective-permute-start(bf16[4,1,256,128]{3,2,1,0:T(8,128)(2,1)S(1)} %fusion.68), channel_id=1, source_target_pairs={{0,8},{8,16},{16,24},{24,32},{32,40},{40,48},{48,56},{1,9},{9,17},... | collective-permute-start | bytes 786440 | tf_op jit(solution)/shard_map/while/body/eval_jaxpr/ppermute | solution.py:16
  184.3 19.7 %collective-permute-start = (bf16[4,1,256,128]{3,2,1,0:T(8,128)(2,1)S(1)}, bf16[4,1,256,128]{3,2,1,0:T(8,128)(2,1)S(1)}, u32[]{:S(2)}, u32[]{:S(2)}) collective-permute-start(bf16[4,1,256,128]{3,2,1,0:T(8,128)(2,1)S(1)} %fusion.68), channel_id=1, source_target_pairs={{0,8},{8,16},{16,24},{24,32},{32,40},{40,48},{48,56},{1,9},{9,17},... | collective-permute-start | bytes 786440 | tf_op jit(solution)/shard_map/while/body/eval_jaxpr/ppermute | solution.py:16
  221.5 19.6 %collective-permute-start = (bf16[4,1,256,128]{3,2,1,0:T(8,128)(2,1)S(1)}, bf16[4,1,256,128]{3,2,1,0:T(8,128)(2,1)S(1)}, u32[]{:S(2)}, u32[]{:S(2)}) collective-permute-start(bf16[4,1,256,128]{3,2,1,0:T(8,128)(2,1)S(1)} %fusion.68), channel_id=1, source_target_pairs={{0,8},{8,16},{16,24},{24,32},{32,40},{40,48},{48,56},{1,9},{9,17},... | collective-permute-start | bytes 786440 | tf_op jit(solution)/shard_map/while/body/eval_jaxpr/ppermute | solution.py:16
  258.6 19.6 %collective-permute-start = (bf16[4,1,256,128]{3,2,1,0:T(8,128)(2,1)S(1)}, bf16[4,1,256,128]{3,2,1,0:T(8,128)(2,1)S(1)}, u32[]{:S(2)}, u32[]{:S(2)}) collective-permute-start(bf16[4,1,256,128]{3,2,1,0:T(8,128)(2,1)S(1)} %fusion.68), channel_id=1, source_target_pairs={{0,8},{8,16},{16,24},{24,32},{32,40},{40,48},{48,56},{1,9},{9,17},... | collective-permute-start | bytes 786440 | tf_op jit(solution)/shard_map/while/body/eval_jaxpr/ppermute | solution.py:16
  295.7 23.3 %collective-permute-start = (bf16[4,1,256,128]{3,2,1,0:T(8,128)(2,1)S(1)}, bf16[4,1,256,128]{3,2,1,0:T(8,128)(2,1)S(1)}, u32[]{:S(2)}, u32[]{:S(2)}) collective-permute-start(bf16[4,1,256,128]{3,2,1,0:T(8,128)(2,1)S(1)} %fusion.68), channel_id=1, source_target_pairs={{0,8},{8,16},{16,24},{24,32},{32,40},{40,48},{48,56},{1,9},{9,17},... | collective-permute-start | bytes 786440 | tf_op jit(solution)/shard_map/while/body/eval_jaxpr/ppermute | solution.py:16
  336.5 19.6 %collective-permute-start = (bf16[4,1,256,128]{3,2,1,0:T(8,128)(2,1)S(1)}, bf16[4,1,256,128]{3,2,1,0:T(8,128)(2,1)S(1)}, u32[]{:S(2)}, u32[]{:S(2)}) collective-permute-start(bf16[4,1,256,128]{3,2,1,0:T(8,128)(2,1)S(1)} %fusion.68), channel_id=1, source_target_pairs={{0,8},{8,16},{16,24},{24,32},{32,40},{40,48},{48,56},{1,9},{9,17},... | collective-permute-start | bytes 786440 | tf_op jit(solution)/shard_map/while/body/eval_jaxpr/ppermute | solution.py:16
  373.6 23.3 %collective-permute-start = (bf16[4,1,256,128]{3,2,1,0:T(8,128)(2,1)S(1)}, bf16[4,1,256,128]{3,2,1,0:T(8,128)(2,1)S(1)}, u32[]{:S(2)}, u32[]{:S(2)}) collective-permute-start(bf16[4,1,256,128]{3,2,1,0:T(8,128)(2,1)S(1)} %fusion.68), channel_id=1, source_target_pairs={{0,8},{8,16},{16,24},{24,32},{32,40},{40,48},{48,56},{1,9},{9,17},... | collective-permute-start | bytes 786440 | tf_op jit(solution)/shard_map/while/body/eval_jaxpr/ppermute | solution.py:16
  397.6 74.5 %copy-start.1 = (bf16[4,1,256,128]{3,2,1,0:T(8,128)(2,1)}, bf16[4,1,256,128]{3,2,1,0:T(8,128)(2,1)S(1)}, u32[]{:S(2)}) copy-start(bf16[4,1,256,128]{3,2,1,0:T(8,128)(2,1)S(1)} %get-tuple-element.1623) | copy-start | bytes 786436 | tf_op jit(solution)/shard_map/while
  397.6 72.6 %reduce-scatter.6.cloned.1.call-start = ((), (), s32[]{:S(2)}) async-start(), calls=%async_computation.2 | async-start | bytes 589824 | tf_op jit(solution)/shard_map/while
  398.7 72.5 %copy-start.3 = (f32[1,128]{1,0:T(1,128)S(1)}, f32[1,128]{1,0:T(1,128)}, u32[]{:S(2)}) copy-start(f32[1,128]{1,0:T(1,128)} %get-tuple-element.1625) | copy-start | bytes 1540 | tf_op jit(solution)/shard_map/while
  398.7 72.5 %copy-start.4 = (f32[1,128]{1,0:T(1,128)S(1)}, f32[1,128]{1,0:T(1,128)}, u32[]{:S(2)}) copy-start(f32[1,128]{1,0:T(1,128)} %get-tuple-element.1626) | copy-start | bytes 1540 | tf_op jit(solution)/shard_map/while
  472.8 28.4 %collective-permute-start.1 = (bf16[4,1,256,128]{3,2,1,0:T(8,128)(2,1)}, bf16[4,1,256,128]{3,2,1,0:T(8,128)(2,1)}, u32[]{:S(2)}, u32[]{:S(2)}) collective-permute-start(bf16[4,1,256,128]{3,2,1,0:T(8,128)(2,1)} %fusion.72), channel_id=1, source_target_pairs={{8,0},{16,8},{24,16},{32,24},{40,32},{48,40},{56,48},{9,1},{17,9},... | collective-permute-start | bytes 786440 | tf_op jit(solution)/shard_map/while/body/eval_jaxpr/ppermute | solution.py:16
  502.9 64.2 %copy-start.1 = (bf16[4,1,256,128]{3,2,1,0:T(8,128)(2,1)}, bf16[4,1,256,128]{3,2,1,0:T(8,128)(2,1)S(1)}, u32[]{:S(2)}) copy-start(bf16[4,1,256,128]{3,2,1,0:T(8,128)(2,1)S(1)} %get-tuple-element.1623) | copy-start | bytes 786436 | tf_op jit(solution)/shard_map/while
  502.9 62.2 %reduce-scatter.6.cloned.1.call-start = ((), (), s32[]{:S(2)}) async-start(), calls=%async_computation.2 | async-start | bytes 589824 | tf_op jit(solution)/shard_map/while
  504.0 62.2 %copy-start.3 = (f32[1,128]{1,0:T(1,128)S(1)}, f32[1,128]{1,0:T(1,128)}, u32[]{:S(2)}) copy-start(f32[1,128]{1,0:T(1,128)} %get-tuple-element.1625) | copy-start | bytes 1540 | tf_op jit(solution)/shard_map/while
  504.0 62.2 %copy-start.4 = (f32[1,128]{1,0:T(1,128)S(1)}, f32[1,128]{1,0:T(1,128)}, u32[]{:S(2)}) copy-start(f32[1,128]{1,0:T(1,128)} %get-tuple-element.1626) | copy-start | bytes 1540 | tf_op jit(solution)/shard_map/while
  567.7 29.8 %collective-permute-start.1 = (bf16[4,1,256,128]{3,2,1,0:T(8,128)(2,1)}, bf16[4,1,256,128]{3,2,1,0:T(8,128)(2,1)}, u32[]{:S(2)}, u32[]{:S(2)}) collective-permute-start(bf16[4,1,256,128]{3,2,1,0:T(8,128)(2,1)} %fusion.72), channel_id=1, source_target_pairs={{8,0},{16,8},{24,16},{32,24},{40,32},{48,40},{56,48},{9,1},{17,9},... | collective-permute-start | bytes 786440 | tf_op jit(solution)/shard_map/while/body/eval_jaxpr/ppermute | solution.py:16
  599.2 64.0 %copy-start.1 = (bf16[4,1,256,128]{3,2,1,0:T(8,128)(2,1)}, bf16[4,1,256,128]{3,2,1,0:T(8,128)(2,1)S(1)}, u32[]{:S(2)}) copy-start(bf16[4,1,256,128]{3,2,1,0:T(8,128)(2,1)S(1)} %get-tuple-element.1623) | copy-start | bytes 786436 | tf_op jit(solution)/shard_map/while
  599.2 62.0 %reduce-scatter.6.cloned.1.call-start = ((), (), s32[]{:S(2)}) async-start(), calls=%async_computation.2 | async-start | bytes 589824 | tf_op jit(solution)/shard_map/while
  600.3 62.0 %copy-start.3 = (f32[1,128]{1,0:T(1,128)S(1)}, f32[1,128]{1,0:T(1,128)}, u32[]{:S(2)}) copy-start(f32[1,128]{1,0:T(1,128)} %get-tuple-element.1625) | copy-start | bytes 1540 | tf_op jit(solution)/shard_map/while
  600.3 62.0 %copy-start.4 = (f32[1,128]{1,0:T(1,128)S(1)}, f32[1,128]{1,0:T(1,128)}, u32[]{:S(2)}) copy-start(f32[1,128]{1,0:T(1,128)} %get-tuple-element.1626) | copy-start | bytes 1540 | tf_op jit(solution)/shard_map/while
  663.8 29.9 %collective-permute-start.1 = (bf16[4,1,256,128]{3,2,1,0:T(8,128)(2,1)}, bf16[4,1,256,128]{3,2,1,0:T(8,128)(2,1)}, u32[]{:S(2)}, u32[]{:S(2)}) collective-permute-start(bf16[4,1,256,128]{3,2,1,0:T(8,128)(2,1)} %fusion.72), channel_id=1, source_target_pairs={{8,0},{16,8},{24,16},{32,24},{40,32},{48,40},{56,48},{9,1},{17,9},... | collective-permute-start | bytes 786440 | tf_op jit(solution)/shard_map/while/body/eval_jaxpr/ppermute | solution.py:16
  695.4 64.0 %copy-start.1 = (bf16[4,1,256,128]{3,2,1,0:T(8,128)(2,1)}, bf16[4,1,256,128]{3,2,1,0:T(8,128)(2,1)S(1)}, u32[]{:S(2)}) copy-start(bf16[4,1,256,128]{3,2,1,0:T(8,128)(2,1)S(1)} %get-tuple-element.1623) | copy-start | bytes 786436 | tf_op jit(solution)/shard_map/while
  695.4 62.1 %reduce-scatter.6.cloned.1.call-start = ((), (), s32[]{:S(2)}) async-start(), calls=%async_computation.2 | async-start | bytes 589824 | tf_op jit(solution)/shard_map/while
  696.5 62.0 %copy-start.3 = (f32[1,128]{1,0:T(1,128)S(1)}, f32[1,128]{1,0:T(1,128)}, u32[]{:S(2)}) copy-start(f32[1,128]{1,0:T(1,128)} %get-tuple-element.1625) | copy-start | bytes 1540 | tf_op jit(solution)/shard_map/while
  696.5 62.0 %copy-start.4 = (f32[1,128]{1,0:T(1,128)S(1)}, f32[1,128]{1,0:T(1,128)}, u32[]{:S(2)}) copy-start(f32[1,128]{1,0:T(1,128)} %get-tuple-element.1626) | copy-start | bytes 1540 | tf_op jit(solution)/shard_map/while
  760.1 29.9 %collective-permute-start.1 = (bf16[4,1,256,128]{3,2,1,0:T(8,128)(2,1)}, bf16[4,1,256,128]{3,2,1,0:T(8,128)(2,1)}, u32[]{:S(2)}, u32[]{:S(2)}) collective-permute-start(bf16[4,1,256,128]{3,2,1,0:T(8,128)(2,1)} %fusion.72), channel_id=1, source_target_pairs={{8,0},{16,8},{24,16},{32,24},{40,32},{48,40},{56,48},{9,1},{17,9},... | collective-permute-start | bytes 786440 | tf_op jit(solution)/shard_map/while/body/eval_jaxpr/ppermute | solution.py:16
  791.8 68.6 %copy-start.1 = (bf16[4,1,256,128]{3,2,1,0:T(8,128)(2,1)}, bf16[4,1,256,128]{3,2,1,0:T(8,128)(2,1)S(1)}, u32[]{:S(2)}) copy-start(bf16[4,1,256,128]{3,2,1,0:T(8,128)(2,1)S(1)} %get-tuple-element.1623) | copy-start | bytes 786436 | tf_op jit(solution)/shard_map/while
  791.8 66.7 %reduce-scatter.6.cloned.1.call-start = ((), (), s32[]{:S(2)}) async-start(), calls=%async_computation.2 | async-start | bytes 589824 | tf_op jit(solution)/shard_map/while
  792.8 66.7 %copy-start.3 = (f32[1,128]{1,0:T(1,128)S(1)}, f32[1,128]{1,0:T(1,128)}, u32[]{:S(2)}) copy-start(f32[1,128]{1,0:T(1,128)} %get-tuple-element.1625) | copy-start | bytes 1540 | tf_op jit(solution)/shard_map/while
  792.9 66.7 %copy-start.4 = (f32[1,128]{1,0:T(1,128)S(1)}, f32[1,128]{1,0:T(1,128)}, u32[]{:S(2)}) copy-start(f32[1,128]{1,0:T(1,128)} %get-tuple-element.1626) | copy-start | bytes 1540 | tf_op jit(solution)/shard_map/while
  861.1 30.1 %collective-permute-start.1 = (bf16[4,1,256,128]{3,2,1,0:T(8,128)(2,1)}, bf16[4,1,256,128]{3,2,1,0:T(8,128)(2,1)}, u32[]{:S(2)}, u32[]{:S(2)}) collective-permute-start(bf16[4,1,256,128]{3,2,1,0:T(8,128)(2,1)} %fusion.72), channel_id=1, source_target_pairs={{8,0},{16,8},{24,16},{32,24},{40,32},{48,40},{56,48},{9,1},{17,9},... | collective-permute-start | bytes 786440 | tf_op jit(solution)/shard_map/while/body/eval_jaxpr/ppermute | solution.py:16
  892.8 68.7 %copy-start.1 = (bf16[4,1,256,128]{3,2,1,0:T(8,128)(2,1)}, bf16[4,1,256,128]{3,2,1,0:T(8,128)(2,1)S(1)}, u32[]{:S(2)}) copy-start(bf16[4,1,256,128]{3,2,1,0:T(8,128)(2,1)S(1)} %get-tuple-element.1623) | copy-start | bytes 786436 | tf_op jit(solution)/shard_map/while
  892.8 66.7 %reduce-scatter.6.cloned.1.call-start = ((), (), s32[]{:S(2)}) async-start(), calls=%async_computation.2 | async-start | bytes 589824 | tf_op jit(solution)/shard_map/while
  893.9 66.7 %copy-start.3 = (f32[1,128]{1,0:T(1,128)S(1)}, f32[1,128]{1,0:T(1,128)}, u32[]{:S(2)}) copy-start(f32[1,128]{1,0:T(1,128)} %get-tuple-element.1625) | copy-start | bytes 1540 | tf_op jit(solution)/shard_map/while
  893.9 66.7 %copy-start.4 = (f32[1,128]{1,0:T(1,128)S(1)}, f32[1,128]{1,0:T(1,128)}, u32[]{:S(2)}) copy-start(f32[1,128]{1,0:T(1,128)} %get-tuple-element.1626) | copy-start | bytes 1540 | tf_op jit(solution)/shard_map/while
  962.2 29.8 %collective-permute-start.1 = (bf16[4,1,256,128]{3,2,1,0:T(8,128)(2,1)}, bf16[4,1,256,128]{3,2,1,0:T(8,128)(2,1)}, u32[]{:S(2)}, u32[]{:S(2)}) collective-permute-start(bf16[4,1,256,128]{3,2,1,0:T(8,128)(2,1)} %fusion.72), channel_id=1, source_target_pairs={{8,0},{16,8},{24,16},{32,24},{40,32},{48,40},{56,48},{9,1},{17,9},... | collective-permute-start | bytes 786440 | tf_op jit(solution)/shard_map/while/body/eval_jaxpr/ppermute | solution.py:16
  993.7 68.6 %copy-start.1 = (bf16[4,1,256,128]{3,2,1,0:T(8,128)(2,1)}, bf16[4,1,256,128]{3,2,1,0:T(8,128)(2,1)S(1)}, u32[]{:S(2)}) copy-start(bf16[4,1,256,128]{3,2,1,0:T(8,128)(2,1)S(1)} %get-tuple-element.1623) | copy-start | bytes 786436 | tf_op jit(solution)/shard_map/while
  993.7 66.7 %reduce-scatter.6.cloned.1.call-start = ((), (), s32[]{:S(2)}) async-start(), calls=%async_computation.2 | async-start | bytes 589824 | tf_op jit(solution)/shard_map/while
  994.8 66.6 %copy-start.3 = (f32[1,128]{1,0:T(1,128)S(1)}, f32[1,128]{1,0:T(1,128)}, u32[]{:S(2)}) copy-start(f32[1,128]{1,0:T(1,128)} %get-tuple-element.1625) | copy-start | bytes 1540 | tf_op jit(solution)/shard_map/while
  994.8 66.6 %copy-start.4 = (f32[1,128]{1,0:T(1,128)S(1)}, f32[1,128]{1,0:T(1,128)}, u32[]{:S(2)}) copy-start(f32[1,128]{1,0:T(1,128)} %get-tuple-element.1626) | copy-start | bytes 1540 | tf_op jit(solution)/shard_map/while
  1063.0 29.9 %collective-permute-start.1 = (bf16[4,1,256,128]{3,2,1,0:T(8,128)(2,1)}, bf16[4,1,256,128]{3,2,1,0:T(8,128)(2,1)}, u32[]{:S(2)}, u32[]{:S(2)}) collective-permute-start(bf16[4,1,256,128]{3,2,1,0:T(8,128)(2,1)} %fusion.72), channel_id=1, source_target_pairs={{8,0},{16,8},{24,16},{32,24},{40,32},{48,40},{56,48},{9,1},{17,9},... | collective-permute-start | bytes 786440 | tf_op jit(solution)/shard_map/while/body/eval_jaxpr/ppermute | solution.py:16
  1094.6 66.3 %copy-start.1 = (bf16[4,1,256,128]{3,2,1,0:T(8,128)(2,1)}, bf16[4,1,256,128]{3,2,1,0:T(8,128)(2,1)S(1)}, u32[]{:S(2)}) copy-start(bf16[4,1,256,128]{3,2,1,0:T(8,128)(2,1)S(1)} %get-tuple-element.1623) | copy-start | bytes 786436 | tf_op jit(solution)/shard_map/while
  1094.6 64.3 %reduce-scatter.6.cloned.1.call-start = ((), (), s32[]{:S(2)}) async-start(), calls=%async_computation.2 | async-start | bytes 589824 | tf_op jit(solution)/shard_map/while
  1095.7 64.3 %copy-start.3 = (f32[1,128]{1,0:T(1,128)S(1)}, f32[1,128]{1,0:T(1,128)}, u32[]{:S(2)}) copy-start(f32[1,128]{1,0:T(1,128)} %get-tuple-element.1625) | copy-start | bytes 1540 | tf_op jit(solution)/shard_map/while
  1095.7 64.3 %copy-start.4 = (f32[1,128]{1,0:T(1,128)S(1)}, f32[1,128]{1,0:T(1,128)}, u32[]{:S(2)}) copy-start(f32[1,128]{1,0:T(1,128)} %get-tuple-element.1626) | copy-start | bytes 1540 | tf_op jit(solution)/shard_map/while
  1161.6 54.7 %collective-permute-start.1 = (bf16[4,1,256,128]{3,2,1,0:T(8,128)(2,1)}, bf16[4,1,256,128]{3,2,1,0:T(8,128)(2,1)}, u32[]{:S(2)}, u32[]{:S(2)}) collective-permute-start(bf16[4,1,256,128]{3,2,1,0:T(8,128)(2,1)} %fusion.72), channel_id=1, source_target_pairs={{8,0},{16,8},{24,16},{32,24},{40,32},{48,40},{56,48},{9,1},{17,9},... | collective-permute-start | bytes 786440 | tf_op jit(solution)/shard_map/while/body/eval_jaxpr/ppermute | solution.py:16
  1218.0 36.4 %copy-start.1 = (bf16[4,1,256,128]{3,2,1,0:T(8,128)(2,1)}, bf16[4,1,256,128]{3,2,1,0:T(8,128)(2,1)S(1)}, u32[]{:S(2)}) copy-start(bf16[4,1,256,128]{3,2,1,0:T(8,128)(2,1)S(1)} %get-tuple-element.1623) | copy-start | bytes 786436 | tf_op jit(solution)/shard_map/while
  1218.0 34.5 %reduce-scatter.6.cloned.1.call-start = ((), (), s32[]{:S(2)}) async-start(), calls=%async_computation.2 | async-start | bytes 589824 | tf_op jit(solution)/shard_map/while
  1219.1 34.5 %copy-start.3 = (f32[1,128]{1,0:T(1,128)S(1)}, f32[1,128]{1,0:T(1,128)}, u32[]{:S(2)}) copy-start(f32[1,128]{1,0:T(1,128)} %get-tuple-element.1625) | copy-start | bytes 1540 | tf_op jit(solution)/shard_map/while
  1219.1 34.4 %copy-start.4 = (f32[1,128]{1,0:T(1,128)S(1)}, f32[1,128]{1,0:T(1,128)}, u32[]{:S(2)}) copy-start(f32[1,128]{1,0:T(1,128)} %get-tuple-element.1626) | copy-start | bytes 1540 | tf_op jit(solution)/shard_map/while
  1255.1 54.9 %collective-permute-start.1 = (bf16[4,1,256,128]{3,2,1,0:T(8,128)(2,1)}, bf16[4,1,256,128]{3,2,1,0:T(8,128)(2,1)}, u32[]{:S(2)}, u32[]{:S(2)}) collective-permute-start(bf16[4,1,256,128]{3,2,1,0:T(8,128)(2,1)} %fusion.72), channel_id=1, source_target_pairs={{8,0},{16,8},{24,16},{32,24},{40,32},{48,40},{56,48},{9,1},{17,9},... | collective-permute-start | bytes 786440 | tf_op jit(solution)/shard_map/while/body/eval_jaxpr/ppermute | solution.py:16
  1311.7 35.1 %copy-start.1 = (bf16[4,1,256,128]{3,2,1,0:T(8,128)(2,1)}, bf16[4,1,256,128]{3,2,1,0:T(8,128)(2,1)S(1)}, u32[]{:S(2)}) copy-start(bf16[4,1,256,128]{3,2,1,0:T(8,128)(2,1)S(1)} %get-tuple-element.1623) | copy-start | bytes 786436 | tf_op jit(solution)/shard_map/while
  1311.7 33.1 %reduce-scatter.6.cloned.1.call-start = ((), (), s32[]{:S(2)}) async-start(), calls=%async_computation.2 | async-start | bytes 589824 | tf_op jit(solution)/shard_map/while
  1312.8 33.1 %copy-start.3 = (f32[1,128]{1,0:T(1,128)S(1)}, f32[1,128]{1,0:T(1,128)}, u32[]{:S(2)}) copy-start(f32[1,128]{1,0:T(1,128)} %get-tuple-element.1625) | copy-start | bytes 1540 | tf_op jit(solution)/shard_map/while
  1347.5 54.9 %collective-permute-start.1 = (bf16[4,1,256,128]{3,2,1,0:T(8,128)(2,1)}, bf16[4,1,256,128]{3,2,1,0:T(8,128)(2,1)}, u32[]{:S(2)}, u32[]{:S(2)}) collective-permute-start(bf16[4,1,256,128]{3,2,1,0:T(8,128)(2,1)} %fusion.72), channel_id=1, source_target_pairs={{8,0},{16,8},{24,16},{32,24},{40,32},{48,40},{56,48},{9,1},{17,9},... | collective-permute-start | bytes 786440 | tf_op jit(solution)/shard_map/while/body/eval_jaxpr/ppermute | solution.py:16
  1404.0 35.0 %copy-start.1 = (bf16[4,1,256,128]{3,2,1,0:T(8,128)(2,1)}, bf16[4,1,256,128]{3,2,1,0:T(8,128)(2,1)S(1)}, u32[]{:S(2)}) copy-start(bf16[4,1,256,128]{3,2,1,0:T(8,128)(2,1)S(1)} %get-tuple-element.1623) | copy-start | bytes 786436 | tf_op jit(solution)/shard_map/while
  1404.0 33.1 %reduce-scatter.6.cloned.1.call-start = ((), (), s32[]{:S(2)}) async-start(), calls=%async_computation.2 | async-start | bytes 589824 | tf_op jit(solution)/shard_map/while
  1439.7 55.1 %collective-permute-start.1 = (bf16[4,1,256,128]{3,2,1,0:T(8,128)(2,1)}, bf16[4,1,256,128]{3,2,1,0:T(8,128)(2,1)}, u32[]{:S(2)}, u32[]{:S(2)}) collective-permute-start(bf16[4,1,256,128]{3,2,1,0:T(8,128)(2,1)} %fusion.72), channel_id=1, source_target_pairs={{8,0},{16,8},{24,16},{32,24},{40,32},{48,40},{56,48},{9,1},{17,9},... | collective-permute-start | bytes 786440 | tf_op jit(solution)/shard_map/while/body/eval_jaxpr/ppermute | solution.py:16
  1496.5 65.3 %all-reduce.6.cloned.1.call-start = ((), (), s32[]{:S(2)}) async-start(), calls=%async_computation.1 | async-start | bytes 4718592 | tf_op jit(solution)/shard_map/psum | solution.py:212
  (18 other events, 194.3 us)
Sparse Core Ops, SparseCore 0:
  400.9 69.1 reduce-scatter.5
  506.2 58.8 reduce-scatter.5
  602.5 58.6 reduce-scatter.5
  698.5 58.9 reduce-scatter.5
  794.8 63.5 reduce-scatter.5
  895.9 63.5 reduce-scatter.5
  997.0 63.3 reduce-scatter.5
  1100.4 58.4 reduce-scatter.5
  1223.8 28.6 reduce-scatter.5
  1317.5 27.2 reduce-scatter.5
  1409.8 27.2 reduce-scatter.5
Sparse Core Ops, SparseCore 1:
  1500.7 61.0 all-reduce.5
where the time goes:
time: 1580 us; the launch traced here: 1570 us
  waiting for transfers between devices  688 us (44%)
  blocking collectives  389 us (25%)
  local copies, waits for them, and re-layouts  178 us (11%)
  starting transfers between devices  133 us (8%)
  other arithmetic  126 us (8%)
  matrix products  39.6 us (3%)
    while x22, waiting for transfers between devices  577 us
    all_gather x11, blocking collectives, backward_tick(): shard_piece = lax.all_gather(hidden, 'chan', axis=2, tiled=True)  216 us
    all_gather x11, blocking collectives, forward_tick(): shard_piece = lax.all_gather(hidden, 'chan', axis=2, tiled=True)  165 us
    ppermute x22, starting transfers between devices, shifted(): return lax.ppermute(shard, axis, pairs)  133 us
    add x11, other arithmetic, backward_tick(): grad_weight + lax.cond(active, lambda: jnp.einsum('trc,ro->tco', shifted_...  69.6 us
    ppermute x22, waiting for transfers between devices, shifted(): return lax.ppermute(shard, axis, pairs)  60.2 us
    psum x1, waiting for transfers between devices, local(): lax.psum(backward_state[1].astype(jnp.bfloat16), 'dp').astype(jnp.float32)  51.4 us
    cond x104, local copies, waits for them, and re-layouts  50.2 us
  transfers between devices with their start and end apart: 34, of which 23 were waited for; matrix products, arithmetic and copies ran while one was open for 13% of the time, Pallas kernels for 0%

commit v1 on v0

v1 whole, which is shorter than its diff:
```python
import jax
import jax.numpy as jnp
from jax import lax
from jax.experimental import pallas as pl
from jax.experimental.pallas import tpu as pltpu
from jax.sharding import PartitionSpec as P

GROUPS = 32
SIDE = 16
EPSILON = 1e-05
PIX = SIDE * SIDE
BF = jnp.bfloat16
F32 = jnp.float32


def _groups(width):
    r = lax.broadcasted_iota(jnp.int32, (128, 128), 0) // width
    c = lax.broadcasted_iota(jnp.int32, (128, 128), 1) // width
    return jnp.where(r == c, 1.0, 0.0).astype(BF)


def _group_sum(v, ones):
    n = v.shape[1] // 128
    rows = jnp.concatenate([v[:, i * 128:(i + 1) * 128] for i in range(n)], axis=0)
    hi = rows.astype(BF)
    rest = rows - hi.astype(F32)
    mid = rest.astype(BF)
    low = (rest - mid.astype(F32)).astype(BF)
    out = (jnp.dot(hi, ones, preferred_element_type=F32)
           + jnp.dot(mid, ones, preferred_element_type=F32)
           + jnp.dot(low, ones, preferred_element_type=F32))
    return jnp.concatenate([out[i:i + 1] for i in range(n)], axis=1)


def _normalized(a, count, width):
    ones = _groups(width)
    v = a.astype(F32)
    mean = _group_sum(jnp.sum(v, axis=0, keepdims=True), ones) * (1.0 / count)
    cen = v - mean
    var = _group_sum(jnp.sum(cen * cen, axis=0, keepdims=True), ones) * (1.0 / count)
    rstd = lax.rsqrt(var + EPSILON)
    return cen * rstd, rstd


def _gn_kernel(width, a_ref, gain_ref, bias_ref, h_ref):
    xhat, _ = _normalized(a_ref[...], PIX * width, width)
    n = xhat * gain_ref[...] + bias_ref[...]
    h_ref[...] = (n * jax.nn.sigmoid(n)).astype(BF)


def _prep_kernel(width, a_ref, gain_ref, bias_ref, h_ref, xhat_ref, slope_ref, rstd_ref):
    xhat, rstd = _normalized(a_ref[...], PIX * width, width)
    n = xhat * gain_ref[...] + bias_ref[...]
    s = jax.nn.sigmoid(n)
    h_ref[...] = (n * s).astype(BF)
    xhat_ref[...] = xhat
    slope_ref[...] = s * (1.0 + n * (1.0 - s))
    rstd_ref[...] = rstd


def _gn_bwd_kernel(width, dy_ref, own_ref, oth_ref, xhat_ref, slope_ref, rstd_ref, gain_ref,
                   da_ref, dg_ref, db_ref):
    ones = _groups(width)
    count = PIX * width
    dn = (own_ref[...] + oth_ref[...].astype(F32)) * slope_ref[...]
    xhat = xhat_ref[...]
    gain = gain_ref[...]
    db = jnp.sum(dn, axis=0, keepdims=True)
    dg = jnp.sum(dn * xhat, axis=0, keepdims=True)
    m1 = _group_sum(db * gain, ones) * (1.0 / count)
    m2 = _group_sum(dg * gain, ones) * (1.0 / count)
    da = dy_ref[...].astype(F32) + rstd_ref[...] * (dn * gain - m1 - xhat * m2)
    da_ref[...] = da.astype(BF)
    dg_ref[...] = dg
    db_ref[...] = db


def _pad_into(ref, value):
    zero = jnp.zeros((SIDE, ref.shape[1]), ref.dtype)
    ref[0:SIDE, :] = zero
    ref[SIDE:SIDE + PIX, :] = value
    ref[SIDE + PIX:, :] = zero


def _join_shifts(left, mid, right):
    x = lax.broadcasted_iota(jnp.int32, mid.shape, 0) % SIDE
    out = mid + jnp.where(x > 0, pltpu.roll(left, 1, 0), 0.0)
    return out + jnp.where(x < SIDE - 1, pltpu.roll(right, PIX - 1, 0), 0.0)


def _conv_kernel(own_ref, oth_ref, a_ref, w_ref, y_ref, hp_ref, hq_ref, acc_ref):
    t = pl.program_id(0)

    @pl.when(t == 0)
    def _():
        _pad_into(hp_ref, own_ref[...])
        _pad_into(hq_ref, oth_ref[...])

    ky = t // 3
    kx = t % 3
    half = own_ref.shape[1]
    row = pl.multiple_of(ky * SIDE, SIDE)
    part = (jnp.dot(hp_ref[pl.ds(row, PIX), :], w_ref[0, :half, :], preferred_element_type=F32)
            + jnp.dot(hq_ref[pl.ds(row, PIX), :], w_ref[0, half:, :], preferred_element_type=F32))

    @pl.when(ky == 0)
    def _():
        acc_ref[kx] = part

    @pl.when(ky > 0)
    def _():
        acc_ref[kx] += part

    @pl.when(t == 8)
    def _():
        z = _join_shifts(acc_ref[0], acc_ref[1], acc_ref[2])
        y_ref[...] = (a_ref[...].astype(F32) + z).astype(BF)


def _dgrad_kernel(dy_ref, w_ref, own_ref, oth_ref, dp_ref, acc_ref):
    t = pl.program_id(0)

    @pl.when(t == 0)
    def _():
        _pad_into(dp_ref, dy_ref[...])

    ky = t // 3
    kx = t % 3
    half = dy_ref.shape[1]
    row = pl.multiple_of((2 - ky) * SIDE, SIDE)
    part = lax.dot_general(dp_ref[pl.ds(row, PIX), :], w_ref[0], (((1,), (1,)), ((), ())),
                           preferred_element_type=F32)

    @pl.when(ky == 0)
    def _():
        acc_ref[kx] = part

    @pl.when(ky > 0)
    def _():
        acc_ref[kx] += part

    @pl.when(t == 8)
    def _():
        p = _join_shifts(acc_ref[2], acc_ref[1], acc_ref[0])
        own_ref[...] = p[:, :half]
        oth_ref[...] = p[:, half:].astype(BF)


def _dw_kernel(ht_ref, dy_ref, out_ref, pad_ref, rhs_ref):
    step = pl.program_id(0)
    count = dy_ref.shape[0]
    x = lax.broadcasted_iota(jnp.int32, (PIX, 128), 0) % SIDE
    for i in range(count):
        v = dy_ref[i].astype(F32)
        moved = (jnp.where(x < SIDE - 1, pltpu.roll(v, PIX - 1, 0), 0.0), v,
                 jnp.where(x > 0, pltpu.roll(v, 1, 0), 0.0))
        for kx in range(3):
            _pad_into(pad_ref.at[kx], moved[kx].astype(BF))
        for t in range(9):
            start = (2 - t // 3) * SIDE
            rhs_ref[i * PIX:(i + 1) * PIX, t * 128:(t + 1) * 128] = pad_ref[t % 3, start:start + PIX, :]

    for lo, taps in ((0, 2), (2, 2), (4, 2), (6, 2), (8, 1)):
        part = jnp.dot(ht_ref[...], rhs_ref[:, lo * 128:(lo + taps) * 128], preferred_element_type=F32)
        for i in range(taps):
            piece = part[:, i * 128:(i + 1) * 128]

            @pl.when(step == 0)
            def _():
                out_ref[lo + i] = piece

            @pl.when(step > 0)
            def _():
                out_ref[lo + i] += piece


def _assemble_kernel(idx_ref, w0, w1, w2, w3, out_ref, sem):
    copies = []
    for r, src in enumerate((w0, w1, w2, w3)):
        for z in range(4):
            for side in range(2):
                copies.append(pltpu.make_async_copy(
                    src.at[z, :, side],
                    out_ref.at[:, idx_ref[4 + side], idx_ref[r], :, pl.ds(z * 128, 128)],
                    sem.at[(r * 4 + z) * 2 + side]))
    for c in copies:
        c.start()
    for c in copies:
        c.wait()


def local(x_input, d_output, weights, gains, biases):
    row = lax.axis_index("dp")
    segment = lax.axis_index("segment")
    chan = lax.axis_index("chan")
    core = chan % 2
    width = weights.shape[2] // GROUPS
    half = 4 * 128
    ZG = [[0, 2, 4, 6], [1, 3, 5, 7]]
    axes = ("dp", "segment", "chan")

    def lin(d, s, k):
        return (d * 8 + s) * 8 + k

    def move(value, source, target):
        flip = (source < 4) != (target < 4)
        pairs = [(lin(d, source, k), lin(d, target, (6 - k + 2 * (k % 2)) if flip else k))
                 for d in range(4) for k in range(8)]
        return lax.ppermute(value, axes, pairs)

    def swap(value, seg):
        pairs = [(lin(d, seg, k), lin(d, seg, k ^ 1)) for d in range(4) for k in range(8)]
        return lax.ppermute(value, axes, pairs)

    def swap_all(value):
        return lax.ppermute(value, "chan", [(k, k ^ 1) for k in range(8)])

    def turn(value, by):
        return lax.ppermute(value, "dp", [(i, (i + by) % 4) for i in range(4)])

    def scatter_z(value):
        return lax.all_to_all(value, "chan", 0, 0, axis_index_groups=ZG, tiled=True)

    def flat(blocks):
        return jnp.transpose(blocks, (1, 0, 2)).reshape(PIX, half)

    def unflat(value):
        return jnp.transpose(value.reshape(PIX, 4, 128), (1, 0, 2))

    quarter = lax.dynamic_slice_in_dim(weights[0], row * 256, 256, 1)
    wz = scatter_z(jnp.broadcast_to(quarter[None], (4,) + quarter.shape))
    below = turn(wz, 1)
    above = turn(wz, -1)
    across = jnp.concatenate([turn(below[:2], 1), turn(above[2:], -1)], axis=0)
    pieces = [p.reshape(4, 9, 2, 128, 128) for p in (wz, above, across, below)]
    places = jnp.concatenate([(row + jnp.arange(4)) % 4, (core + jnp.arange(2)) % 2]).astype(jnp.int32)
    anyspec = pl.BlockSpec(memory_space=pl.ANY)
    w = pl.pallas_call(
        _assemble_kernel,
        out_shape=jax.ShapeDtypeStruct((9, 2, 4, 128, half), BF),
        grid_spec=pltpu.PrefetchScalarGridSpec(
            num_scalar_prefetch=1, grid=(), in_specs=[anyspec] * 4, out_specs=anyspec,
            scratch_shapes=[pltpu.SemaphoreType.DMA((32,))]),
        name="assemble",
    )(places, *pieces).reshape(9, 2 * half, half)

    rows = jnp.concatenate([gains, biases], axis=0)
    rows = scatter_z(jnp.broadcast_to(rows[None], (4, 2, 128)))
    rows = jnp.transpose(rows, (1, 0, 2)).reshape(2, half)
    gain = rows[0:1]
    bias = rows[1:2]

    act = jax.ShapeDtypeStruct((PIX, half), BF)
    act32 = jax.ShapeDtypeStruct((PIX, half), F32)
    line = jax.ShapeDtypeStruct((1, half), F32)

    def normed(a):
        return pl.pallas_call(lambda *r: _gn_kernel(width, *r), out_shape=act, name="gn")(a, gain, bias)

    def prep(a):
        return pl.pallas_call(lambda *r: _prep_kernel(width, *r), out_shape=(act, act32, act32, line),
                              name="prep")(a, gain, bias)

    full = pl.BlockSpec((PIX, half), lambda t: (0, 0))
    wspec = pl.BlockSpec((1, 2 * half, half), lambda t: (t, 0, 0))

    def conv(own, oth, a):
        return pl.pallas_call(
            _conv_kernel, grid=(9,), in_specs=[full, full, full, wspec], out_specs=full, out_shape=act,
            scratch_shapes=[pltpu.VMEM((PIX + 2 * SIDE, half), BF), pltpu.VMEM((PIX + 2 * SIDE, half), BF),
                            pltpu.VMEM((3, PIX, half), F32)],
            name="conv")(own, oth, a, w)

    def dgrad(dy):
        return pl.pallas_call(
            _dgrad_kernel, grid=(9,), in_specs=[full, wspec], out_specs=(full, full), out_shape=(act32, act),
            scratch_shapes=[pltpu.VMEM((PIX + 2 * SIDE, half), BF), pltpu.VMEM((3, PIX, 2 * half), F32)],
            name="dgrad")(dy, w)

    def added(p, q):
        return (p.astype(F32) + q.astype(F32)).astype(BF)

    first = flat(scatter_z(x_input[:, 0]))
    a = jnp.where(segment == 0, first, jnp.zeros_like(first))
    inputs = [a]
    skips = {}
    for j in range(7):
        own = normed(a)
        y = conv(own, swap(own, j), a)
        if j < 3:
            skips[j] = move(y, j, 7 - j)
        a = move(y, j, j + 1)
        if j >= 4:
            a = added(a, skips[6 - j])
        inputs.append(a)
    mine = inputs[0]
    for a in inputs[1:]:
        mine = mine + a

    hidden, xhat, slope, rstd = prep(mine)

    last = flat(scatter_z(d_output[::-1, 0]))
    dy = jnp.where(segment == 7, last, jnp.zeros_like(last))
    grads = []
    gain_sum = bias_sum = 0.0
    skip_grads = {}
    h_turned = None
    for j in reversed(range(8)):
        if j == 3:
            hidden, dy = lax.optimization_barrier((hidden, dy))
            hz = scatter_z(jnp.broadcast_to(hidden[None], (4, PIX, half)))
            hall = jnp.concatenate([hz, turn(hz, -1), turn(hz, 2), turn(hz, 1)], axis=0)
            hoth = swap_all(hall)
            pair = jnp.stack([jnp.where(core == 0, hall, hoth), jnp.where(core == 0, hoth, hall)])
            pair = pair.reshape(2, 16 * PIX, 4, 128)
            h_turned = jnp.transpose(pair, (2, 0, 3, 1)).reshape(2 * half, 16 * PIX)
            h_turned, dy = lax.optimization_barrier((h_turned, dy))
        grads.append(dy)
        own, oth = dgrad(dy)
        da, dg, db = pl.pallas_call(
            lambda *r: _gn_bwd_kernel(width, *r), out_shape=(act, line, line), name="gn_bwd",
        )(dy, own, swap(oth, j), xhat, slope, rstd, gain)
        gain_sum = gain_sum + dg
        bias_sum = bias_sum + db
        if j > 4:
            skip_grads[7 - j] = move(da, j, 7 - j)
        if j > 0:
            dy = move(da, j, j - 1)
            if j - 1 < 3:
                dy = added(dy, skip_grads[j - 1])

    mine = grads[0]
    for g in grads[1:]:
        mine = mine + g
    dz = scatter_z(unflat(mine))
    dall = jnp.concatenate([dz, turn(dz, -1), turn(dz, 2), turn(dz, 1)], axis=0)
    grad_weight = pl.pallas_call(
        _dw_kernel, grid=(4,),
        in_specs=[pl.BlockSpec((2 * half, 4 * PIX), lambda i: (0, i)),
                  pl.BlockSpec((4, PIX, 128), lambda i: (i, 0, 0))],
        out_specs=pl.BlockSpec((9, 2 * half, 128), lambda i: (0, 0, 0)),
        out_shape=jax.ShapeDtypeStruct((9, 2 * half, 128), F32),
        scratch_shapes=[pltpu.VMEM((3, PIX + 2 * SIDE, 128), BF), pltpu.VMEM((4 * PIX, 9 * 128), BF)],
        name="dw")(h_turned, dall)

    small = jnp.concatenate([gain_sum, bias_sum], axis=0).reshape(2, 4, 128)
    small = jnp.sum(scatter_z(jnp.transpose(small, (1, 0, 2))), axis=0)
    small = lax.psum(small, "dp")
    return (grad_weight[None], small[0:1], small[1:2])


def solution(mesh):
    in_specs = (
        P(None, "dp", None, "chan"),
        P(None, "dp", None, "chan"),
        P("segment", None, None, "chan"),
        P("segment", "chan"),
        P("segment", "chan"),
    )
    out_specs = (P("segment", None, None, "chan"), P("segment", "chan"), P("segment", "chan"))
    return jax.shard_map(local, mesh=mesh, in_specs=in_specs, out_specs=out_specs, check_vma=False)
```

time: 1580 us -> 1030 us (0.65)
  Pallas kernels: 0 us -> 508 us
  waiting for transfers between devices: 688 us -> 258 us
  blocking collectives: 389 us -> 105 us
  local copies, waits for them, and re-layouts: 178 us -> 62.8 us
  other arithmetic: 126 us -> 25 us
  starting transfers between devices: 133 us -> 60.9 us
  matrix products: 39.6 us -> 0 us
    while x22 -> x0, waiting for transfers between devices: 577 us -> none
    pallas_call x0 -> x33, Pallas kernels: none -> 508 us  [the longest x1 288 us: local(): pl.pallas_call(_assemble_kernel, out_shape=jax.ShapeDtypeStruct((9, 2, 4,...]
    all_gather x22 -> x0, blocking collectives: 381 us -> none  [the longest x11 216 us: backward_tick(): shard_piece = lax.all_gather(hidden, 'chan', axis=2, tiled=True)]
    ppermute x22 -> x46, waiting for transfers between devices: 60.2 us -> 244 us  [the longest x20 144 us: move(): return lax.ppermute(value, axes, pairs)]
    all_to_all x0 -> x3, blocking collectives: none -> 96 us  [scatter_z(): return lax.all_to_all(value, 'chan', 0, 0, axis_index_groups=ZG, tiled=True)]
    ppermute x22 -> x46, starting transfers between devices: 133 us -> 46.4 us  [the longest x15 18.4 us: swap(): return lax.ppermute(value, axes, pairs)]
    add x22 -> x2, other arithmetic: 69.8 us -> 1.72 us  [the longest x1 1.03 us: local(): mine = mine + a]
    psum x1 -> x0, waiting for transfers between devices: 51.4 us -> none  [local(): lax.psum(backward_state[1].astype(jnp.bfloat16), 'dp').astype(jnp.float32)]
  transfers between devices with their start and end apart: 34 -> 50, of which waited for: 23 -> 11; matrix products, arithmetic and copies ran while one was open for 13% -> 2% of each run, Pallas kernels for 0% -> 34%
where the time goes in v1:
time: 1030 us; the launch traced here: 1020 us
  Pallas kernels  508 us (49%)
  waiting for transfers between devices  258 us (25%)
  blocking collectives  105 us (10%)
  local copies, waits for them, and re-layouts  62.8 us (6%)
  starting transfers between devices  60.9 us (6%)
  other arithmetic  25 us (2%)
    pallas_call x1, Pallas kernels, local(): pl.pallas_call(_assemble_kernel, out_shape=jax.ShapeDtypeStruct((9, 2, 4,...  288 us
    ppermute x20, waiting for transfers between devices, move(): return lax.ppermute(value, axes, pairs)  144 us
    all_to_all x3, blocking collectives, scatter_z(): return lax.all_to_all(value, 'chan', 0, 0, axis_index_groups=ZG, tiled=True)  96 us
    ppermute x10, waiting for transfers between devices, turn(): return lax.ppermute(value, 'dp', [(i, (i + by) % 4) for i in range(4)])  92.7 us
    pallas_call x8, Pallas kernels, dgrad(): pl.pallas_call(_dgrad_kernel, grid=(9,), in_specs=[full, wspec], out_spec...  82 us
    pallas_call x7, Pallas kernels, conv(): pl.pallas_call(_conv_kernel, grid=(9,), in_specs=[full, full, full, wspec...  68.5 us
    pallas_call x1, Pallas kernels, local(): pl.pallas_call(_dw_kernel, grid=(4,), in_specs=[pl.BlockSpec((2 * half, 4...  29.5 us
    unnamed x131, local copies, waits for them, and re-layouts  21.9 us
  transfers between devices with their start and end apart: 50, of which 11 were waited for; matrix products, arithmetic and copies ran while one was open for 2% of the time, Pallas kernels for 34%

profile of v1, /device:TPU:1, one launch (start us, length us, event | category | flops | bytes accessed | tf_op | source)
XLA Modules:
  0.0 1021.2 jit_solution(11092352010446402232)
XLA Ops:
  2.9 59.2 %all_to_all.35 = bf16[4,9,256,128]{3,2,1,0:T(8,128)(2,1)S(1)} all-to-all(bf16[4,9,256,128]{3,2,1,0:T(8,128)(2,1)S(1)} %broadcast_in_dim.12), channel_id=1, replica_groups={{0,2,4,6},{1,3,5,7},{8,10,12,14},{9,11,13,15},{16,18,20,22},{17,19,21,2..., dimensions={0} | all-to-all | bytes 4718592 | tf_op jit(solution)/shard_map/all_to_all | solution.py:222
  63.6 2.7 collective-permute-start.1
  66.3 48.2 %collective-permute-done.2 = bf16[4,9,256,128]{3,2,1,0:T(8,128)(2,1)S(1)} collective-permute-done((bf16[4,9,256,128]{3,2,1,0:T(8,128)(2,1)S(1)}, bf16[4,9,256,128]{3,2,1,0:T(8,128)(2,1)S(1)}, u32[]{:S(2)}, u32[]{:S(2)}) %collective-permute-start.2) | collective-permute-done | bytes 2359328 | tf_op jit(solution)/shard_map/ppermute | solution.py:219
  118.3 2.8 collective-permute-start.4
  121.7 3.9 all-to-all-start.1
  125.6 4.4 all-to-all-done.1
  130.0 3.4 all-to-all-start
  134.0 5.4 all-to-all-done
  140.1 2.3 gn.7.own_ref
  142.4 6.5 collective-permute-start
  149.5 3.2 pad_maximum_fusion
  152.7 287.9 %assemble.1 = bf16[9,2,4,128,512]{4,3,2,1,0:T(8,128)(2,1)} custom-call(s32[6]{0:T(128)} %pad_add_fusion.idx_ref, bf16[4,9,2,128,128]{4,3,2,1,0:T(8,128)(2,1)} %bitcast.69, bf16[4,9,2,128,128]{4,3,2,1,0:T(8,128)(2,1)} %bitcast.72, bf16[4,9,2,128,128]{4,3,2,1,0:T(8,128)(2,1)} %bitcast.70, bf16[4,9,2,128,128]{4,3,2,1,0:T(8,128)(2,1)} %bitcast.71), custom_call_target="tpu_custom_call" | custom-call | tf_op jit(solution)/shard_map/assemble/pallas_call | solution.py:238
  441.4 9.8 conv.7
  452.4 5.3 collective-permute-done.5.r_0_.a_ref
  458.5 2.3 gn.8.own_ref
  462.2 9.8 conv.8
  473.4 2.3 gn.9.own_ref
  477.0 9.8 conv.9
  488.2 2.3 gn.10.own_ref
  492.0 9.8 conv.10
  503.1 2.3 gn.11.own_ref
  507.6 9.8 conv.11
  518.9 2.3 gn.12.own_ref
  523.4 9.8 conv.12
  534.6 3.9 all-to-all-start.3
  539.3 2.3 gn.13.own_ref
  544.3 9.8 conv.13
  555.6 10.4 %dgrad.8 = (f32[256,512]{1,0:T(8,128)}, bf16[256,512]{1,0:T(8,128)(2,1)}) custom-call(bf16[256,512]{1,0:T(8,128)(2,1)} %copy_bitcast_fusion.dy_ref.r_0_, bf16[9,1024,512]{2,1,0:T(8,128)(2,1)} %bitcast.60), custom_call_target="tpu_custom_call" | custom-call | tf_op jit(solution)/shard_map/dgrad/pallas_call | solution.py:275
  567.7 2.6 prep.1
  571.0 2.7 gn_bwd.8
  575.1 10.2 dgrad.9
  586.7 2.7 gn_bwd.9
  590.9 10.2 %dgrad.10 = (f32[256,512]{1,0:T(8,128)}, bf16[256,512]{1,0:T(8,128)(2,1)}) custom-call(bf16[256,512]{1,0:T(8,128)(2,1)} %copy-done.11, bf16[9,1024,512]{2,1,0:T(8,128)(2,1)} %bitcast.62), custom_call_target="tpu_custom_call" | custom-call | tf_op jit(solution)/shard_map/dgrad/pallas_call | solution.py:275
  602.5 2.7 gn_bwd.10
  606.7 10.2 dgrad.11
  618.3 2.7 gn_bwd.11
  621.9 29.1 %all_to_all.36 = bf16[4,256,512]{1,2,0:T(8,128)(2,1)S(1)} all-to-all(bf16[4,256,512]{1,2,0:T(8,128)(2,1)S(1)} %broadcast_in_dim.26), channel_id=1, replica_groups={{0,2,4,6},{1,3,5,7},{8,10,12,14},{9,11,13,15},{16,18,20,22},{17,19,21,2..., dimensions={0} | all-to-all | bytes 2097152 | tf_op jit(solution)/shard_map/all_to_all | solution.py:222
  653.6 20.3 %collective-permute-done.29 = bf16[4,256,512]{1,2,0:T(8,128)(2,1)S(1)} collective-permute-done((bf16[4,256,512]{1,2,0:T(8,128)(2,1)S(1)}, bf16[4,256,512]{1,2,0:T(8,128)(2,1)S(1)}, u32[]{:S(2)}, u32[]{:S(2)}) %collective-permute-start.29) | collective-permute-done | bytes 1048608 | tf_op jit(solution)/shard_map/ppermute | solution.py:219
  676.5 23.6 %collective-permute-done.31 = bf16[4,256,512]{1,2,0:T(8,128)(2,1)S(1)} collective-permute-done((bf16[4,256,512]{1,2,0:T(8,128)(2,1)S(1)}, bf16[4,256,512]{1,2,0:T(8,128)(2,1)S(1)}, u32[]{:S(2)}, u32[]{:S(2)}) %collective-permute-start.31) | collective-permute-done | bytes 1048608 | tf_op jit(solution)/shard_map/ppermute | solution.py:219
  701.8 7.1 collective-permute-done.32
  708.9 5.1 broadcast_select_fusion.1
  714.0 4.4 copy.20
  718.4 7.4 stack.9
  725.8 6.5 copy.21
  732.3 7.4 stack.10
  739.6 7.6 maximum_bitcast_fusion
  747.3 7.8 copy.22
  755.1 10.2 %dgrad.12 = (f32[256,512]{1,0:T(8,128)}, bf16[256,512]{1,0:T(8,128)(2,1)}) custom-call(bf16[256,512]{1,0:T(8,128)(2,1)} %copy-done.15, bf16[9,1024,512]{2,1,0:T(8,128)(2,1)} %bitcast.64), custom_call_target="tpu_custom_call" | custom-call | tf_op jit(solution)/shard_map/dgrad/pallas_call | solution.py:275
  767.4 2.7 gn_bwd.12
  771.6 10.2 %dgrad.13 = (f32[256,512]{1,0:T(8,128)}, bf16[256,512]{1,0:T(8,128)(2,1)}) custom-call(bf16[256,512]{1,0:T(8,128)(2,1)} %add_convert_fusion.2.dy_ref.r_0_, bf16[9,1024,512]{2,1,0:T(8,128)(2,1)} %bitcast.65), custom_call_target="tpu_custom_call" | custom-call | tf_op jit(solution)/shard_map/dgrad/pallas_call | solution.py:275
  783.9 2.7 gn_bwd.13
  788.1 10.3 %dgrad.14 = (f32[256,512]{1,0:T(8,128)}, bf16[256,512]{1,0:T(8,128)(2,1)}) custom-call(bf16[256,512]{1,0:T(8,128)(2,1)} %add_convert_fusion.1.dy_ref.r_0_, bf16[9,1024,512]{2,1,0:T(8,128)(2,1)} %bitcast.66), custom_call_target="tpu_custom_call" | custom-call | tf_op jit(solution)/shard_map/dgrad/pallas_call | solution.py:275
  801.2 2.7 gn_bwd.14
  805.4 79.0 %collective-permute-done.41 = bf16[256,512]{1,0:T(8,128)(2,1)S(1)} collective-permute-done((bf16[256,512]{1,0:T(8,128)(2,1)S(1)}, bf16[256,512]{1,0:T(8,128)(2,1)S(1)}, u32[]{:S(2)}, u32[]{:S(2)}) %collective-permute-start.41) | collective-permute-done | bytes 262176 | tf_op jit(solution)/shard_map/ppermute | solution.py:209
  884.4 59.9 %collective-permute-done.40 = bf16[256,512]{1,0:T(8,128)(2,1)S(1)} collective-permute-done((bf16[256,512]{1,0:T(8,128)(2,1)}, bf16[256,512]{1,0:T(8,128)(2,1)S(1)}, u32[]{:S(2)}, u32[]{:S(2)}) %collective-permute-start.40) | collective-permute-done | bytes 262176 | tf_op jit(solution)/shard_map/ppermute | solution.py:209
  945.4 10.2 %dgrad.15 = (f32[256,512]{1,0:T(8,128)}, bf16[256,512]{1,0:T(8,128)(2,1)}) custom-call(bf16[256,512]{1,0:T(8,128)(2,1)} %get-tuple-element.98.dy_ref.r_0_, bf16[9,1024,512]{2,1,0:T(8,128)(2,1)} %bitcast.67), custom_call_target="tpu_custom_call" | custom-call | tf_op jit(solution)/shard_map/dgrad/pallas_call | solution.py:275
  955.6 2.8 collective-permute-start.45
  959.2 3.4 all-to-all-start.5
  963.4 2.7 gn_bwd.15
  966.9 3.8 all-to-all-done.5
  970.7 2.9 collective-permute-start.43
  973.5 7.6 all_to_all.37
  981.1 8.7 psum.7
  991.5 29.5 %dw.1 = f32[9,1024,128]{2,1,0:T(8,128)} custom-call(bf16[1024,4096]{1,0:T(8,128)(2,1)} %bitcast.68, bf16[16,256,128]{2,1,0:T(8,128)(2,1)} %pad_maximum_fusion.1.dy_ref), custom_call_target="tpu_custom_call" | custom-call | tf_op jit(solution)/shard_map/dw/pallas_call | solution.py:337
  (240 shorter events, 67.6 us)
Async XLA Ops:
  2.9 118.2 %copy-start.59 = (f32[1,128]{1,0:T(1,128)S(1)}, f32[1,128]{1,0:T(1,128)}, u32[]{:S(2)}) copy-start(f32[1,128]{1,0:T(1,128)} %param.9) | copy-start | bytes 1540
  2.9 118.2 %copy-start.60 = (f32[1,128]{1,0:T(1,128)S(1)}, f32[1,128]{1,0:T(1,128)}, u32[]{:S(2)}) copy-start(f32[1,128]{1,0:T(1,128)} %param.8) | copy-start | bytes 1540
  62.2 52.4 %collective-permute-start.2 = (bf16[4,9,256,128]{3,2,1,0:T(8,128)(2,1)S(1)}, bf16[4,9,256,128]{3,2,1,0:T(8,128)(2,1)S(1)}, u32[]{:S(2)}, u32[]{:S(2)}) collective-permute-start(bf16[4,9,256,128]{3,2,1,0:T(8,128)(2,1)S(1)} %all_to_all.35), channel_id=1, source_target_pairs={{0,64},{64,128},{128,192},{192,0},{1,65},{65,129},{129,193},{193,1... | collective-permute-start | bytes 7077896 | tf_op jit(solution)/shard_map/ppermute | solution.py:219
  63.6 52.2 %collective-permute-start.1 = (bf16[4,9,256,128]{3,2,1,0:T(8,128)(2,1)S(1)}, bf16[4,9,256,128]{3,2,1,0:T(8,128)(2,1)S(1)}, u32[]{:S(2)}, u32[]{:S(2)}) collective-permute-start(bf16[4,9,256,128]{3,2,1,0:T(8,128)(2,1)S(1)} %all_to_all.35), channel_id=1, source_target_pairs={{0,192},{64,0},{128,64},{192,128},{1,193},{65,1},{129,65},{193,129... | collective-permute-start | bytes 7077896 | tf_op jit(solution)/shard_map/ppermute | solution.py:219
  114.5 38.2 %copy-start.3 = (bf16[4,9,256,128]{3,2,1,0:T(8,128)(2,1)}, bf16[4,9,256,128]{3,2,1,0:T(8,128)(2,1)S(1)}, u32[]{:S(2)}) copy-start(bf16[4,9,256,128]{3,2,1,0:T(8,128)(2,1)S(1)} %collective-permute-done.2) | copy-start | bytes 7077892
  115.8 33.7 %collective-permute-start.3 = (bf16[2,9,256,128]{3,2,1,0:T(8,128)(2,1)}, bf16[2,9,256,128]{3,2,1,0:T(8,128)(2,1)}, u32[]{:S(2)}, u32[]{:S(2)}) collective-permute-start(bf16[2,9,256,128]{3,2,1,0:T(8,128)(2,1)} %slice.34), channel_id=1, source_target_pairs={{0,64},{64,128},{128,192},{192,0},{1,65},{65,129},{129,193},{193,1... | collective-permute-start | bytes 3538952 | tf_op jit(solution)/shard_map/ppermute | solution.py:219
  118.3 31.1 %collective-permute-start.4 = (bf16[2,9,256,128]{3,2,1,0:T(8,128)(2,1)}, bf16[2,9,256,128]{3,2,1,0:T(8,128)(2,1)}, u32[]{:S(2)}, u32[]{:S(2)}) collective-permute-start(bf16[2,9,256,128]{3,2,1,0:T(8,128)(2,1)} %slice.35), channel_id=1, source_target_pairs={{0,192},{64,0},{128,64},{192,128},{1,193},{65,1},{129,65},{193,129... | collective-permute-start | bytes 3538952 | tf_op jit(solution)/shard_map/ppermute | solution.py:219
  121.7 8.3 all-to-all-start.1
  130.0 9.4 all-to-all-start
  142.4 298.3 %collective-permute-start = (bf16[256,512]{1,0:T(8,128)(2,1)}, bf16[256,512]{1,0:T(8,128)(2,1)S(1)}, u32[]{:S(2)}, u32[]{:S(2)}) collective-permute-start(bf16[256,512]{1,0:T(8,128)(2,1)} %gn.7.own_ref), channel_id=1, source_target_pairs={{0,1},{1,0},{2,3},{3,2},{4,5},{5,4},{6,7},{7,6},{64,65},{65,64},{6... | collective-permute-start | bytes 786440 | tf_op jit(solution)/shard_map/ppermute | solution.py:213
  451.1 6.7 collective-permute-start.5
  460.8 0.7 collective-permute-start.6
  472.0 0.7 collective-permute-start.7
  475.6 0.7 collective-permute-start.8
  486.8 0.7 collective-permute-start.9
  490.4 0.8 collective-permute-start.10
  501.7 0.7 collective-permute-start.11
  505.4 1.5 collective-permute-start.12
  506.2 11.9 %collective-permute-start.14 = (bf16[256,512]{1,0:T(8,128)(2,1)S(1)}, bf16[256,512]{1,0:T(8,128)(2,1)S(1)}, u32[]{:S(2)}, u32[]{:S(2)}) collective-permute-start(bf16[256,512]{1,0:T(8,128)(2,1)S(1)} %copy-done.27), channel_id=1, source_target_pairs={{16,46},{17,47},{18,44},{19,45},{20,42},{21,43},{22,40},{23,41},{8... | collective-permute-start | bytes 786440 | tf_op jit(solution)/shard_map/ppermute | solution.py:209
  517.4 0.7 collective-permute-start.13
  521.2 21.1 %copy-start.25 = (bf16[256,512]{1,0:T(8,128)(2,1)S(1)}, bf16[256,512]{1,0:T(8,128)(2,1)}, u32[]{:S(2)}) copy-start(bf16[256,512]{1,0:T(8,128)(2,1)} %conv.7) | copy-start | bytes 786436
  521.2 1.5 collective-permute-start.15
  522.0 16.5 %collective-permute-start.17 = (bf16[256,512]{1,0:T(8,128)(2,1)S(1)}, bf16[256,512]{1,0:T(8,128)(2,1)S(1)}, u32[]{:S(2)}, u32[]{:S(2)}) collective-permute-start(bf16[256,512]{1,0:T(8,128)(2,1)S(1)} %copy-done.26), channel_id=1, source_target_pairs={{8,54},{9,55},{10,52},{11,53},{12,50},{13,51},{14,48},{15,49},{72,... | collective-permute-start | bytes 786440 | tf_op jit(solution)/shard_map/ppermute | solution.py:209
  533.2 5.3 collective-permute-start.16
  534.6 20.1 %all-to-all-start.3 = ((bf16[4,256,128]{2,1,0:T(8,128)(2,1)}), bf16[4,256,128]{2,1,0:T(8,128)(2,1)S(1)}, u32[]{:S(2)}, u32[]{:S(2)}) async-start(bf16[4,256,128]{2,1,0:T(8,128)(2,1)} %reverse_bitcast_fusion), calls=%async_computation.3 | async-start | bytes 524288 | tf_op jit(solution)/shard_map/all_to_all | solution.py:222
  541.6 2.0 collective-permute-start.18
  542.3 24.3 %collective-permute-start.20 = (bf16[256,512]{1,0:T(8,128)(2,1)S(1)}, bf16[256,512]{1,0:T(8,128)(2,1)S(1)}, u32[]{:S(2)}, u32[]{:S(2)}) collective-permute-start(bf16[256,512]{1,0:T(8,128)(2,1)S(1)} %copy-done.25), channel_id=1, source_target_pairs={{0,62},{1,63},{2,60},{3,61},{4,58},{5,59},{6,56},{7,57},{64,126},{... | collective-permute-start | bytes 786440 | tf_op jit(solution)/shard_map/ppermute | solution.py:209
  554.1 12.5 %collective-permute-start.19 = (bf16[256,512]{1,0:T(8,128)(2,1)}, bf16[256,512]{1,0:T(8,128)(2,1)S(1)}, u32[]{:S(2)}, u32[]{:S(2)}) collective-permute-start(bf16[256,512]{1,0:T(8,128)(2,1)} %conv.13), channel_id=1, source_target_pairs={{48,56},{49,57},{50,58},{51,59},{52,60},{53,61},{54,62},{55,63},{1... | collective-permute-start | bytes 786440 | tf_op jit(solution)/shard_map/ppermute | solution.py:209
  565.9 4.3 collective-permute-start.21
  573.7 0.7 collective-permute-start.22
  585.3 0.7 collective-permute-start.23
  589.5 0.7 collective-permute-start.24
  601.1 0.7 collective-permute-start.25
  605.2 0.8 collective-permute-start.26
  616.9 0.7 collective-permute-start.27
  621.0 0.7 collective-permute-start.28
  621.7 54.8 %copy-start.15 = (bf16[256,512]{1,0:T(8,128)(2,1)}, bf16[256,512]{1,0:T(8,128)(2,1)S(1)}, u32[]{:S(2)}) copy-start(bf16[256,512]{1,0:T(8,128)(2,1)S(1)} %collective-permute-done.28.dy_ref.r_0_) | copy-start | bytes 786436
  651.0 22.8 %collective-permute-start.29 = (bf16[4,256,512]{1,2,0:T(8,128)(2,1)S(1)}, bf16[4,256,512]{1,2,0:T(8,128)(2,1)S(1)}, u32[]{:S(2)}, u32[]{:S(2)}) collective-permute-start(bf16[4,256,512]{1,2,0:T(8,128)(2,1)S(1)} %all_to_all.36), channel_id=1, source_target_pairs={{0,192},{64,0},{128,64},{192,128},{1,193},{65,1},{129,65},{193,129... | collective-permute-start | bytes 3145736 | tf_op jit(solution)/shard_map/ppermute | solution.py:219
  651.0 24.4 %collective-permute-start.30 = (bf16[4,256,512]{1,2,0:T(8,128)(2,1)S(1)}, bf16[4,256,512]{1,2,0:T(8,128)(2,1)S(1)}, u32[]{:S(2)}, u32[]{:S(2)}) collective-permute-start(bf16[4,256,512]{1,2,0:T(8,128)(2,1)S(1)} %all_to_all.36), channel_id=1, source_target_pairs={{0,128},{64,192},{128,0},{192,64},{1,129},{65,193},{129,1},{193,65... | collective-permute-start | bytes 3145736 | tf_op jit(solution)/shard_map/ppermute | solution.py:219
  651.0 49.1 %collective-permute-start.31 = (bf16[4,256,512]{1,2,0:T(8,128)(2,1)S(1)}, bf16[4,256,512]{1,2,0:T(8,128)(2,1)S(1)}, u32[]{:S(2)}, u32[]{:S(2)}) collective-permute-start(bf16[4,256,512]{1,2,0:T(8,128)(2,1)S(1)} %all_to_all.36), channel_id=1, source_target_pairs={{0,64},{64,128},{128,192},{192,0},{1,65},{65,129},{129,193},{193,1... | collective-permute-start | bytes 3145736 | tf_op jit(solution)/shard_map/ppermute | solution.py:219
  701.1 7.8 collective-permute-start.32
  765.3 1.4 collective-permute-start.33
  766.0 4.8 collective-permute-start.35
  770.1 0.7 collective-permute-start.34
  781.8 1.4 collective-permute-start.36
  782.5 4.8 collective-permute-start.38
  786.6 0.7 collective-permute-start.37
  788.1 156.2 %copy-start.5 = (bf16[256,512]{1,0:T(8,128)(2,1)S(1)}, bf16[256,512]{1,0:T(8,128)(2,1)}, u32[]{:S(2)}) copy-start(bf16[256,512]{1,0:T(8,128)(2,1)} %add_convert_fusion.2.dy_ref.r_0_) | copy-start | bytes 786436
  788.1 156.2 %copy-start.6 = (bf16[256,512]{1,0:T(8,128)(2,1)S(1)}, bf16[256,512]{1,0:T(8,128)(2,1)}, u32[]{:S(2)}) copy-start(bf16[256,512]{1,0:T(8,128)(2,1)} %add_convert_fusion.1.dy_ref.r_0_) | copy-start | bytes 786436
  788.1 156.2 %copy-start.10 = (bf16[256,512]{1,0:T(8,128)(2,1)S(1)}, bf16[256,512]{1,0:T(8,128)(2,1)}, u32[]{:S(2)}) copy-start(bf16[256,512]{1,0:T(8,128)(2,1)} %copy-done.9) | copy-start | bytes 786436
  788.1 156.2 %copy-start.12 = (bf16[256,512]{1,0:T(8,128)(2,1)S(1)}, bf16[256,512]{1,0:T(8,128)(2,1)}, u32[]{:S(2)}) copy-start(bf16[256,512]{1,0:T(8,128)(2,1)} %copy-done.11) | copy-start | bytes 786436
  788.1 156.2 %copy-start.14 = (bf16[256,512]{1,0:T(8,128)(2,1)S(1)}, bf16[256,512]{1,0:T(8,128)(2,1)}, u32[]{:S(2)}) copy-start(bf16[256,512]{1,0:T(8,128)(2,1)} %copy-done.13) | copy-start | bytes 786436
  788.1 156.2 %copy-start.16 = (bf16[256,512]{1,0:T(8,128)(2,1)S(1)}, bf16[256,512]{1,0:T(8,128)(2,1)}, u32[]{:S(2)}) copy-start(bf16[256,512]{1,0:T(8,128)(2,1)} %copy-done.15) | copy-start | bytes 786436
  798.4 2.0 collective-permute-start.39
  799.1 85.2 %collective-permute-start.41 = (bf16[256,512]{1,0:T(8,128)(2,1)S(1)}, bf16[256,512]{1,0:T(8,128)(2,1)S(1)}, u32[]{:S(2)}, u32[]{:S(2)}) collective-permute-start(bf16[256,512]{1,0:T(8,128)(2,1)S(1)} %copy-done.61), channel_id=1, source_target_pairs={{56,6},{57,7},{58,4},{59,5},{60,2},{61,3},{62,0},{63,1},{120,70},{... | collective-permute-start | bytes 786440 | tf_op jit(solution)/shard_map/ppermute | solution.py:209
  803.9 140.3 %collective-permute-start.40 = (bf16[256,512]{1,0:T(8,128)(2,1)}, bf16[256,512]{1,0:T(8,128)(2,1)S(1)}, u32[]{:S(2)}, u32[]{:S(2)}) collective-permute-start(bf16[256,512]{1,0:T(8,128)(2,1)} %get-tuple-element.78), channel_id=1, source_target_pairs={{8,0},{9,1},{10,2},{11,3},{12,4},{13,5},{14,6},{15,7},{72,64},{73,... | collective-permute-start | bytes 786440 | tf_op jit(solution)/shard_map/ppermute | solution.py:209
  945.3 20.8 %copy-start.49 = (f32[1,512]{1,0:T(1,128)S(1)}, f32[1,512]{1,0:T(1,128)}, u32[]{:S(2)}) copy-start(f32[1,512]{1,0:T(1,128)} %get-tuple-element.81) | copy-start | bytes 6148
  945.3 20.8 %copy-start.50 = (f32[1,512]{1,0:T(1,128)S(1)}, f32[1,512]{1,0:T(1,128)}, u32[]{:S(2)}) copy-start(f32[1,512]{1,0:T(1,128)} %get-tuple-element.91) | copy-start | bytes 6148
  955.6 7.0 collective-permute-start.45
  959.2 11.4 %all-to-all-start.5 = ((bf16[4,256,128]{2,1,0:T(8,128)(2,1)}), bf16[4,256,128]{2,1,0:T(8,128)(2,1)S(1)}, u32[]{:S(2)}, u32[]{:S(2)}) async-start(bf16[4,256,128]{2,1,0:T(8,128)(2,1)} %bitcast.52), calls=%async_computation.5 | async-start | bytes 524288 | tf_op jit(solution)/shard_map/all_to_all | solution.py:222
  970.7 19.7 %collective-permute-start.44 = (bf16[4,256,128]{2,1,0:T(8,128)(2,1)S(1)}, bf16[4,256,128]{2,1,0:T(8,128)(2,1)S(1)}, u32[]{:S(2)}, u32[]{:S(2)}) collective-permute-start(bf16[4,256,128]{2,1,0:T(8,128)(2,1)S(1)} %all-to-all-done.5), channel_id=1, source_target_pairs={{0,64},{64,128},{128,192},{192,0},{1,65},{65,129},{129,193},{193,1... | collective-permute-start | bytes 786440 | tf_op jit(solution)/shard_map/ppermute | solution.py:219
  970.7 19.7 %collective-permute-start.43 = (bf16[4,256,128]{2,1,0:T(8,128)(2,1)S(1)}, bf16[4,256,128]{2,1,0:T(8,128)(2,1)S(1)}, u32[]{:S(2)}, u32[]{:S(2)}) collective-permute-start(bf16[4,256,128]{2,1,0:T(8,128)(2,1)S(1)} %all-to-all-done.5), channel_id=1, source_target_pairs={{0,128},{64,192},{128,0},{192,64},{1,129},{65,193},{129,1},{193,65... | collective-permute-start | bytes 786440 | tf_op jit(solution)/shard_map/ppermute | solution.py:219
  973.5 16.8 %collective-permute-start.42 = (bf16[4,256,128]{2,1,0:T(8,128)(2,1)S(1)}, bf16[4,256,128]{2,1,0:T(8,128)(2,1)S(1)}, u32[]{:S(2)}, u32[]{:S(2)}) collective-permute-start(bf16[4,256,128]{2,1,0:T(8,128)(2,1)S(1)} %all-to-all-done.5), channel_id=1, source_target_pairs={{0,192},{64,0},{128,64},{192,128},{1,193},{65,1},{129,65},{193,129... | collective-permute-start | bytes 786440 | tf_op jit(solution)/shard_map/ppermute | solution.py:219
  990.3 30.6 %copy-start.1 = (bf16[1,9,1024,128]{3,2,1,0:T(8,128)(2,1)S(1)}, bf16[1,9,1024,128]{3,2,1,0:T(8,128)(2,1)}, u32[]{:S(2)}) copy-start(bf16[1,9,1024,128]{3,2,1,0:T(8,128)(2,1)} %param.7) | copy-start | bytes 7077892
  (50 other events, 430.5 us)

commit v2 on v1

v2 whole, which is shorter than its diff:
```python
import jax
import jax.numpy as jnp
from jax import lax
from jax.experimental import pallas as pl
from jax.experimental.pallas import tpu as pltpu
from jax.sharding import PartitionSpec as P


GROUPS = 32
SIDE = 16
EPSILON = 1e-05
PIX = SIDE * SIDE
BF = jnp.bfloat16
F32 = jnp.float32


def _groups(width):
    r = lax.broadcasted_iota(jnp.int32, (128, 128), 0) // width
    c = lax.broadcasted_iota(jnp.int32, (128, 128), 1) // width
    return jnp.where(r == c, 1.0, 0.0).astype(BF)


def _group_sum(v, ones):
    n = v.shape[1] // 128
    rows = jnp.concatenate([v[:, i * 128:(i + 1) * 128] for i in range(n)], axis=0)
    hi = rows.astype(BF)
    rest = rows - hi.astype(F32)
    mid = rest.astype(BF)
    low = (rest - mid.astype(F32)).astype(BF)
    out = (jnp.dot(hi, ones, preferred_element_type=F32)
           + jnp.dot(mid, ones, preferred_element_type=F32)
           + jnp.dot(low, ones, preferred_element_type=F32))
    return jnp.concatenate([out[i:i + 1] for i in range(n)], axis=1)


def _normalized(a, count, width):
    ones = _groups(width)
    v = a.astype(F32)
    mean = _group_sum(jnp.sum(v, axis=0, keepdims=True), ones) * (1.0 / count)
    cen = v - mean
    var = _group_sum(jnp.sum(cen * cen, axis=0, keepdims=True), ones) * (1.0 / count)
    rstd = lax.rsqrt(var + EPSILON)
    return cen * rstd, rstd


def _gn_kernel(width, a_ref, gain_ref, bias_ref, h_ref):
    xhat, _ = _normalized(a_ref[...], PIX * width, width)
    n = xhat * gain_ref[...] + bias_ref[...]
    h_ref[...] = (n * jax.nn.sigmoid(n)).astype(BF)


def _prep_kernel(width, a_ref, gain_ref, bias_ref, h_ref, xhat_ref, slope_ref, rstd_ref):
    xhat, rstd = _normalized(a_ref[...], PIX * width, width)
    n = xhat * gain_ref[...] + bias_ref[...]
    s = jax.nn.sigmoid(n)
    h_ref[...] = (n * s).astype(BF)
    xhat_ref[...] = xhat
    slope_ref[...] = s * (1.0 + n * (1.0 - s))
    rstd_ref[...] = rstd


def _gn_bwd_kernel(width, dy_ref, own_ref, oth_ref, xhat_ref, slope_ref, rstd_ref, gain_ref,
                   da_ref, dg_ref, db_ref):
    ones = _groups(width)
    count = PIX * width
    dn = (own_ref[...] + oth_ref[...].astype(F32)) * slope_ref[...]
    xhat = xhat_ref[...]
    gain = gain_ref[...]
    db = jnp.sum(dn, axis=0, keepdims=True)
    dg = jnp.sum(dn * xhat, axis=0, keepdims=True)
    m1 = _group_sum(db * gain, ones) * (1.0 / count)
    m2 = _group_sum(dg * gain, ones) * (1.0 / count)
    da = dy_ref[...].astype(F32) + rstd_ref[...] * (dn * gain - m1 - xhat * m2)
    da_ref[...] = da.astype(BF)
    dg_ref[...] = dg
    db_ref[...] = db


def _pad_into(ref, value):
    zero = jnp.zeros((SIDE, ref.shape[1]), ref.dtype)
    ref[0:SIDE, :] = zero
    ref[SIDE:SIDE + PIX, :] = value
    ref[SIDE + PIX:, :] = zero


def _join_shifts(left, mid, right):
    x = lax.broadcasted_iota(jnp.int32, mid.shape, 0) % SIDE
    out = mid + jnp.where(x > 0, pltpu.roll(left, 1, 0), 0.0)
    return out + jnp.where(x < SIDE - 1, pltpu.roll(right, PIX - 1, 0), 0.0)


def _cat_into(ref, col, value, turn):
    wide = value.shape[1]
    zero = jnp.zeros((SIDE, wide), value.dtype)
    for ky in range(3):
        lo = ky * (ref.shape[1] // 3) + col
        by = (ky - 1) * turn
        if by == 0:
            ref[:, lo:lo + wide] = value
        elif by < 0:
            ref[0:SIDE, lo:lo + wide] = zero
            ref[SIDE:, lo:lo + wide] = value[:PIX - SIDE]
        else:
            ref[0:PIX - SIDE, lo:lo + wide] = value[SIDE:]
            ref[PIX - SIDE:, lo:lo + wide] = zero


def _conv_kernel(own_ref, oth_ref, a_ref, w_ref, y_ref, cat_ref, acc_ref):
    kx = pl.program_id(0)

    @pl.when(kx == 0)
    def _():
        _cat_into(cat_ref, 0, own_ref[...], 1)
        _cat_into(cat_ref, own_ref.shape[1], oth_ref[...], 1)

    acc_ref[kx] = jnp.dot(cat_ref[...], w_ref[0], preferred_element_type=F32)

    @pl.when(kx == 2)
    def _():
        z = _join_shifts(acc_ref[0], acc_ref[1], acc_ref[2])
        y_ref[...] = (a_ref[...].astype(F32) + z).astype(BF)


def _dgrad_kernel(dy_ref, w_ref, own_ref, oth_ref, cat_ref, acc_ref):
    kx = pl.program_id(0)

    @pl.when(kx == 0)
    def _():
        _cat_into(cat_ref, 0, dy_ref[...], -1)

    acc_ref[kx] = jnp.dot(cat_ref[...], w_ref[0], preferred_element_type=F32)

    @pl.when(kx == 2)
    def _():
        half = dy_ref.shape[1]
        p = _join_shifts(acc_ref[2], acc_ref[1], acc_ref[0])
        own_ref[...] = p[:, :half]
        oth_ref[...] = p[:, half:].astype(BF)


def _dw_kernel(idx_ref, own_ref, oth_ref, dy_ref, out_ref, pad_ref, rhs_ref):
    @pl.when(pl.program_id(0) == 0)
    def _():
        x = lax.broadcasted_iota(jnp.int32, (PIX, 128), 0) % SIDE

        def build(i, carry):
            v = dy_ref[i].astype(F32)
            moved = (jnp.where(x < SIDE - 1, pltpu.roll(v, PIX - 1, 0), 0.0), v,
                     jnp.where(x > 0, pltpu.roll(v, 1, 0), 0.0))
            for kx in range(3):
                _pad_into(pad_ref.at[kx], moved[kx].astype(BF))
            for t in range(9):
                start = (2 - t // 3) * SIDE
                rhs_ref[pl.ds(pl.multiple_of(i * PIX, PIX), PIX), t * 128:(t + 1) * 128] = (
                    pad_ref[t % 3, start:start + PIX, :])
            return carry

        lax.fori_loop(0, dy_ref.shape[0], build, 0)

    h = jnp.concatenate([own_ref[...], oth_ref[...]], axis=1)
    for lo, taps in ((0, 2), (2, 2), (4, 2), (6, 2), (8, 1)):
        part = lax.dot_general(h, rhs_ref[:, lo * 128:(lo + taps) * 128], (((0,), (0,)), ((), ())),
                               preferred_element_type=F32)
        for i in range(taps):
            for side in range(2):
                at = pl.multiple_of(idx_ref[side] * 128, 128)
                out_ref[lo + i, pl.ds(at, 128), :] = part[side * 128:(side + 1) * 128, i * 128:(i + 1) * 128]


def _assemble_kernel(idx_ref, *refs):
    out_ref = refs[-1]
    for r in range(4):
        for side in range(2):
            for kx in range(3):
                out_ref[kx, 0, idx_ref[4 + side], idx_ref[r]] = refs[r][kx, side]


def local(x_input, d_output, weights, gains, biases):
    row = lax.axis_index("dp")
    segment = lax.axis_index("segment")
    chan = lax.axis_index("chan")
    z = chan // 2
    core = chan % 2
    width = weights.shape[2] // GROUPS
    half = 4 * 128
    axes = ("dp", "segment", "chan")

    def lin(d, s, k):
        return (d * 8 + s) * 8 + k

    def move(value, source, target):
        flip = (source < 4) != (target < 4)
        pairs = [(lin(d, source, k), lin(d, target, (6 - k + 2 * (k % 2)) if flip else k))
                 for d in range(4) for k in range(8)]
        return lax.ppermute(value, axes, pairs)

    def swap(value):
        return lax.ppermute(value, "chan", [(k, k ^ 1) for k in range(8)])

    def turn(value, by):
        return lax.ppermute(value, "dp", [(i, (i + by) % 4) for i in range(4)])

    def turn_z(value, by):
        return lax.ppermute(value, "chan", [(k, (k + 2 * by) % 8) for k in range(8)])

    def ordered(parts):
        turn_of = [parts[0], parts[3], parts[2], parts[1]]
        return lax.dynamic_slice_in_dim(jnp.concatenate(turn_of * 2, axis=1), (4 - z) % 4 * 128, half, 1)

    def spread(pick):
        return ordered([pick(z)] + [turn_z(pick((z + by) % 4), by) for by in (1, 2, 3)])

    quarter = lax.dynamic_slice_in_dim(weights[0], row * 256, 256, 1)
    sides = [(row + jnp.arange(4)) % 4, (core + jnp.arange(2)) % 2]
    w = None
    token = None
    pieces = {}
    for by in (0, 1, 3, 2):
        piece = quarter
        if by > 1:
            piece, token = lax.optimization_barrier((piece, token))
        if by > 0:
            piece = turn_z(piece, by)
        token = piece
        below = turn(piece, 1)
        above = turn(piece, -1)
        across = jnp.concatenate([turn(below[:5], 1), turn(above[5:], -1)], axis=0)
        pieces[by] = [p.reshape(9, 2, 128, 128) for p in (piece, above, across, below)]
    for by in (0, 1, 3, 2):
        places = jnp.concatenate(sides + [(z - by)[None] % 4]).astype(jnp.int32)
        w = pl.pallas_call(
            _assemble_kernel,
            out_shape=jax.ShapeDtypeStruct((3, 3, 2, 4, 128, half), BF),
            grid_spec=pltpu.PrefetchScalarGridSpec(
                num_scalar_prefetch=1, grid=(3,),
                in_specs=[pl.BlockSpec((3, 2, 128, 128), lambda t, i: (t, 0, 0, 0))] * 4
                + ([] if w is None else [pl.BlockSpec(memory_space=pl.ANY)]),
                out_specs=pl.BlockSpec((3, 1, 2, 4, 128, 128), lambda t, i: (0, t, 0, 0, 0, i[6]))),
            input_output_aliases={} if w is None else {5: 0},
            name="assemble",
        )(places, *pieces[by], *([] if w is None else [w]))
    w = w.reshape(3, 6 * half, half)

    rows = jnp.concatenate([gains, biases], axis=0)
    rows = spread(lambda t: rows)
    gain = rows[0:1]
    bias = rows[1:2]

    act = jax.ShapeDtypeStruct((PIX, half), BF)
    act32 = jax.ShapeDtypeStruct((PIX, half), F32)
    line = jax.ShapeDtypeStruct((1, half), F32)

    def normed(a):
        return pl.pallas_call(lambda *r: _gn_kernel(width, *r), out_shape=act, name="gn")(a, gain, bias)

    def prep(a):
        return pl.pallas_call(lambda *r: _prep_kernel(width, *r), out_shape=(act, act32, act32, line),
                              name="prep")(a, gain, bias)

    full = pl.BlockSpec((PIX, half), lambda t: (0, 0))

    def conv(own, oth, a):
        return pl.pallas_call(
            _conv_kernel, grid=(3,),
            in_specs=[full, full, full, pl.BlockSpec((1, 6 * half, half), lambda t: (t, 0, 0))],
            out_specs=full, out_shape=act,
            scratch_shapes=[pltpu.VMEM((PIX, 6 * half), BF), pltpu.VMEM((3, PIX, half), F32)],
            name="conv")(own, oth, a, w)

    def dgrad(dy):
        return pl.pallas_call(
            _dgrad_kernel, grid=(3,),
            in_specs=[full, pl.BlockSpec((1, 3 * half, 2 * half), lambda t: (t, 0, 0))],
            out_specs=(full, full), out_shape=(act32, act),
            scratch_shapes=[pltpu.VMEM((PIX, 3 * half), BF), pltpu.VMEM((3, PIX, 2 * half), F32)],
            name="dgrad")(dy, w_turned)

    def added(p, q):
        return (p.astype(F32) + q.astype(F32)).astype(BF)

    first = spread(lambda t: lax.dynamic_index_in_dim(x_input[:, 0], t, 0, keepdims=False))
    last = spread(lambda t: lax.dynamic_index_in_dim(d_output[:, 0], 3 - t, 0, keepdims=False))
    first, last, gain, bias, w = lax.optimization_barrier((first, last, gain, bias, w))
    a = jnp.where(segment == 0, first, jnp.zeros_like(first))
    inputs = [a]
    skips = {}
    for j in range(7):
        own = normed(a)
        oth = swap(own)
        y = conv(own, oth, a)
        if j == 3:
            late, y = lax.optimization_barrier((w, y))
        a = move(y, j, j + 1)
        if j < 3:
            skips[j] = move(y, j, 7 - j)
        if j >= 4:
            a = added(a, skips[6 - j])
        inputs.append(a)
    mine = inputs[0]
    for a in inputs[1:]:
        mine = mine + a

    hidden, xhat, slope, rstd = prep(mine)
    w_turned = jnp.transpose(late.reshape(3, 3, 2 * half, half), (0, 1, 3, 2)).reshape(3, 3 * half, 2 * half)

    dy = jnp.where(segment == 7, last, jnp.zeros_like(last))
    grads = []
    gain_sum = bias_sum = 0.0
    skip_grads = {}
    for j in reversed(range(8)):
        if j == 3:
            own_all, oth_all, dy = lax.optimization_barrier((own_all, oth_all, dy))
        if j == 0:
            mine = grads[0]
            for g in grads[1:]:
                mine = mine + g
            mine = mine + dy
            dz = [lax.dynamic_slice_in_dim(mine, (z + by) % 4 * 128, 128, 1) for by in range(4)]
            dz = jnp.stack(dz[:1] + [turn_z(dz[by], by) for by in (1, 2, 3)])
            dz, dy = lax.optimization_barrier((dz, dy))
            turned = [turn(dz, -1), turn(dz, 2), turn(dz, 1)]
            dall = jnp.concatenate([dz] + turned, axis=0)
        grads.append(dy)
        own, oth = dgrad(dy)
        oth = swap(oth)
        da, dg, db = pl.pallas_call(
            lambda *r: _gn_bwd_kernel(width, *r), out_shape=(act, line, line), name="gn_bwd",
        )(dy, own, oth, xhat, slope, rstd, gain)
        gain_sum = gain_sum + dg
        bias_sum = bias_sum + db
        if j > 0:
            dy = move(da, j, j - 1)
        if j > 4:
            skip_grads[7 - j] = move(da, j, 7 - j)
        if 0 < j < 4:
            dy = added(dy, skip_grads[j - 1])
        if j == 4:
            hidden, dg = lax.optimization_barrier((hidden, dg))
            hz = jnp.stack([hidden] + [turn_z(hidden, by) for by in (1, 2, 3)])
            own_all = jnp.concatenate([hz, turn(hz, -1), turn(hz, 2), turn(hz, 1)], axis=0)
            oth_all = swap(own_all)

    flip = jnp.stack([core, 1 - core]).astype(jnp.int32)
    hspec = pl.BlockSpec((16 * PIX, 128), lambda i, c: (0, i))
    grad_weight = pl.pallas_call(
        _dw_kernel,
        out_shape=jax.ShapeDtypeStruct((9, 2 * half, 128), F32),
        grid_spec=pltpu.PrefetchScalarGridSpec(
            num_scalar_prefetch=1, grid=(4,),
            in_specs=[hspec, hspec, pl.BlockSpec((16, PIX, 128), lambda i, c: (0, 0, 0))],
            out_specs=pl.BlockSpec((9, 256, 128), lambda i, c: (0, i, 0)),
            scratch_shapes=[pltpu.VMEM((3, PIX + 2 * SIDE, 128), BF), pltpu.VMEM((16 * PIX, 9 * 128), BF)]),
        name="dw")(flip, own_all.reshape(16 * PIX, half), oth_all.reshape(16 * PIX, half), dall)

    small = jnp.transpose(jnp.concatenate([gain_sum, bias_sum], axis=0).reshape(2, 4, 128), (1, 0, 2))
    total = lax.dynamic_index_in_dim(small, z, 0, keepdims=False)
    for by in (1, 2, 3):
        piece = lax.dynamic_index_in_dim(small, (z + by) % 4, 0, keepdims=False)
        total = total + turn_z(piece, by)
    small = total + turn(total, 1) + turn(total, 2) + turn(total, -1)
    return (grad_weight[None], small[0:1], small[1:2])


def solution(mesh):
    in_specs = (
        P(None, "dp", None, "chan"),
        P(None, "dp", None, "chan"),
        P("segment", None, None, "chan"),
        P("segment", "chan"),
        P("segment", "chan"),
    )
    out_specs = (P("segment", None, None, "chan"), P("segment", "chan"), P("segment", "chan"))

    return jax.shard_map(local, mesh=mesh, in_specs=in_specs, out_specs=out_specs, check_vma=False)
```

time: 1030 us -> 632 us (0.61)
  Pallas kernels: 508 us -> 181 us
  blocking collectives: 105 us -> 0 us
  starting transfers between devices: 60.9 us -> 96.7 us
    pallas_call x17 -> x20, Pallas kernels: 468 us -> 141 us  [the longest x8 56.2 us: dgrad(): pl.pallas_call(_dgrad_kernel, grid=(3,), in_specs=[full, pl.BlockSpec((1,...]
    all_to_all x3 -> x0, blocking collectives: 96 us -> none  [scatter_z(): return lax.all_to_all(value, 'chan', 0, 0, axis_index_groups=ZG, tiled=True)]
    ppermute x16 -> x37, waiting for transfers between devices: 7.17 us -> 71.8 us  [the longest x21 51 us: turn_z(): lax.ppermute(value, 'chan', [(k, (k + 2 * by) % 8) for k in range(8)])]
    ppermute x16 -> x37, starting transfers between devices: 19 us -> 52.9 us  [the longest x21 39.6 us: turn_z(): lax.ppermute(value, 'chan', [(k, (k + 2 * by) % 8) for k in range(8)])]
    ppermute x20, waiting for transfers between devices: 144 us -> 117 us  [move(): return lax.ppermute(value, axes, pairs)]
    another operation x2, local copies, waits for them, and re-layouts: 14.8 us -> 0.06 us  [the longest x1 0.05 us: local(): dz = jnp.stack(dz[:1] + [turn_z(dz[by], by) for by in (1, 2, 3)])]
    ppermute x10 -> x25, starting transfers between devices: 11.1 us -> 25.8 us  [turn(): return lax.ppermute(value, 'dp', [(i, (i + by) % 4) for i in range(4)])]
    all_to_all x4 -> x0, starting transfers between devices: 14.6 us -> none  [scatter_z(): return lax.all_to_all(value, 'chan', 0, 0, axis_index_groups=ZG, tiled=True)]
  transfers between devices with their start and end apart: 50 -> 82, of which waited for: 11 -> 38; matrix products, arithmetic and copies ran while one was open for 2% -> 7% of each run, Pallas kernels for 34% -> 11%
where the time goes in v2:
time: 632 us; the launch traced here: 621 us
  waiting for transfers between devices  268 us (42%)
  Pallas kernels  181 us (29%)
  starting transfers between devices  96.7 us (15%)
  local copies, waits for them, and re-layouts  53.1 us (8%)
  other arithmetic  19.5 us (3%)
    ppermute x20, waiting for transfers between devices, move(): return lax.ppermute(value, axes, pairs)  117 us
    ppermute x25, waiting for transfers between devices, turn(): return lax.ppermute(value, 'dp', [(i, (i + by) % 4) for i in range(4)])  79.6 us
    pallas_call x8, Pallas kernels, dgrad(): pl.pallas_call(_dgrad_kernel, grid=(3,), in_specs=[full, pl.BlockSpec((1,...  56.2 us
    ppermute x21, waiting for transfers between devices, turn_z(): lax.ppermute(value, 'chan', [(k, (k + 2 * by) % 8) for k in range(8)])  51 us
    pallas_call x7, Pallas kernels, conv(): pl.pallas_call(_conv_kernel, grid=(3,), in_specs=[full, full, full, pl.Bl...  48.3 us
    ppermute x21, starting transfers between devices, turn_z(): lax.ppermute(value, 'chan', [(k, (k + 2 * by) % 8) for k in range(8)])  39.6 us
    unnamed x169, local copies, waits for them, and re-layouts  28.7 us
    ppermute x25, starting transfers between devices, turn(): return lax.ppermute(value, 'dp', [(i, (i + by) % 4) for i in range(4)])  25.8 us
  transfers between devices with their start and end apart: 82, of which 38 were waited for; matrix products, arithmetic and copies ran while one was open for 7% of the time, Pallas kernels for 11%

profile of v2, /device:TPU:1, one launch (start us, length us, event | category | flops | bytes accessed | tf_op | source)
XLA Modules:
  0.0 621.3 jit_solution(4055295122282689646)
XLA Ops:
  3.2 2.1 collective-permute-start.25
  9.6 2.7 collective-permute-start.6
  21.5 3.1 collective-permute-start.3
  29.4 13.4 %collective-permute-start = (bf16[256,128]{1,0:T(8,128)(2,1)S(1)}, bf16[256,128]{1,0:T(8,128)(2,1)S(1)}, u32[]{:S(2)}, u32[]{:S(2)}) collective-permute-start(bf16[256,128]{1,0:T(8,128)(2,1)S(1)} %get-tuple-element.131), channel_id=1, source_target_pairs={{0,6},{1,7},{2,0},{3,1},{4,2},{5,3},{6,4},{7,5},{8,14},{9,15},{10,... | collective-permute-start | bytes 196616 | tf_op jit(solution)/shard_map/ppermute | solution.py:204
  43.9 4.7 collective-permute-start.11
  50.8 28.3 %collective-permute-done.1 = bf16[256,128]{1,0:T(8,128)(2,1)S(1)} collective-permute-done((bf16[256,128]{1,0:T(8,128)(2,1)S(1)}, bf16[256,128]{1,0:T(8,128)(2,1)S(1)}, u32[]{:S(2)}, u32[]{:S(2)}) %collective-permute-start.1) | collective-permute-done | bytes 65568 | tf_op jit(solution)/shard_map/ppermute | solution.py:204
  83.7 2.5 collective-permute-done.27
  88.6 2.7 collective-permute-start.12
  94.2 2.2 collective-permute-done.21
  96.3 12.6 %collective-permute-done.17 = bf16[9,256,128]{2,1,0:T(8,128)(2,1)S(1)} collective-permute-done((bf16[9,256,128]{2,1,0:T(8,128)(2,1)S(1)}, bf16[9,256,128]{2,1,0:T(8,128)(2,1)S(1)}, u32[]{:S(2)}, u32[]{:S(2)}) %collective-permute-start.17) | collective-permute-done | bytes 589856 | tf_op jit(solution)/shard_map/ppermute | solution.py:201
  114.0 7.7 %collective-permute-done.13 = bf16[9,256,128]{2,1,0:T(8,128)(2,1)S(1)} collective-permute-done((bf16[9,256,128]{2,1,0:T(8,128)(2,1)S(1)}, bf16[9,256,128]{2,1,0:T(8,128)(2,1)S(1)}, u32[]{:S(2)}, u32[]{:S(2)}) %collective-permute-start.13) | collective-permute-done | bytes 589856 | tf_op jit(solution)/shard_map/ppermute | solution.py:201
  121.6 2.7 collective-permute-start.19
  128.7 2.7 collective-permute-start.15
  132.2 4.7 assemble.4.refs_4_
  138.9 4.7 assemble.5.refs_4_
  145.4 4.7 assemble.6.refs_4_
  151.9 4.7 assemble.7
  157.4 2.3 gn.7.own_ref
  159.6 4.4 collective-permute-start.28
  166.1 6.9 %conv.7 = bf16[256,512]{1,0:T(8,128)(2,1)} custom-call(bf16[256,512]{1,0:T(8,128)(2,1)} %gn.7.own_ref, bf16[256,512]{1,0:T(8,128)(2,1)} %copy-done.40, bf16[256,512]{1,0:T(8,128)(2,1)} %broadcast_select_fusion.1.r_0_.a_ref, bf16[3,3072,512]{2,1,0:T(8,128)(2,1)} %bitcast.67), custom_call_target="tpu_custom_call" | custom-call | tf_op jit(solution)/shard_map/conv/pallas_call | solution.py:263
  173.0 3.1 collective-permute-start.29
  176.2 5.6 collective-permute-done.29.r_0_.a_ref
  182.4 2.3 gn.8.own_ref
  188.4 6.9 %conv.8 = bf16[256,512]{1,0:T(8,128)(2,1)} custom-call(bf16[256,512]{1,0:T(8,128)(2,1)} %gn.8.own_ref, bf16[256,512]{1,0:T(8,128)(2,1)} %copy-done.41, bf16[256,512]{1,0:T(8,128)(2,1)} %copy-done.15, bf16[3,3072,512]{2,1,0:T(8,128)(2,1)} %bitcast.68), custom_call_target="tpu_custom_call" | custom-call | tf_op jit(solution)/shard_map/conv/pallas_call | solution.py:263
  196.7 2.3 gn.9.own_ref
  201.4 6.9 %conv.9 = bf16[256,512]{1,0:T(8,128)(2,1)} custom-call(bf16[256,512]{1,0:T(8,128)(2,1)} %gn.9.own_ref, bf16[256,512]{1,0:T(8,128)(2,1)} %copy-done.42, bf16[256,512]{1,0:T(8,128)(2,1)} %copy-done.17, bf16[3,3072,512]{2,1,0:T(8,128)(2,1)} %bitcast.69), custom_call_target="tpu_custom_call" | custom-call | tf_op jit(solution)/shard_map/conv/pallas_call | solution.py:263
  209.6 2.3 gn.10.own_ref
  214.3 6.9 %conv.10 = bf16[256,512]{1,0:T(8,128)(2,1)} custom-call(bf16[256,512]{1,0:T(8,128)(2,1)} %gn.10.own_ref, bf16[256,512]{1,0:T(8,128)(2,1)} %copy-done.43, bf16[256,512]{1,0:T(8,128)(2,1)} %copy-done.19, bf16[3,3072,512]{2,1,0:T(8,128)(2,1)} %bitcast.70), custom_call_target="tpu_custom_call" | custom-call | tf_op jit(solution)/shard_map/conv/pallas_call | solution.py:263
  222.6 2.3 gn.11.own_ref
  227.3 6.9 %conv.11 = bf16[256,512]{1,0:T(8,128)(2,1)} custom-call(bf16[256,512]{1,0:T(8,128)(2,1)} %gn.11.own_ref, bf16[256,512]{1,0:T(8,128)(2,1)} %copy-done.37, bf16[256,512]{1,0:T(8,128)(2,1)} %copy-done.21, bf16[3,3072,512]{2,1,0:T(8,128)(2,1)} %bitcast.71), custom_call_target="tpu_custom_call" | custom-call | tf_op jit(solution)/shard_map/conv/pallas_call | solution.py:263
  235.7 2.3 gn.12.own_ref
  240.4 6.9 %conv.12 = bf16[256,512]{1,0:T(8,128)(2,1)} custom-call(bf16[256,512]{1,0:T(8,128)(2,1)} %gn.12.own_ref, bf16[256,512]{1,0:T(8,128)(2,1)} %copy-done.38, bf16[256,512]{1,0:T(8,128)(2,1)} %add_convert_fusion.5.r_0_.a_ref, bf16[3,3072,512]{2,1,0:T(8,128)(2,1)} %bitcast.72), custom_call_target="tpu_custom_call" | custom-call | tf_op jit(solution)/shard_map/conv/pallas_call | solution.py:263
  248.7 2.3 gn.13.own_ref
  253.4 6.9 %conv.13 = bf16[256,512]{1,0:T(8,128)(2,1)} custom-call(bf16[256,512]{1,0:T(8,128)(2,1)} %gn.13.own_ref, bf16[256,512]{1,0:T(8,128)(2,1)} %copy-done.39, bf16[256,512]{1,0:T(8,128)(2,1)} %add_convert_fusion.4.r_0_.a_ref, bf16[3,3072,512]{2,1,0:T(8,128)(2,1)} %bitcast.73), custom_call_target="tpu_custom_call" | custom-call | tf_op jit(solution)/shard_map/conv/pallas_call | solution.py:263
  261.9 12.6 %copy.11 = bf16[3,3,1024,512]{2,3,1,0:T(8,128)(2,1)} copy(bf16[3,3,1024,512]{3,2,1,0:T(8,128)(2,1)} %bitcast.74) | data formatting | bytes 18874368 | tf_op jit(solution)/shard_map/reshape | solution.py:304
  274.6 7.1 %dgrad.8 = (f32[256,512]{1,0:T(8,128)}, bf16[256,512]{1,0:T(8,128)(2,1)}) custom-call(bf16[256,512]{1,0:T(8,128)(2,1)} %broadcast_select_fusion.dy_ref.r_0_, bf16[3,1536,1024]{2,1,0:T(8,128)(2,1)} %bitcast.75), custom_call_target="tpu_custom_call" | custom-call | tf_op jit(solution)/shard_map/dgrad/pallas_call | solution.py:271
  283.0 2.5 prep.1
  286.2 2.7 gn_bwd.8
  290.3 7.0 %dgrad.9 = (f32[256,512]{1,0:T(8,128)}, bf16[256,512]{1,0:T(8,128)(2,1)}) custom-call(bf16[256,512]{1,0:T(8,128)(2,1)} %copy-done.7, bf16[3,1536,1024]{2,1,0:T(8,128)(2,1)} %bitcast.76), custom_call_target="tpu_custom_call" | custom-call | tf_op jit(solution)/shard_map/dgrad/pallas_call | solution.py:271
  299.7 2.7 gn_bwd.9
  303.8 7.0 %dgrad.10 = (f32[256,512]{1,0:T(8,128)}, bf16[256,512]{1,0:T(8,128)(2,1)}) custom-call(bf16[256,512]{1,0:T(8,128)(2,1)} %copy-done.9, bf16[3,1536,1024]{2,1,0:T(8,128)(2,1)} %bitcast.77), custom_call_target="tpu_custom_call" | custom-call | tf_op jit(solution)/shard_map/dgrad/pallas_call | solution.py:271
  313.3 2.7 gn_bwd.10
  317.5 7.0 %dgrad.11 = (f32[256,512]{1,0:T(8,128)}, bf16[256,512]{1,0:T(8,128)(2,1)}) custom-call(bf16[256,512]{1,0:T(8,128)(2,1)} %copy-done.11, bf16[3,1536,1024]{2,1,0:T(8,128)(2,1)} %bitcast.78), custom_call_target="tpu_custom_call" | custom-call | tf_op jit(solution)/shard_map/dgrad/pallas_call | solution.py:271
  326.9 2.7 gn_bwd.11
  329.9 3.1 collective-permute-start.54
  332.9 6.3 %collective-permute-done.52 = bf16[256,512]{1,0:T(8,128)(2,1)S(1)} collective-permute-done((bf16[256,512]{1,0:T(8,128)(2,1)S(1)}, bf16[256,512]{1,0:T(8,128)(2,1)S(1)}, u32[]{:S(2)}, u32[]{:S(2)}) %collective-permute-start.52) | collective-permute-done | bytes 262176 | tf_op jit(solution)/shard_map/ppermute | solution.py:204
  339.3 10.4 %collective-permute-done.53 = bf16[256,512]{1,0:T(8,128)(2,1)S(1)} collective-permute-done((bf16[256,512]{1,0:T(8,128)(2,1)S(1)}, bf16[256,512]{1,0:T(8,128)(2,1)S(1)}, u32[]{:S(2)}, u32[]{:S(2)}) %collective-permute-start.53) | collective-permute-done | bytes 262176 | tf_op jit(solution)/shard_map/ppermute | solution.py:204
  351.7 21.5 %collective-permute-done.55 = bf16[4,256,512]{2,1,0:T(8,128)(2,1)S(1)} collective-permute-done((bf16[4,256,512]{2,1,0:T(8,128)(2,1)S(1)}, bf16[4,256,512]{2,1,0:T(8,128)(2,1)S(1)}, u32[]{:S(2)}, u32[]{:S(2)}) %collective-permute-start.55) | collective-permute-done | bytes 1048608 | tf_op jit(solution)/shard_map/ppermute | solution.py:201
  375.0 24.3 %collective-permute-done.57 = bf16[4,256,512]{2,1,0:T(8,128)(2,1)S(1)} collective-permute-done((bf16[4,256,512]{2,1,0:T(8,128)(2,1)S(1)}, bf16[4,256,512]{2,1,0:T(8,128)(2,1)S(1)}, u32[]{:S(2)}, u32[]{:S(2)}) %collective-permute-start.57) | collective-permute-done | bytes 1048608 | tf_op jit(solution)/shard_map/ppermute | solution.py:201
  402.6 6.1 collective-permute-done.58
  408.7 7.0 %dgrad.12 = (f32[256,512]{1,0:T(8,128)}, bf16[256,512]{1,0:T(8,128)(2,1)}) custom-call(bf16[256,512]{1,0:T(8,128)(2,1)} %copy-done.13, bf16[3,1536,1024]{2,1,0:T(8,128)(2,1)} %bitcast.79), custom_call_target="tpu_custom_call" | custom-call | tf_op jit(solution)/shard_map/dgrad/pallas_call | solution.py:271
  418.1 2.7 gn_bwd.12
  422.3 7.0 %dgrad.13 = (f32[256,512]{1,0:T(8,128)}, bf16[256,512]{1,0:T(8,128)(2,1)}) custom-call(bf16[256,512]{1,0:T(8,128)(2,1)} %add_convert_fusion.2.dy_ref.r_0_, bf16[3,1536,1024]{2,1,0:T(8,128)(2,1)} %bitcast.80), custom_call_target="tpu_custom_call" | custom-call | tf_op jit(solution)/shard_map/dgrad/pallas_call | solution.py:271
  431.8 2.7 gn_bwd.13
  436.0 7.1 %dgrad.14 = (f32[256,512]{1,0:T(8,128)}, bf16[256,512]{1,0:T(8,128)(2,1)}) custom-call(bf16[256,512]{1,0:T(8,128)(2,1)} %add_convert_fusion.1.dy_ref.r_0_, bf16[3,1536,1024]{2,1,0:T(8,128)(2,1)} %bitcast.81), custom_call_target="tpu_custom_call" | custom-call | tf_op jit(solution)/shard_map/dgrad/pallas_call | solution.py:271
  445.6 2.7 gn_bwd.14
  449.6 68.7 %collective-permute-done.68 = bf16[256,512]{1,0:T(8,128)(2,1)S(1)} collective-permute-done((bf16[256,512]{1,0:T(8,128)(2,1)S(1)}, bf16[256,512]{1,0:T(8,128)(2,1)S(1)}, u32[]{:S(2)}, u32[]{:S(2)}) %collective-permute-start.68) | collective-permute-done | bytes 262176 | tf_op jit(solution)/shard_map/ppermute | solution.py:195
  518.3 42.5 %collective-permute-done.67 = bf16[256,512]{1,0:T(8,128)(2,1)S(1)} collective-permute-done((bf16[256,512]{1,0:T(8,128)(2,1)}, bf16[256,512]{1,0:T(8,128)(2,1)S(1)}, u32[]{:S(2)}, u32[]{:S(2)}) %collective-permute-start.67) | collective-permute-done | bytes 262176 | tf_op jit(solution)/shard_map/ppermute | solution.py:195
  562.3 3.1 collective-permute-start.71
  568.0 7.0 %dgrad.15 = (f32[256,512]{1,0:T(8,128)}, bf16[256,512]{1,0:T(8,128)(2,1)}) custom-call(bf16[256,512]{1,0:T(8,128)(2,1)} %get-tuple-element.107.dy_ref.r_0_, bf16[3,1536,1024]{2,1,0:T(8,128)(2,1)} %bitcast.82), custom_call_target="tpu_custom_call" | custom-call | tf_op jit(solution)/shard_map/dgrad/pallas_call | solution.py:271
  575.0 3.0 collective-permute-start.75
  580.1 2.7 gn_bwd.15
  595.7 5.4 collective-permute-done.74
  602.2 18.0 %dw.1 = f32[9,1024,128]{2,1,0:T(8,128)} custom-call(s32[2]{0:T(128)} %pad_add_fusion.idx_ref, bf16[4096,512]{1,0:T(8,128)(2,1)} %bitcast.83, bf16[4096,512]{1,0:T(8,128)(2,1)} %bitcast.41.oth_ref, bf16[16,256,128]{2,1,0:T(8,128)(2,1)} %pad_maximum_fusion.1.dy_ref), custom_call_target="tpu_custom_call" | custom-call | tf_op jit(solution)/shard_map/dw/pallas_call | solution.py:345
  (355 shorter events, 130.2 us)
Async XLA Ops:
  3.2 78.9 %collective-permute-start.25 = (bf16[9,256,128]{2,1,0:T(8,128)(2,1)}, bf16[9,256,128]{2,1,0:T(8,128)(2,1)S(1)}, u32[]{:S(2)}, u32[]{:S(2)}) collective-permute-start(bf16[9,256,128]{2,1,0:T(8,128)(2,1)} %fusion.5), channel_id=1, source_target_pairs={{0,64},{64,128},{128,192},{192,0},{1,65},{65,129},{129,193},{193,1... | collective-permute-start | bytes 1769480 | tf_op jit(solution)/shard_map/ppermute | solution.py:201
  5.3 45.0 %collective-permute-start.24 = (bf16[9,256,128]{2,1,0:T(8,128)(2,1)}, bf16[9,256,128]{2,1,0:T(8,128)(2,1)S(1)}, u32[]{:S(2)}, u32[]{:S(2)}) collective-permute-start(bf16[9,256,128]{2,1,0:T(8,128)(2,1)} %fusion.5), channel_id=1, source_target_pairs={{0,192},{64,0},{128,64},{192,128},{1,193},{65,1},{129,65},{193,129... | collective-permute-start | bytes 1769480 | tf_op jit(solution)/shard_map/ppermute | solution.py:201
  6.7 19.8 %collective-permute-start.9 = (bf16[9,256,128]{2,1,0:T(8,128)(2,1)}, bf16[9,256,128]{2,1,0:T(8,128)(2,1)}, u32[]{:S(2)}, u32[]{:S(2)}) collective-permute-start(bf16[9,256,128]{2,1,0:T(8,128)(2,1)} %fusion.5), channel_id=1, source_target_pairs={{0,2},{1,3},{2,4},{3,5},{4,6},{5,7},{6,0},{7,1},{8,10},{9,11},{10,... | collective-permute-start | bytes 1769480 | tf_op jit(solution)/shard_map/ppermute | solution.py:204
  9.6 10.6 %collective-permute-start.6 = (f32[2,128]{1,0:T(2,128)}, f32[2,128]{1,0:T(2,128)S(1)}, u32[]{:S(2)}, u32[]{:S(2)}) collective-permute-start(f32[2,128]{1,0:T(2,128)} %get-tuple-element.141), channel_id=1, source_target_pairs={{0,6},{1,7},{2,0},{3,1},{4,2},{5,3},{6,4},{7,5},{8,14},{9,15},{10,... | collective-permute-start | bytes 3080 | tf_op jit(solution)/shard_map/ppermute | solution.py:204
  12.3 9.2 %collective-permute-start.7 = (f32[2,128]{1,0:T(2,128)}, f32[2,128]{1,0:T(2,128)S(1)}, u32[]{:S(2)}, u32[]{:S(2)}) collective-permute-start(f32[2,128]{1,0:T(2,128)} %get-tuple-element.141), channel_id=1, source_target_pairs={{0,4},{1,5},{2,6},{3,7},{4,0},{5,1},{6,2},{7,3},{8,12},{9,13},{10,... | collective-permute-start | bytes 3080 | tf_op jit(solution)/shard_map/ppermute | solution.py:204
  20.2 5.1 collective-permute-start.8
  21.5 6.7 %collective-permute-start.3 = (bf16[256,128]{1,0:T(8,128)(2,1)S(1)}, bf16[256,128]{1,0:T(8,128)(2,1)S(1)}, u32[]{:S(2)}, u32[]{:S(2)}) collective-permute-start(bf16[256,128]{1,0:T(8,128)(2,1)S(1)} %get-tuple-element.128), channel_id=1, source_target_pairs={{0,6},{1,7},{2,0},{3,1},{4,2},{5,3},{6,4},{7,5},{8,14},{9,15},{10,... | collective-permute-start | bytes 196616 | tf_op jit(solution)/shard_map/ppermute | solution.py:204
  25.2 4.2 collective-permute-start.4
  26.6 17.4 %collective-permute-start.10 = (bf16[9,256,128]{2,1,0:T(8,128)(2,1)}, bf16[9,256,128]{2,1,0:T(8,128)(2,1)S(1)}, u32[]{:S(2)}, u32[]{:S(2)}) collective-permute-start(bf16[9,256,128]{2,1,0:T(8,128)(2,1)} %fusion.5), channel_id=1, source_target_pairs={{0,6},{1,7},{2,0},{3,1},{4,2},{5,3},{6,4},{7,5},{8,14},{9,15},{10,... | collective-permute-start | bytes 1769480 | tf_op jit(solution)/shard_map/ppermute | solution.py:204
  28.2 14.7 %collective-permute-start.5 = (bf16[256,128]{1,0:T(8,128)(2,1)S(1)}, bf16[256,128]{1,0:T(8,128)(2,1)S(1)}, u32[]{:S(2)}, u32[]{:S(2)}) collective-permute-start(bf16[256,128]{1,0:T(8,128)(2,1)S(1)} %get-tuple-element.127), channel_id=1, source_target_pairs={{0,2},{1,3},{2,4},{3,5},{4,6},{5,7},{6,0},{7,1},{8,10},{9,11},{10,... | collective-permute-start | bytes 196616 | tf_op jit(solution)/shard_map/ppermute | solution.py:204
  29.4 20.0 %collective-permute-start = (bf16[256,128]{1,0:T(8,128)(2,1)S(1)}, bf16[256,128]{1,0:T(8,128)(2,1)S(1)}, u32[]{:S(2)}, u32[]{:S(2)}) collective-permute-start(bf16[256,128]{1,0:T(8,128)(2,1)S(1)} %get-tuple-element.131), channel_id=1, source_target_pairs={{0,6},{1,7},{2,0},{3,1},{4,2},{5,3},{6,4},{7,5},{8,14},{9,15},{10,... | collective-permute-start | bytes 196616 | tf_op jit(solution)/shard_map/ppermute | solution.py:204
  42.9 45.6 %collective-permute-start.20 = (bf16[9,256,128]{2,1,0:T(8,128)(2,1)}, bf16[9,256,128]{2,1,0:T(8,128)(2,1)S(1)}, u32[]{:S(2)}, u32[]{:S(2)}) collective-permute-start(bf16[9,256,128]{2,1,0:T(8,128)(2,1)} %collective-permute-done.9), channel_id=1, source_target_pairs={{0,192},{64,0},{128,64},{192,128},{1,193},{65,1},{129,65},{193,129... | collective-permute-start | bytes 1769480 | tf_op jit(solution)/shard_map/ppermute | solution.py:201
  43.9 44.6 %collective-permute-start.11 = (bf16[9,256,128]{2,1,0:T(8,128)(2,1)}, bf16[9,256,128]{2,1,0:T(8,128)(2,1)S(1)}, u32[]{:S(2)}, u32[]{:S(2)}) collective-permute-start(bf16[9,256,128]{2,1,0:T(8,128)(2,1)} %fusion.5), channel_id=1, source_target_pairs={{0,4},{1,5},{2,6},{3,7},{4,0},{5,1},{6,2},{7,3},{8,12},{9,13},{10,... | collective-permute-start | bytes 1769480 | tf_op jit(solution)/shard_map/ppermute | solution.py:204
  49.5 29.7 %collective-permute-start.1 = (bf16[256,128]{1,0:T(8,128)(2,1)S(1)}, bf16[256,128]{1,0:T(8,128)(2,1)S(1)}, u32[]{:S(2)}, u32[]{:S(2)}) collective-permute-start(bf16[256,128]{1,0:T(8,128)(2,1)S(1)} %get-tuple-element.132), channel_id=1, source_target_pairs={{0,4},{1,5},{2,6},{3,7},{4,0},{5,1},{6,2},{7,3},{8,12},{9,13},{10,... | collective-permute-start | bytes 196616 | tf_op jit(solution)/shard_map/ppermute | solution.py:204
  50.3 30.2 %collective-permute-start.2 = (bf16[256,128]{1,0:T(8,128)(2,1)S(1)}, bf16[256,128]{1,0:T(8,128)(2,1)S(1)}, u32[]{:S(2)}, u32[]{:S(2)}) collective-permute-start(bf16[256,128]{1,0:T(8,128)(2,1)S(1)} %get-tuple-element.130), channel_id=1, source_target_pairs={{0,2},{1,3},{2,4},{3,5},{4,6},{5,7},{6,0},{7,1},{8,10},{9,11},{10,... | collective-permute-start | bytes 196616 | tf_op jit(solution)/shard_map/ppermute | solution.py:204
  79.1 7.1 %collective-permute-start.27 = (bf16[4,256,128]{2,1,0:T(8,128)(2,1)S(1)}, bf16[4,256,128]{2,1,0:T(8,128)(2,1)S(1)}, u32[]{:S(2)}, u32[]{:S(2)}) collective-permute-start(bf16[4,256,128]{2,1,0:T(8,128)(2,1)S(1)} %slice.55), channel_id=1, source_target_pairs={{0,192},{64,0},{128,64},{192,128},{1,193},{65,1},{129,65},{193,129... | collective-permute-start | bytes 786440 | tf_op jit(solution)/shard_map/ppermute | solution.py:201
  81.1 15.2 %collective-permute-start.21 = (bf16[9,256,128]{2,1,0:T(8,128)(2,1)}, bf16[9,256,128]{2,1,0:T(8,128)(2,1)S(1)}, u32[]{:S(2)}, u32[]{:S(2)}) collective-permute-start(bf16[9,256,128]{2,1,0:T(8,128)(2,1)} %collective-permute-done.9), channel_id=1, source_target_pairs={{0,64},{64,128},{128,192},{192,0},{1,65},{65,129},{129,193},{193,1... | collective-permute-start | bytes 1769480 | tf_op jit(solution)/shard_map/ppermute | solution.py:201
  82.1 26.9 %collective-permute-start.17 = (bf16[9,256,128]{2,1,0:T(8,128)(2,1)S(1)}, bf16[9,256,128]{2,1,0:T(8,128)(2,1)S(1)}, u32[]{:S(2)}, u32[]{:S(2)}) collective-permute-start(bf16[9,256,128]{2,1,0:T(8,128)(2,1)S(1)} %collective-permute-done.10), channel_id=1, source_target_pairs={{0,64},{64,128},{128,192},{192,0},{1,65},{65,129},{129,193},{193,1... | collective-permute-start | bytes 1769480 | tf_op jit(solution)/shard_map/ppermute | solution.py:201
  86.2 24.3 %collective-permute-start.16 = (bf16[9,256,128]{2,1,0:T(8,128)(2,1)S(1)}, bf16[9,256,128]{2,1,0:T(8,128)(2,1)S(1)}, u32[]{:S(2)}, u32[]{:S(2)}) collective-permute-start(bf16[9,256,128]{2,1,0:T(8,128)(2,1)S(1)} %collective-permute-done.10), channel_id=1, source_target_pairs={{0,192},{64,0},{128,64},{192,128},{1,193},{65,1},{129,65},{193,129... | collective-permute-start | bytes 1769480 | tf_op jit(solution)/shard_map/ppermute | solution.py:201
  88.5 33.1 %collective-permute-start.13 = (bf16[9,256,128]{2,1,0:T(8,128)(2,1)S(1)}, bf16[9,256,128]{2,1,0:T(8,128)(2,1)S(1)}, u32[]{:S(2)}, u32[]{:S(2)}) collective-permute-start(bf16[9,256,128]{2,1,0:T(8,128)(2,1)S(1)} %collective-permute-done.11), channel_id=1, source_target_pairs={{0,64},{64,128},{128,192},{192,0},{1,65},{65,129},{129,193},{193,1... | collective-permute-start | bytes 1769480 | tf_op jit(solution)/shard_map/ppermute | solution.py:201
  88.6 33.1 %collective-permute-start.12 = (bf16[9,256,128]{2,1,0:T(8,128)(2,1)S(1)}, bf16[9,256,128]{2,1,0:T(8,128)(2,1)S(1)}, u32[]{:S(2)}, u32[]{:S(2)}) collective-permute-start(bf16[9,256,128]{2,1,0:T(8,128)(2,1)S(1)} %collective-permute-done.11), channel_id=1, source_target_pairs={{0,192},{64,0},{128,64},{192,128},{1,193},{65,1},{129,65},{193,129... | collective-permute-start | bytes 1769480 | tf_op jit(solution)/shard_map/ppermute | solution.py:201
  96.3 32.3 %collective-permute-start.26 = (bf16[5,256,128]{2,1,0:T(8,128)(2,1)S(1)}, bf16[5,256,128]{2,1,0:T(8,128)(2,1)S(1)}, u32[]{:S(2)}, u32[]{:S(2)}) collective-permute-start(bf16[5,256,128]{2,1,0:T(8,128)(2,1)S(1)} %slice.54), channel_id=1, source_target_pairs={{0,64},{64,128},{128,192},{192,0},{1,65},{65,129},{129,193},{193,1... | collective-permute-start | bytes 983048 | tf_op jit(solution)/shard_map/ppermute | solution.py:201
  109.0 19.7 %collective-permute-start.23 = (bf16[4,256,128]{2,1,0:T(8,128)(2,1)S(1)}, bf16[4,256,128]{2,1,0:T(8,128)(2,1)S(1)}, u32[]{:S(2)}, u32[]{:S(2)}) collective-permute-start(bf16[4,256,128]{2,1,0:T(8,128)(2,1)S(1)} %slice.53), channel_id=1, source_target_pairs={{0,192},{64,0},{128,64},{192,128},{1,193},{65,1},{129,65},{193,129... | collective-permute-start | bytes 786440 | tf_op jit(solution)/shard_map/ppermute | solution.py:201
  110.4 26.5 %collective-permute-start.22 = (bf16[5,256,128]{2,1,0:T(8,128)(2,1)}, bf16[5,256,128]{2,1,0:T(8,128)(2,1)}, u32[]{:S(2)}, u32[]{:S(2)}) collective-permute-start(bf16[5,256,128]{2,1,0:T(8,128)(2,1)} %slice.52), channel_id=1, source_target_pairs={{0,64},{64,128},{128,192},{192,0},{1,65},{65,129},{129,193},{193,1... | collective-permute-start | bytes 983048 | tf_op jit(solution)/shard_map/ppermute | solution.py:201
  121.6 22.0 %collective-permute-start.18 = (bf16[5,256,128]{2,1,0:T(8,128)(2,1)}, bf16[5,256,128]{2,1,0:T(8,128)(2,1)S(1)}, u32[]{:S(2)}, u32[]{:S(2)}) collective-permute-start(bf16[5,256,128]{2,1,0:T(8,128)(2,1)} %slice.50), channel_id=1, source_target_pairs={{0,64},{64,128},{128,192},{192,0},{1,65},{65,129},{129,193},{193,1... | collective-permute-start | bytes 983048 | tf_op jit(solution)/shard_map/ppermute | solution.py:201
  121.6 22.0 %collective-permute-start.19 = (bf16[4,256,128]{2,1,0:T(8,128)(2,1)}, bf16[4,256,128]{2,1,0:T(8,128)(2,1)}, u32[]{:S(2)}, u32[]{:S(2)}) collective-permute-start(bf16[4,256,128]{2,1,0:T(8,128)(2,1)} %slice.51), channel_id=1, source_target_pairs={{0,192},{64,0},{128,64},{192,128},{1,193},{65,1},{129,65},{193,129... | collective-permute-start | bytes 786440 | tf_op jit(solution)/shard_map/ppermute | solution.py:201
  128.6 21.5 %collective-permute-start.14 = (bf16[5,256,128]{2,1,0:T(8,128)(2,1)}, bf16[5,256,128]{2,1,0:T(8,128)(2,1)S(1)}, u32[]{:S(2)}, u32[]{:S(2)}) collective-permute-start(bf16[5,256,128]{2,1,0:T(8,128)(2,1)} %slice.48), channel_id=1, source_target_pairs={{0,64},{64,128},{128,192},{192,0},{1,65},{65,129},{129,193},{193,1... | collective-permute-start | bytes 983048 | tf_op jit(solution)/shard_map/ppermute | solution.py:201
  128.7 21.5 %collective-permute-start.15 = (bf16[4,256,128]{2,1,0:T(8,128)(2,1)}, bf16[4,256,128]{2,1,0:T(8,128)(2,1)}, u32[]{:S(2)}, u32[]{:S(2)}) collective-permute-start(bf16[4,256,128]{2,1,0:T(8,128)(2,1)} %slice.49), channel_id=1, source_target_pairs={{0,192},{64,0},{128,64},{192,128},{1,193},{65,1},{129,65},{193,129... | collective-permute-start | bytes 786440 | tf_op jit(solution)/shard_map/ppermute | solution.py:201
  159.6 5.8 collective-permute-start.28
  173.0 8.7 %collective-permute-start.29 = (bf16[256,512]{1,0:T(8,128)(2,1)}, bf16[256,512]{1,0:T(8,128)(2,1)S(1)}, u32[]{:S(2)}, u32[]{:S(2)}) collective-permute-start(bf16[256,512]{1,0:T(8,128)(2,1)} %conv.7), channel_id=1, source_target_pairs={{0,8},{1,9},{2,10},{3,11},{4,12},{5,13},{6,14},{7,15},{64,72},{65,... | collective-permute-start | bytes 786440 | tf_op jit(solution)/shard_map/ppermute | solution.py:195
  184.7 3.0 collective-permute-start.30
  211.9 1.7 collective-permute-start.34
  225.3 9.6 %collective-permute-start.38 = (bf16[256,512]{1,0:T(8,128)(2,1)S(1)}, bf16[256,512]{1,0:T(8,128)(2,1)S(1)}, u32[]{:S(2)}, u32[]{:S(2)}) collective-permute-start(bf16[256,512]{1,0:T(8,128)(2,1)S(1)} %copy-done.36), channel_id=1, source_target_pairs={{16,46},{17,47},{18,44},{19,45},{20,42},{21,43},{22,40},{23,41},{8... | collective-permute-start | bytes 786440 | tf_op jit(solution)/shard_map/ppermute | solution.py:195
  238.3 9.6 %collective-permute-start.41 = (bf16[256,512]{1,0:T(8,128)(2,1)S(1)}, bf16[256,512]{1,0:T(8,128)(2,1)S(1)}, u32[]{:S(2)}, u32[]{:S(2)}) collective-permute-start(bf16[256,512]{1,0:T(8,128)(2,1)S(1)} %copy-done.35), channel_id=1, source_target_pairs={{8,54},{9,55},{10,52},{11,53},{12,50},{13,51},{14,48},{15,49},{72,... | collective-permute-start | bytes 786440 | tf_op jit(solution)/shard_map/ppermute | solution.py:195
  251.0 1.7 collective-permute-start.42
  251.4 30.7 %collective-permute-start.44 = (bf16[256,512]{1,0:T(8,128)(2,1)S(1)}, bf16[256,512]{1,0:T(8,128)(2,1)S(1)}, u32[]{:S(2)}, u32[]{:S(2)}) collective-permute-start(bf16[256,512]{1,0:T(8,128)(2,1)S(1)} %copy-done.34), channel_id=1, source_target_pairs={{0,62},{1,63},{2,60},{3,61},{4,58},{5,59},{6,56},{7,57},{64,126},{... | collective-permute-start | bytes 786440 | tf_op jit(solution)/shard_map/ppermute | solution.py:195
  260.4 21.7 %collective-permute-start.43 = (bf16[256,512]{1,0:T(8,128)(2,1)}, bf16[256,512]{1,0:T(8,128)(2,1)S(1)}, u32[]{:S(2)}, u32[]{:S(2)}) collective-permute-start(bf16[256,512]{1,0:T(8,128)(2,1)} %conv.13), channel_id=1, source_target_pairs={{48,56},{49,57},{50,58},{51,59},{52,60},{53,61},{54,62},{55,63},{1... | collective-permute-start | bytes 786440 | tf_op jit(solution)/shard_map/ppermute | solution.py:195
  281.7 3.8 collective-permute-start.45
  329.7 9.6 %collective-permute-start.52 = (bf16[256,512]{1,0:T(8,128)(2,1)S(1)}, bf16[256,512]{1,0:T(8,128)(2,1)S(1)}, u32[]{:S(2)}, u32[]{:S(2)}) collective-permute-start(bf16[256,512]{1,0:T(8,128)(2,1)S(1)} %copy-done.31), channel_id=1, source_target_pairs={{0,2},{1,3},{2,4},{3,5},{4,6},{5,7},{6,0},{7,1},{8,10},{9,11},{10,... | collective-permute-start | bytes 786440 | tf_op jit(solution)/shard_map/ppermute | solution.py:204
  329.7 20.0 %collective-permute-start.53 = (bf16[256,512]{1,0:T(8,128)(2,1)S(1)}, bf16[256,512]{1,0:T(8,128)(2,1)S(1)}, u32[]{:S(2)}, u32[]{:S(2)}) collective-permute-start(bf16[256,512]{1,0:T(8,128)(2,1)S(1)} %copy-done.31), channel_id=1, source_target_pairs={{0,4},{1,5},{2,6},{3,7},{4,0},{5,1},{6,2},{7,3},{8,12},{9,13},{10,... | collective-permute-start | bytes 786440 | tf_op jit(solution)/shard_map/ppermute | solution.py:204
  329.9 19.8 %collective-permute-start.54 = (bf16[256,512]{1,0:T(8,128)(2,1)S(1)}, bf16[256,512]{1,0:T(8,128)(2,1)S(1)}, u32[]{:S(2)}, u32[]{:S(2)}) collective-permute-start(bf16[256,512]{1,0:T(8,128)(2,1)S(1)} %copy-done.31), channel_id=1, source_target_pairs={{0,6},{1,7},{2,0},{3,1},{4,2},{5,3},{6,4},{7,5},{8,14},{9,15},{10,... | collective-permute-start | bytes 786440 | tf_op jit(solution)/shard_map/ppermute | solution.py:204
  349.8 23.4 %collective-permute-start.55 = (bf16[4,256,512]{2,1,0:T(8,128)(2,1)S(1)}, bf16[4,256,512]{2,1,0:T(8,128)(2,1)S(1)}, u32[]{:S(2)}, u32[]{:S(2)}) collective-permute-start(bf16[4,256,512]{2,1,0:T(8,128)(2,1)S(1)} %pad_maximum_fusion), channel_id=1, source_target_pairs={{0,192},{64,0},{128,64},{192,128},{1,193},{65,1},{129,65},{193,129... | collective-permute-start | bytes 3145736 | tf_op jit(solution)/shard_map/ppermute | solution.py:201
  350.1 24.8 %collective-permute-start.56 = (bf16[4,256,512]{2,1,0:T(8,128)(2,1)S(1)}, bf16[4,256,512]{2,1,0:T(8,128)(2,1)S(1)}, u32[]{:S(2)}, u32[]{:S(2)}) collective-permute-start(bf16[4,256,512]{2,1,0:T(8,128)(2,1)S(1)} %pad_maximum_fusion), channel_id=1, source_target_pairs={{0,128},{64,192},{128,0},{192,64},{1,129},{65,193},{129,1},{193,65... | collective-permute-start | bytes 3145736 | tf_op jit(solution)/shard_map/ppermute | solution.py:201
  350.4 48.8 %collective-permute-start.57 = (bf16[4,256,512]{2,1,0:T(8,128)(2,1)S(1)}, bf16[4,256,512]{2,1,0:T(8,128)(2,1)S(1)}, u32[]{:S(2)}, u32[]{:S(2)}) collective-permute-start(bf16[4,256,512]{2,1,0:T(8,128)(2,1)S(1)} %pad_maximum_fusion), channel_id=1, source_target_pairs={{0,64},{64,128},{128,192},{192,0},{1,65},{65,129},{129,193},{193,1... | collective-permute-start | bytes 3145736 | tf_op jit(solution)/shard_map/ppermute | solution.py:201
  401.3 7.4 %collective-permute-start.58 = (bf16[16,256,512]{2,1,0:T(8,128)(2,1)S(1)}, bf16[16,256,512]{2,1,0:T(8,128)(2,1)}, u32[]{:S(2)}, u32[]{:S(2)}) collective-permute-start(bf16[16,256,512]{2,1,0:T(8,128)(2,1)S(1)} %constant_dynamic-update-slice_fusion.24), channel_id=1, source_target_pairs={{0,1},{1,0},{2,3},{3,2},{4,5},{5,4},{6,7},{7,6},{8,9},{9,8},{10,11... | collective-permute-start | bytes 12582920 | tf_op jit(solution)/shard_map/ppermute | solution.py:198
  416.1 5.5 collective-permute-start.62
  429.4 1.7 collective-permute-start.63
  429.7 5.5 collective-permute-start.65
  443.1 1.7 collective-permute-start.66
  443.5 74.8 %collective-permute-start.68 = (bf16[256,512]{1,0:T(8,128)(2,1)S(1)}, bf16[256,512]{1,0:T(8,128)(2,1)S(1)}, u32[]{:S(2)}, u32[]{:S(2)}) collective-permute-start(bf16[256,512]{1,0:T(8,128)(2,1)S(1)} %copy-done.68), channel_id=1, source_target_pairs={{56,6},{57,7},{58,4},{59,5},{60,2},{61,3},{62,0},{63,1},{120,70},{... | collective-permute-start | bytes 786440 | tf_op jit(solution)/shard_map/ppermute | solution.py:195
  448.3 112.6 %collective-permute-start.67 = (bf16[256,512]{1,0:T(8,128)(2,1)}, bf16[256,512]{1,0:T(8,128)(2,1)S(1)}, u32[]{:S(2)}, u32[]{:S(2)}) collective-permute-start(bf16[256,512]{1,0:T(8,128)(2,1)} %get-tuple-element.99), channel_id=1, source_target_pairs={{8,0},{9,1},{10,2},{11,3},{12,4},{13,5},{14,6},{15,7},{72,64},{73,... | collective-permute-start | bytes 786440 | tf_op jit(solution)/shard_map/ppermute | solution.py:195
  561.8 5.0 collective-permute-start.69
  561.9 4.9 collective-permute-start.70
  562.3 5.6 collective-permute-start.71
  575.0 4.4 collective-permute-start.75
  583.7 4.3 collective-permute-start.76
  584.9 8.9 %collective-permute-start.72 = (bf16[4,256,128]{2,1,0:T(8,128)(2,1)S(1)}, bf16[4,256,128]{2,1,0:T(8,128)(2,1)S(1)}, u32[]{:S(2)}, u32[]{:S(2)}) collective-permute-start(bf16[4,256,128]{2,1,0:T(8,128)(2,1)S(1)} %pad_maximum_fusion.6), channel_id=1, source_target_pairs={{0,192},{64,0},{128,64},{192,128},{1,193},{65,1},{129,65},{193,129... | collective-permute-start | bytes 786440 | tf_op jit(solution)/shard_map/ppermute | solution.py:201
  585.8 9.9 %collective-permute-start.73 = (bf16[4,256,128]{2,1,0:T(8,128)(2,1)S(1)}, bf16[4,256,128]{2,1,0:T(8,128)(2,1)S(1)}, u32[]{:S(2)}, u32[]{:S(2)}) collective-permute-start(bf16[4,256,128]{2,1,0:T(8,128)(2,1)S(1)} %pad_maximum_fusion.6), channel_id=1, source_target_pairs={{0,128},{64,192},{128,0},{192,64},{1,129},{65,193},{129,1},{193,65... | collective-permute-start | bytes 786440 | tf_op jit(solution)/shard_map/ppermute | solution.py:201
  585.8 15.4 %collective-permute-start.74 = (bf16[4,256,128]{2,1,0:T(8,128)(2,1)S(1)}, bf16[4,256,128]{2,1,0:T(8,128)(2,1)S(1)}, u32[]{:S(2)}, u32[]{:S(2)}) collective-permute-start(bf16[4,256,128]{2,1,0:T(8,128)(2,1)S(1)} %pad_maximum_fusion.6), channel_id=1, source_target_pairs={{0,64},{64,128},{128,192},{192,0},{1,65},{65,129},{129,193},{193,1... | collective-permute-start | bytes 786440 | tf_op jit(solution)/shard_map/ppermute | solution.py:201
  586.4 3.3 collective-permute-start.77
  588.0 2.7 collective-permute-start.78
  590.7 29.6 %collective-permute-start.79 = (f32[2,128]{1,0:T(2,128)S(1)}, f32[2,128]{1,0:T(2,128)S(1)}, u32[]{:S(2)}, u32[]{:S(2)}) collective-permute-start(f32[2,128]{1,0:T(2,128)S(1)} %add_add_fusion.4), channel_id=1, source_target_pairs={{0,64},{64,128},{128,192},{192,0},{1,65},{65,129},{129,193},{193,1... | collective-permute-start | bytes 3080 | tf_op jit(solution)/shard_map/ppermute | solution.py:201
  592.0 28.3 %collective-permute-start.80 = (f32[2,128]{1,0:T(2,128)S(1)}, f32[2,128]{1,0:T(2,128)S(1)}, u32[]{:S(2)}, u32[]{:S(2)}) collective-permute-start(f32[2,128]{1,0:T(2,128)S(1)} %add_add_fusion.4), channel_id=1, source_target_pairs={{0,128},{64,192},{128,0},{192,64},{1,129},{65,193},{129,1},{193,65... | collective-permute-start | bytes 3080 | tf_op jit(solution)/shard_map/ppermute | solution.py:201
  593.7 26.5 %collective-permute-start.81 = (f32[2,128]{1,0:T(2,128)S(1)}, f32[2,128]{1,0:T(2,128)S(1)}, u32[]{:S(2)}, u32[]{:S(2)}) collective-permute-start(f32[2,128]{1,0:T(2,128)S(1)} %add_add_fusion.4), channel_id=1, source_target_pairs={{0,192},{64,0},{128,64},{192,128},{1,193},{65,1},{129,65},{193,129... | collective-permute-start | bytes 3080 | tf_op jit(solution)/shard_map/ppermute | solution.py:201
  (90 other events, 1579.3 us)

commit v3 on v2

--- a/solution.py
+++ b/solution.py
@@ -105,8 +105,19 @@
             ref[PIX - SIDE:, lo:lo + wide] = zero
 
 
-def _conv_kernel(own_ref, oth_ref, a_ref, w_ref, y_ref, cat_ref, acc_ref):
+def _conv_kernel(on_ref, own_ref, oth_ref, a_ref, w_ref, y_ref, cat_ref, acc_ref):
     kx = pl.program_id(0)
+
+    @pl.when(on_ref[0] > 0)
+    def _():
+        _conv_step(kx, own_ref, oth_ref, a_ref, w_ref, y_ref, cat_ref, acc_ref)
+
+    @pl.when((on_ref[0] == 0) & (kx == 0))
+    def _():
+        y_ref[...] = jnp.zeros_like(y_ref)
+
+
+def _conv_step(kx, own_ref, oth_ref, a_ref, w_ref, y_ref, cat_ref, acc_ref):
 
     @pl.when(kx == 0)
     def _():
@@ -121,8 +132,20 @@
         y_ref[...] = (a_ref[...].astype(F32) + z).astype(BF)
 
 
-def _dgrad_kernel(dy_ref, w_ref, own_ref, oth_ref, cat_ref, acc_ref):
+def _dgrad_kernel(on_ref, dy_ref, w_ref, own_ref, oth_ref, cat_ref, acc_ref):
     kx = pl.program_id(0)
+
+    @pl.when(on_ref[0] > 0)
+    def _():
+        _dgrad_step(kx, dy_ref, w_ref, own_ref, oth_ref, cat_ref, acc_ref)
+
+    @pl.when((on_ref[0] == 0) & (kx == 0))
+    def _():
+        own_ref[...] = jnp.zeros_like(own_ref)
+        oth_ref[...] = jnp.zeros_like(oth_ref)
+
+
+def _dgrad_step(kx, dy_ref, w_ref, own_ref, oth_ref, cat_ref, acc_ref):
 
     @pl.when(kx == 0)
     def _():
@@ -167,12 +190,24 @@
                 out_ref[lo + i, pl.ds(at, 128), :] = part[side * 128:(side + 1) * 128, i * 128:(i + 1) * 128]
 
 
-def _assemble_kernel(idx_ref, *refs):
-    out_ref = refs[-1]
-    for r in range(4):
-        for side in range(2):
-            for kx in range(3):
-                out_ref[kx, 0, idx_ref[4 + side], idx_ref[r]] = refs[r][kx, side]
+def _assemble_kernel(idx_ref, near, up, down, far0, far1, *rest):
+    out_ref = rest[-1]
+    for side in range(2):
+        at = idx_ref[4 + side]
+        for kx in range(3):
+            out_ref[kx, 0, at, idx_ref[0]] = near[side, kx]
+            out_ref[kx, 0, at, idx_ref[1]] = up[side, kx]
+            out_ref[kx, 0, at, idx_ref[2]] = (far0, far1)[side][kx]
+            out_ref[kx, 0, at, idx_ref[3]] = down[side, kx]
+
+
+def _place_kernel(idx_ref, *refs):
+    for by in range(4):
+        refs[4][:, pl.ds(pl.multiple_of(idx_ref[by] * 128, 128), 128)] = refs[by][...]
+
+
+def _limit(mib):
+    return pltpu.CompilerParams(vmem_limit_bytes=mib << 20)
 
 
 def local(x_input, d_output, weights, gains, biases):
@@ -203,14 +238,29 @@
     def turn_z(value, by):
         return lax.ppermute(value, "chan", [(k, (k + 2 * by) % 8) for k in range(8)])
 
-    def ordered(parts):
-        turn_of = [parts[0], parts[3], parts[2], parts[1]]
-        return lax.dynamic_slice_in_dim(jnp.concatenate(turn_of * 2, axis=1), (4 - z) % 4 * 128, half, 1)
-
-    def spread(pick):
-        return ordered([pick(z)] + [turn_z(pick((z + by) % 4), by) for by in (1, 2, 3)])
+    sources = ((z - jnp.arange(4)) % 4).astype(jnp.int32)
+
+    def send(pick):
+        return [pick(z)] + [turn_z(pick((z + by) % 4), by) for by in (1, 2, 3)]
+
+    def place(parts):
+        shape = jax.ShapeDtypeStruct((parts[0].shape[0], half), parts[0].dtype)
+        return pl.pallas_call(
+            _place_kernel, out_shape=shape,
+            grid_spec=pltpu.PrefetchScalarGridSpec(
+                num_scalar_prefetch=1, grid=(1,),
+                in_specs=[pl.BlockSpec(parts[0].shape, lambda t, i: (0, 0))] * 4,
+                out_specs=pl.BlockSpec(shape.shape, lambda t, i: (0, 0))),
+            compiler_params=_limit(6), name="place")(sources, *parts)
+
+    rows = jnp.concatenate([gains, biases], axis=0)
+    rows = send(lambda t: rows)
+    first = send(lambda t: lax.dynamic_index_in_dim(x_input[:, 0], t, 0, keepdims=False))
+    last = send(lambda t: lax.dynamic_index_in_dim(d_output[:, 0], 3 - t, 0, keepdims=False))
 
     quarter = lax.dynamic_slice_in_dim(weights[0], row * 256, 256, 1)
+    quarter = jnp.transpose(quarter.reshape(9, 2, 128, 128), (1, 0, 2, 3))
+    rows, first, last, quarter = lax.optimization_barrier((rows, first, last, quarter))
     sides = [(row + jnp.arange(4)) % 4, (core + jnp.arange(2)) % 2]
     w = None
     token = None
@@ -224,8 +274,8 @@
         token = piece
         below = turn(piece, 1)
         above = turn(piece, -1)
-        across = jnp.concatenate([turn(below[:5], 1), turn(above[5:], -1)], axis=0)
-        pieces[by] = [p.reshape(9, 2, 128, 128) for p in (piece, above, across, below)]
+        far = [turn(below[0], 1), turn(above[1], -1)]
+        pieces[by] = [piece, above, below] + far
     for by in (0, 1, 3, 2):
         places = jnp.concatenate(sides + [(z - by)[None] % 4]).astype(jnp.int32)
         w = pl.pallas_call(
@@ -233,16 +283,16 @@
             out_shape=jax.ShapeDtypeStruct((3, 3, 2, 4, 128, half), BF),
             grid_spec=pltpu.PrefetchScalarGridSpec(
                 num_scalar_prefetch=1, grid=(3,),
-                in_specs=[pl.BlockSpec((3, 2, 128, 128), lambda t, i: (t, 0, 0, 0))] * 4
+                in_specs=[pl.BlockSpec((2, 3, 128, 128), lambda t, i: (0, t, 0, 0))] * 3
+                + [pl.BlockSpec((3, 128, 128), lambda t, i: (t, 0, 0))] * 2
                 + ([] if w is None else [pl.BlockSpec(memory_space=pl.ANY)]),
                 out_specs=pl.BlockSpec((3, 1, 2, 4, 128, 128), lambda t, i: (0, t, 0, 0, 0, i[6]))),
-            input_output_aliases={} if w is None else {5: 0},
-            name="assemble",
+            input_output_aliases={} if w is None else {6: 0},
+            compiler_params=_limit(52), name="assemble",
         )(places, *pieces[by], *([] if w is None else [w]))
     w = w.reshape(3, 6 * half, half)
 
-    rows = jnp.concatenate([gains, biases], axis=0)
-    rows = spread(lambda t: rows)
+    rows = place(rows)
     gain = rows[0:1]
     bias = rows[1:2]
 
@@ -251,35 +301,42 @@
     line = jax.ShapeDtypeStruct((1, half), F32)
 
     def normed(a):
-        return pl.pallas_call(lambda *r: _gn_kernel(width, *r), out_shape=act, name="gn")(a, gain, bias)
+        return pl.pallas_call(lambda *r: _gn_kernel(width, *r), out_shape=act, compiler_params=_limit(6), name="gn")(a, gain, bias)
 
     def prep(a):
         return pl.pallas_call(lambda *r: _prep_kernel(width, *r), out_shape=(act, act32, act32, line),
-                              name="prep")(a, gain, bias)
-
-    full = pl.BlockSpec((PIX, half), lambda t: (0, 0))
-
-    def conv(own, oth, a):
+                              compiler_params=_limit(10), name="prep")(a, gain, bias)
+
+    full = pl.BlockSpec((PIX, half), lambda t, on: (0, 0))
+
+    def turn_on(j):
+        return jnp.where(segment == j, 1, 0).astype(jnp.int32).reshape(1)
+
+    def conv(j, own, oth, a):
         return pl.pallas_call(
-            _conv_kernel, grid=(3,),
-            in_specs=[full, full, full, pl.BlockSpec((1, 6 * half, half), lambda t: (t, 0, 0))],
-            out_specs=full, out_shape=act,
-            scratch_shapes=[pltpu.VMEM((PIX, 6 * half), BF), pltpu.VMEM((3, PIX, half), F32)],
-            name="conv")(own, oth, a, w)
-
-    def dgrad(dy):
+            _conv_kernel, out_shape=act,
+            grid_spec=pltpu.PrefetchScalarGridSpec(
+                num_scalar_prefetch=1, grid=(3,),
+                in_specs=[full, full, full, pl.BlockSpec((1, 6 * half, half), lambda t, on: (t * on[0], 0, 0))],
+                out_specs=full,
+                scratch_shapes=[pltpu.VMEM((PIX, 6 * half), BF), pltpu.VMEM((3, PIX, half), F32)]),
+            compiler_params=_limit(52), name="conv")(turn_on(j), own, oth, a, w)
+
+    def dgrad(j, dy):
         return pl.pallas_call(
-            _dgrad_kernel, grid=(3,),
-            in_specs=[full, pl.BlockSpec((1, 3 * half, 2 * half), lambda t: (t, 0, 0))],
-            out_specs=(full, full), out_shape=(act32, act),
-            scratch_shapes=[pltpu.VMEM((PIX, 3 * half), BF), pltpu.VMEM((3, PIX, 2 * half), F32)],
-            name="dgrad")(dy, w_turned)
+            _dgrad_kernel, out_shape=(act32, act),
+            grid_spec=pltpu.PrefetchScalarGridSpec(
+                num_scalar_prefetch=1, grid=(3,),
+                in_specs=[full, pl.BlockSpec((1, 3 * half, 2 * half), lambda t, on: (t * on[0], 0, 0))],
+                out_specs=(full, full),
+                scratch_shapes=[pltpu.VMEM((PIX, 3 * half), BF), pltpu.VMEM((3, PIX, 2 * half), F32)]),
+            compiler_params=_limit(52), name="dgrad")(turn_on(j), dy, w_turned)
 
     def added(p, q):
         return (p.astype(F32) + q.astype(F32)).astype(BF)
 
-    first = spread(lambda t: lax.dynamic_index_in_dim(x_input[:, 0], t, 0, keepdims=False))
-    last = spread(lambda t: lax.dynamic_index_in_dim(d_output[:, 0], 3 - t, 0, keepdims=False))
+    first = place(first)
+    last = place(last)
     first, last, gain, bias, w = lax.optimization_barrier((first, last, gain, bias, w))
     a = jnp.where(segment == 0, first, jnp.zeros_like(first))
     inputs = [a]
@@ -287,10 +344,13 @@
     for j in range(7):
         own = normed(a)
         oth = swap(own)
-        y = conv(own, oth, a)
-        if j == 3:
+        y = conv(j, own, oth, a)
+        if j == 1:
             late, y = lax.optimization_barrier((w, y))
+            late = jnp.transpose(late.reshape(3, 3, 2 * half, half), (0, 1, 3, 2))
         a = move(y, j, j + 1)
+        if j == 1:
+            late, a = lax.optimization_barrier((late, a))
         if j < 3:
             skips[j] = move(y, j, 7 - j)
         if j >= 4:
@@ -301,7 +361,7 @@
         mine = mine + a
 
     hidden, xhat, slope, rstd = prep(mine)
-    w_turned = jnp.transpose(late.reshape(3, 3, 2 * half, half), (0, 1, 3, 2)).reshape(3, 3 * half, 2 * half)
+    w_turned = late.reshape(3, 3 * half, 2 * half)
 
     dy = jnp.where(segment == 7, last, jnp.zeros_like(last))
     grads = []
@@ -321,10 +381,11 @@
             turned = [turn(dz, -1), turn(dz, 2), turn(dz, 1)]
             dall = jnp.concatenate([dz] + turned, axis=0)
         grads.append(dy)
-        own, oth = dgrad(dy)
+        own, oth = dgrad(j, dy)
         oth = swap(oth)
         da, dg, db = pl.pallas_call(
-            lambda *r: _gn_bwd_kernel(width, *r), out_shape=(act, line, line), name="gn_bwd",
+            lambda *r: _gn_bwd_kernel(width, *r), out_shape=(act, line, line),
+            compiler_params=_limit(10), name="gn_bwd",
         )(dy, own, oth, xhat, slope, rstd, gain)
         gain_sum = gain_sum + dg
         bias_sum = bias_sum + db
@@ -350,13 +411,14 @@
             in_specs=[hspec, hspec, pl.BlockSpec((16, PIX, 128), lambda i, c: (0, 0, 0))],
             out_specs=pl.BlockSpec((9, 256, 128), lambda i, c: (0, i, 0)),
             scratch_shapes=[pltpu.VMEM((3, PIX + 2 * SIDE, 128), BF), pltpu.VMEM((16 * PIX, 9 * 128), BF)]),
-        name="dw")(flip, own_all.reshape(16 * PIX, half), oth_all.reshape(16 * PIX, half), dall)
+        compiler_params=_limit(58), name="dw")(flip, own_all.reshape(16 * PIX, half), oth_all.reshape(16 * PIX, half), dall)
 
     small = jnp.transpose(jnp.concatenate([gain_sum, bias_sum], axis=0).reshape(2, 4, 128), (1, 0, 2))
     total = lax.dynamic_index_in_dim(small, z, 0, keepdims=False)
     for by in (1, 2, 3):
         piece = lax.dynamic_index_in_dim(small, (z + by) % 4, 0, keepdims=False)
         total = total + turn_z(piece, by)
+    total, grad_weight = lax.optimization_barrier((total, grad_weight))
     small = total + turn(total, 1) + turn(total, 2) + turn(total, -1)
     return (grad_weight[None], small[0:1], small[1:2])
 

time: 632 us -> 518 us (0.82)
  the two profiles are of different devices: /device:TPU:1 before, /device:TPU:8 now
where the time goes in v3:
time: 518 us; the launch traced here: 508 us
  waiting for transfers between devices  315 us (61%)
  Pallas kernels  84.7 us (16%)
  starting transfers between devices  82.5 us (16%)
  local copies, waits for them, and re-layouts  18.9 us (4%)
  other arithmetic  5.66 us (1%)
    ppermute x20, waiting for transfers between devices, move(): return lax.ppermute(value, axes, pairs)  157 us
    ppermute x25, waiting for transfers between devices, turn(): return lax.ppermute(value, 'dp', [(i, (i + by) % 4) for i in range(4)])  83 us
    ppermute x21, waiting for transfers between devices, turn_z(): lax.ppermute(value, 'chan', [(k, (k + 2 * by) % 8) for k in range(8)])  55.7 us
    ppermute x25, starting transfers between devices, turn(): return lax.ppermute(value, 'dp', [(i, (i + by) % 4) for i in range(4)])  33.3 us
    ppermute x21, starting transfers between devices, turn_z(): lax.ppermute(value, 'chan', [(k, (k + 2 * by) % 8) for k in range(8)])  29.6 us
    pallas_call x8, Pallas kernels, dgrad(): pl.pallas_call(_dgrad_kernel, out_shape=(act32, act), grid_spec=pltpu.Pre...  20.4 us
    pallas_call x7, Pallas kernels, conv(): pl.pallas_call(_conv_kernel, out_shape=act, grid_spec=pltpu.PrefetchScala...  18.7 us
    ppermute x16, waiting for transfers between devices, swap(): return lax.ppermute(value, 'chan', [(k, k ^ 1) for k in range(8)])  18.6 us
  transfers between devices with their start and end apart: 82, of which 39 were waited for; matrix products, arithmetic and copies ran while one was open for 4% of the time, Pallas kernels for 9%

profile of v3, /device:TPU:8, one launch (start us, length us, event | category | flops | bytes accessed | tf_op | source)
XLA Modules:
  0.0 508.4 jit_solution(9743967837609519352)
XLA Ops:
  1.5 1.9 collective-permute-start
  3.4 3.3 collective-permute-start.1
  10.7 2.9 collective-permute-start.8
  15.7 2.8 collective-permute-start.5
  20.0 2.3 collective-permute-done.4.refs_2_
  23.8 14.7 %collective-permute-done.9.near = bf16[2,9,128,128]{3,2,1,0:T(8,128)(2,1)S(1)} collective-permute-done((bf16[2,9,128,128]{3,2,1,0:T(8,128)(2,1)S(1)}, bf16[2,9,128,128]{3,2,1,0:T(8,128)(2,1)S(1)}, u32[]{:S(2)}, u32[]{:S(2)}) %collective-permute-start.9) | collective-permute-done | bytes 589856 | tf_op jit(solution)/shard_map/ppermute | solution.py:239
  38.5 1.6 collective-permute-start.25
  40.6 1.6 collective-permute-start.21
  42.7 9.2 %collective-permute-done.10.near = bf16[2,9,128,128]{3,2,1,0:T(8,128)(2,1)S(1)} collective-permute-done((bf16[2,9,128,128]{3,2,1,0:T(8,128)(2,1)S(1)}, bf16[2,9,128,128]{3,2,1,0:T(8,128)(2,1)S(1)}, u32[]{:S(2)}, u32[]{:S(2)}) %collective-permute-start.10) | collective-permute-done | bytes 589856 | tf_op jit(solution)/shard_map/ppermute | solution.py:239
  52.6 2.1 collective-permute-done.25.down
  55.8 1.9 collective-permute-start.26
  58.9 8.5 %collective-permute-done.21.down = bf16[2,9,128,128]{3,2,1,0:T(8,128)(2,1)} collective-permute-done((bf16[2,9,128,128]{3,2,1,0:T(8,128)(2,1)S(1)}, bf16[2,9,128,128]{3,2,1,0:T(8,128)(2,1)}, u32[]{:S(2)}, u32[]{:S(2)}) %collective-permute-start.21) | collective-permute-done | bytes 589856 | tf_op jit(solution)/shard_map/ppermute | solution.py:236
  67.4 1.7 collective-permute-start.16
  70.1 1.9 collective-permute-start.27
  71.9 6.3 %collective-permute-done.11.near = bf16[2,9,128,128]{3,2,1,0:T(8,128)(2,1)S(1)} collective-permute-done((bf16[2,9,128,128]{3,2,1,0:T(8,128)(2,1)S(1)}, bf16[2,9,128,128]{3,2,1,0:T(8,128)(2,1)S(1)}, u32[]{:S(2)}, u32[]{:S(2)}) %collective-permute-start.11) | collective-permute-done | bytes 589856 | tf_op jit(solution)/shard_map/ppermute | solution.py:239
  79.8 6.4 %collective-permute-done.17.down = bf16[2,9,128,128]{3,2,1,0:T(8,128)(2,1)S(1)} collective-permute-done((bf16[2,9,128,128]{3,2,1,0:T(8,128)(2,1)S(1)}, bf16[2,9,128,128]{3,2,1,0:T(8,128)(2,1)S(1)}, u32[]{:S(2)}, u32[]{:S(2)}) %collective-permute-start.17) | collective-permute-done | bytes 589856 | tf_op jit(solution)/shard_map/ppermute | solution.py:236
  86.3 1.7 collective-permute-start.12
  88.4 10.5 %collective-permute-done.13.down = bf16[2,9,128,128]{3,2,1,0:T(8,128)(2,1)S(1)} collective-permute-done((bf16[2,9,128,128]{3,2,1,0:T(8,128)(2,1)S(1)}, bf16[2,9,128,128]{3,2,1,0:T(8,128)(2,1)S(1)}, u32[]{:S(2)}, u32[]{:S(2)}) %collective-permute-start.13) | collective-permute-done | bytes 589856 | tf_op jit(solution)/shard_map/ppermute | solution.py:236
  98.9 1.7 collective-permute-start.23
  101.1 1.7 collective-permute-start.19
  103.2 2.0 collective-permute-done.22.far0
  105.2 1.7 collective-permute-start.15
  108.7 3.8 assemble.4.rest_0_
  112.4 3.8 assemble.5.rest_0_
  116.2 3.8 assemble.6.rest_0_
  120.0 3.8 assemble.7
  126.1 6.1 %conv.7 = bf16[256,512]{1,0:T(8,128)(2,1)S(1)} custom-call(s32[1]{0:T(128)} %bitcast.25.on_ref, bf16[256,512]{1,0:T(8,128)(2,1)S(1)} %gn.7.own_ref, bf16[256,512]{1,0:T(8,128)(2,1)S(1)} %collective-permute-done.28.oth_ref, bf16[256,512]{1,0:T(8,128)(2,1)S(1)} %broadcast_select_fusion.r_0_.a_ref, bf16[3,3072,512]{2,1,0:T(8,128)(2,1)} %bitcast.81), custom_call_target="tpu_custom_call" | custom-call | tf_op jit(solution)/shard_map/conv/pallas_call | solution.py:316
  133.4 6.1 %collective-permute-done.29.r_0_.a_ref = bf16[256,512]{1,0:T(8,128)(2,1)S(1)} collective-permute-done((bf16[256,512]{1,0:T(8,128)(2,1)S(1)}, bf16[256,512]{1,0:T(8,128)(2,1)S(1)}, u32[]{:S(2)}, u32[]{:S(2)}) %collective-permute-start.29) | collective-permute-done | bytes 262176 | tf_op jit(solution)/shard_map/ppermute | solution.py:230
  142.2 2.0 conv.8
  144.9 12.7 %copy.13 = bf16[3,3,1024,512]{2,3,1,0:T(8,128)(2,1)} copy(bf16[3,3,1024,512]{3,2,1,0:T(8,128)(2,1)} %bitcast.83) | data formatting | bytes 18874368 | tf_op jit(solution)/shard_map/reshape | solution.py:350
  159.8 2.0 conv.9
  164.7 2.0 conv.10
  169.7 2.0 conv.11
  174.7 2.0 conv.12
  179.7 2.7 conv.13
  183.3 2.0 dgrad.8
  185.7 5.9 %collective-permute-done.45 = bf16[256,512]{1,0:T(8,128)(2,1)S(1)} collective-permute-done((bf16[256,512]{1,0:T(8,128)(2,1)S(1)}, bf16[256,512]{1,0:T(8,128)(2,1)S(1)}, u32[]{:S(2)}, u32[]{:S(2)}) %collective-permute-start.45) | collective-permute-done | bytes 262176 | tf_op jit(solution)/shard_map/ppermute | solution.py:230
  193.8 2.0 dgrad.9
  198.7 2.0 dgrad.10
  203.6 2.0 dgrad.11
  207.9 1.9 collective-permute-start.53
  209.8 1.9 collective-permute-start.54
  211.8 7.3 %collective-permute-done.52 = bf16[256,512]{1,0:T(8,128)(2,1)S(1)} collective-permute-done((bf16[256,512]{1,0:T(8,128)(2,1)S(1)}, bf16[256,512]{1,0:T(8,128)(2,1)S(1)}, u32[]{:S(2)}, u32[]{:S(2)}) %collective-permute-start.52) | collective-permute-done | bytes 262176 | tf_op jit(solution)/shard_map/ppermute | solution.py:239
  219.0 10.3 %collective-permute-done.53 = bf16[256,512]{1,0:T(8,128)(2,1)S(1)} collective-permute-done((bf16[256,512]{1,0:T(8,128)(2,1)S(1)}, bf16[256,512]{1,0:T(8,128)(2,1)S(1)}, u32[]{:S(2)}, u32[]{:S(2)}) %collective-permute-start.53) | collective-permute-done | bytes 262176 | tf_op jit(solution)/shard_map/ppermute | solution.py:239
  229.5 2.3 collective-permute-start.55
  232.0 1.8 collective-permute-start.57
  233.9 41.7 %collective-permute-done.55 = bf16[4,256,512]{2,1,0:T(8,128)(2,1)S(1)} collective-permute-done((bf16[4,256,512]{2,1,0:T(8,128)(2,1)S(1)}, bf16[4,256,512]{2,1,0:T(8,128)(2,1)S(1)}, u32[]{:S(2)}, u32[]{:S(2)}) %collective-permute-start.55) | collective-permute-done | bytes 1048608 | tf_op jit(solution)/shard_map/ppermute | solution.py:236
  275.8 1.9 collective-permute-done.57
  279.8 5.3 %collective-permute-done.58 = bf16[16,256,512]{2,1,0:T(8,128)(2,1)} collective-permute-done((bf16[16,256,512]{2,1,0:T(8,128)(2,1)S(1)}, bf16[16,256,512]{2,1,0:T(8,128)(2,1)}, u32[]{:S(2)}, u32[]{:S(2)}) %collective-permute-start.58) | collective-permute-done | bytes 4194336 | tf_op jit(solution)/shard_map/ppermute | solution.py:233
  285.1 2.0 dgrad.12
  290.1 2.0 dgrad.13
  295.1 2.0 dgrad.14
  301.3 81.8 %collective-permute-done.68 = bf16[256,512]{1,0:T(8,128)(2,1)} collective-permute-done((bf16[256,512]{1,0:T(8,128)(2,1)S(1)}, bf16[256,512]{1,0:T(8,128)(2,1)}, u32[]{:S(2)}, u32[]{:S(2)}) %collective-permute-start.68) | collective-permute-done | bytes 262176 | tf_op jit(solution)/shard_map/ppermute | solution.py:230
  383.1 63.4 %collective-permute-done.67 = bf16[256,512]{1,0:T(8,128)(2,1)} collective-permute-done((bf16[256,512]{1,0:T(8,128)(2,1)}, bf16[256,512]{1,0:T(8,128)(2,1)}, u32[]{:S(2)}, u32[]{:S(2)}) %collective-permute-start.67) | collective-permute-done | bytes 262176 | tf_op jit(solution)/shard_map/ppermute | solution.py:230
  448.0 3.9 collective-permute-start.71
  451.9 2.7 collective-permute-done.69
  456.2 6.1 %dgrad.15 = (f32[256,512]{1,0:T(8,128)S(1)}, bf16[256,512]{1,0:T(8,128)(2,1)S(1)}) custom-call(s32[1]{0:T(128)} %bitcast.25.on_ref, bf16[256,512]{1,0:T(8,128)(2,1)S(1)} %get-tuple-element.136.dy_ref.r_0_, bf16[3,1536,1024]{2,1,0:T(8,128)(2,1)} %bitcast.96), custom_call_target="tpu_custom_call" | custom-call | tf_op jit(solution)/shard_map/dgrad/pallas_call | solution.py:326
  463.1 1.9 collective-permute-start.76
  471.8 1.8 collective-permute-start.75
  473.6 4.7 collective-permute-done.77
  479.3 2.1 pad_maximum_fusion.1.dy_ref
  481.4 18.0 %dw.1 = f32[9,1024,128]{2,1,0:T(8,128)} custom-call(s32[2]{0:T(128)} %pad_add_fusion.5.idx_ref, bf16[4096,512]{1,0:T(8,128)(2,1)} %bitcast.97, bf16[4096,512]{1,0:T(8,128)(2,1)} %bitcast.49.oth_ref, bf16[16,256,128]{2,1,0:T(8,128)(2,1)} %pad_maximum_fusion.1.dy_ref), custom_call_target="tpu_custom_call" | custom-call | tf_op jit(solution)/shard_map/dw/pallas_call | solution.py:406
  501.0 2.9 collective-permute-start.80
  503.9 2.2 collective-permute-done.80
  (196 shorter events, 79.3 us)
Async XLA Ops:
  1.5 9.2 %collective-permute-start = (f32[2,128]{1,0:T(2,128)S(1)}, f32[2,128]{1,0:T(2,128)S(1)}, u32[]{:S(2)}, u32[]{:S(2)}) collective-permute-start(f32[2,128]{1,0:T(2,128)S(1)} %pad_maximum_fusion.4.refs_0_), channel_id=1, source_target_pairs={{0,2},{1,3},{2,4},{3,5},{4,6},{5,7},{6,0},{7,1},{8,10},{9,11},{10,... | collective-permute-start | bytes 3080 | tf_op jit(solution)/shard_map/ppermute | solution.py:239
  3.4 10.2 %collective-permute-start.1 = (f32[2,128]{1,0:T(2,128)S(1)}, f32[2,128]{1,0:T(2,128)S(1)}, u32[]{:S(2)}, u32[]{:S(2)}) collective-permute-start(f32[2,128]{1,0:T(2,128)S(1)} %pad_maximum_fusion.4.refs_0_), channel_id=1, source_target_pairs={{0,4},{1,5},{2,6},{3,7},{4,0},{5,1},{6,2},{7,3},{8,12},{9,13},{10,... | collective-permute-start | bytes 3080 | tf_op jit(solution)/shard_map/ppermute | solution.py:239
  6.7 7.6 %collective-permute-start.2 = (f32[2,128]{1,0:T(2,128)S(1)}, f32[2,128]{1,0:T(2,128)S(1)}, u32[]{:S(2)}, u32[]{:S(2)}) collective-permute-start(f32[2,128]{1,0:T(2,128)S(1)} %pad_maximum_fusion.4.refs_0_), channel_id=1, source_target_pairs={{0,6},{1,7},{2,0},{3,1},{4,2},{5,3},{6,4},{7,5},{8,14},{9,15},{10,... | collective-permute-start | bytes 3080 | tf_op jit(solution)/shard_map/ppermute | solution.py:239
  8.6 7.1 %collective-permute-start.6 = (bf16[256,128]{1,0:T(8,128)(2,1)S(1)}, bf16[256,128]{1,0:T(8,128)(2,1)S(1)}, u32[]{:S(2)}, u32[]{:S(2)}) collective-permute-start(bf16[256,128]{1,0:T(8,128)(2,1)S(1)} %get-tuple-element.162), channel_id=1, source_target_pairs={{0,2},{1,3},{2,4},{3,5},{4,6},{5,7},{6,0},{7,1},{8,10},{9,11},{10,... | collective-permute-start | bytes 196616 | tf_op jit(solution)/shard_map/ppermute | solution.py:239
  9.7 8.9 %collective-permute-start.7 = (bf16[256,128]{1,0:T(8,128)(2,1)S(1)}, bf16[256,128]{1,0:T(8,128)(2,1)S(1)}, u32[]{:S(2)}, u32[]{:S(2)}) collective-permute-start(bf16[256,128]{1,0:T(8,128)(2,1)S(1)} %get-tuple-element.164), channel_id=1, source_target_pairs={{0,4},{1,5},{2,6},{3,7},{4,0},{5,1},{6,2},{7,3},{8,12},{9,13},{10,... | collective-permute-start | bytes 196616 | tf_op jit(solution)/shard_map/ppermute | solution.py:239
  10.7 8.0 %collective-permute-start.8 = (bf16[256,128]{1,0:T(8,128)(2,1)S(1)}, bf16[256,128]{1,0:T(8,128)(2,1)S(1)}, u32[]{:S(2)}, u32[]{:S(2)}) collective-permute-start(bf16[256,128]{1,0:T(8,128)(2,1)S(1)} %get-tuple-element.161), channel_id=1, source_target_pairs={{0,6},{1,7},{2,0},{3,1},{4,2},{5,3},{6,4},{7,5},{8,14},{9,15},{10,... | collective-permute-start | bytes 196616 | tf_op jit(solution)/shard_map/ppermute | solution.py:239
  13.6 6.4 %collective-permute-start.3 = (bf16[256,128]{1,0:T(8,128)(2,1)S(1)}, bf16[256,128]{1,0:T(8,128)(2,1)S(1)}, u32[]{:S(2)}, u32[]{:S(2)}) collective-permute-start(bf16[256,128]{1,0:T(8,128)(2,1)S(1)} %get-tuple-element.166), channel_id=1, source_target_pairs={{0,2},{1,3},{2,4},{3,5},{4,6},{5,7},{6,0},{7,1},{8,10},{9,11},{10,... | collective-permute-start | bytes 196616 | tf_op jit(solution)/shard_map/ppermute | solution.py:239
  14.3 8.1 %collective-permute-start.4 = (bf16[256,128]{1,0:T(8,128)(2,1)S(1)}, bf16[256,128]{1,0:T(8,128)(2,1)S(1)}, u32[]{:S(2)}, u32[]{:S(2)}) collective-permute-start(bf16[256,128]{1,0:T(8,128)(2,1)S(1)} %get-tuple-element.168), channel_id=1, source_target_pairs={{0,4},{1,5},{2,6},{3,7},{4,0},{5,1},{6,2},{7,3},{8,12},{9,13},{10,... | collective-permute-start | bytes 196616 | tf_op jit(solution)/shard_map/ppermute | solution.py:239
  15.7 6.6 %collective-permute-start.5 = (bf16[256,128]{1,0:T(8,128)(2,1)S(1)}, bf16[256,128]{1,0:T(8,128)(2,1)S(1)}, u32[]{:S(2)}, u32[]{:S(2)}) collective-permute-start(bf16[256,128]{1,0:T(8,128)(2,1)S(1)} %get-tuple-element.165), channel_id=1, source_target_pairs={{0,6},{1,7},{2,0},{3,1},{4,2},{5,3},{6,4},{7,5},{8,14},{9,15},{10,... | collective-permute-start | bytes 196616 | tf_op jit(solution)/shard_map/ppermute | solution.py:239
  22.3 16.2 %collective-permute-start.9 = (bf16[2,9,128,128]{3,2,1,0:T(8,128)(2,1)S(1)}, bf16[2,9,128,128]{3,2,1,0:T(8,128)(2,1)S(1)}, u32[]{:S(2)}, u32[]{:S(2)}) collective-permute-start(bf16[2,9,128,128]{3,2,1,0:T(8,128)(2,1)S(1)} %bitcast.74), channel_id=1, source_target_pairs={{0,2},{1,3},{2,4},{3,5},{4,6},{5,7},{6,0},{7,1},{8,10},{9,11},{10,... | collective-permute-start | bytes 1769480 | tf_op jit(solution)/shard_map/ppermute | solution.py:239
  38.5 13.5 %collective-permute-start.10 = (bf16[2,9,128,128]{3,2,1,0:T(8,128)(2,1)S(1)}, bf16[2,9,128,128]{3,2,1,0:T(8,128)(2,1)S(1)}, u32[]{:S(2)}, u32[]{:S(2)}) collective-permute-start(bf16[2,9,128,128]{3,2,1,0:T(8,128)(2,1)S(1)} %bitcast.75), channel_id=1, source_target_pairs={{0,6},{1,7},{2,0},{3,1},{4,2},{5,3},{6,4},{7,5},{8,14},{9,15},{10,... | collective-permute-start | bytes 1769480 | tf_op jit(solution)/shard_map/ppermute | solution.py:239
  38.5 16.3 %collective-permute-start.25 = (bf16[2,9,128,128]{3,2,1,0:T(8,128)(2,1)S(1)}, bf16[2,9,128,128]{3,2,1,0:T(8,128)(2,1)}, u32[]{:S(2)}, u32[]{:S(2)}) collective-permute-start(bf16[2,9,128,128]{3,2,1,0:T(8,128)(2,1)S(1)} %bitcast.76), channel_id=1, source_target_pairs={{0,64},{64,128},{128,192},{192,0},{1,65},{65,129},{129,193},{193,1... | collective-permute-start | bytes 1769480 | tf_op jit(solution)/shard_map/ppermute | solution.py:236
  40.1 17.6 %collective-permute-start.24 = (bf16[2,9,128,128]{3,2,1,0:T(8,128)(2,1)S(1)}, bf16[2,9,128,128]{3,2,1,0:T(8,128)(2,1)S(1)}, u32[]{:S(2)}, u32[]{:S(2)}) collective-permute-start(bf16[2,9,128,128]{3,2,1,0:T(8,128)(2,1)S(1)} %bitcast.77), channel_id=1, source_target_pairs={{0,192},{64,0},{128,64},{192,128},{1,193},{65,1},{129,65},{193,129... | collective-permute-start | bytes 1769480 | tf_op jit(solution)/shard_map/ppermute | solution.py:236
  40.6 26.8 %collective-permute-start.21 = (bf16[2,9,128,128]{3,2,1,0:T(8,128)(2,1)S(1)}, bf16[2,9,128,128]{3,2,1,0:T(8,128)(2,1)}, u32[]{:S(2)}, u32[]{:S(2)}) collective-permute-start(bf16[2,9,128,128]{3,2,1,0:T(8,128)(2,1)S(1)} %collective-permute-done.9.near), channel_id=1, source_target_pairs={{0,64},{64,128},{128,192},{192,0},{1,65},{65,129},{129,193},{193,1... | collective-permute-start | bytes 1769480 | tf_op jit(solution)/shard_map/ppermute | solution.py:236
  42.3 27.8 %collective-permute-start.20 = (bf16[2,9,128,128]{3,2,1,0:T(8,128)(2,1)S(1)}, bf16[2,9,128,128]{3,2,1,0:T(8,128)(2,1)S(1)}, u32[]{:S(2)}, u32[]{:S(2)}) collective-permute-start(bf16[2,9,128,128]{3,2,1,0:T(8,128)(2,1)S(1)} %collective-permute-done.9.near), channel_id=1, source_target_pairs={{0,192},{64,0},{128,64},{192,128},{1,193},{65,1},{129,65},{193,129... | collective-permute-start | bytes 1769480 | tf_op jit(solution)/shard_map/ppermute | solution.py:236
  52.0 26.3 %collective-permute-start.11 = (bf16[2,9,128,128]{3,2,1,0:T(8,128)(2,1)S(1)}, bf16[2,9,128,128]{3,2,1,0:T(8,128)(2,1)S(1)}, u32[]{:S(2)}, u32[]{:S(2)}) collective-permute-start(bf16[2,9,128,128]{3,2,1,0:T(8,128)(2,1)S(1)} %bitcast.78), channel_id=1, source_target_pairs={{0,4},{1,5},{2,6},{3,7},{4,0},{5,1},{6,2},{7,3},{8,12},{9,13},{10,... | collective-permute-start | bytes 1769480 | tf_op jit(solution)/shard_map/ppermute | solution.py:239
  55.8 45.3 %collective-permute-start.26 = (bf16[9,128,128]{2,1,0:T(8,128)(2,1)S(1)}, bf16[9,128,128]{2,1,0:T(8,128)(2,1)S(1)}, u32[]{:S(2)}, u32[]{:S(2)}) collective-permute-start(bf16[9,128,128]{2,1,0:T(8,128)(2,1)S(1)} %slice_bitcast_fusion.1), channel_id=1, source_target_pairs={{0,64},{64,128},{128,192},{192,0},{1,65},{65,129},{129,193},{193,1... | collective-permute-start | bytes 884744 | tf_op jit(solution)/shard_map/ppermute | solution.py:236
  57.6 28.6 %collective-permute-start.17 = (bf16[2,9,128,128]{3,2,1,0:T(8,128)(2,1)S(1)}, bf16[2,9,128,128]{3,2,1,0:T(8,128)(2,1)S(1)}, u32[]{:S(2)}, u32[]{:S(2)}) collective-permute-start(bf16[2,9,128,128]{3,2,1,0:T(8,128)(2,1)S(1)} %collective-permute-done.10.near), channel_id=1, source_target_pairs={{0,64},{64,128},{128,192},{192,0},{1,65},{65,129},{129,193},{193,1... | collective-permute-start | bytes 1769480 | tf_op jit(solution)/shard_map/ppermute | solution.py:236
  67.4 20.5 %collective-permute-start.16 = (bf16[2,9,128,128]{3,2,1,0:T(8,128)(2,1)S(1)}, bf16[2,9,128,128]{3,2,1,0:T(8,128)(2,1)S(1)}, u32[]{:S(2)}, u32[]{:S(2)}) collective-permute-start(bf16[2,9,128,128]{3,2,1,0:T(8,128)(2,1)S(1)} %collective-permute-done.10.near), channel_id=1, source_target_pairs={{0,192},{64,0},{128,64},{192,128},{1,193},{65,1},{129,65},{193,129... | collective-permute-start | bytes 1769480 | tf_op jit(solution)/shard_map/ppermute | solution.py:236
  70.1 32.8 %collective-permute-start.27 = (bf16[9,128,128]{2,1,0:T(8,128)(2,1)S(1)}, bf16[9,128,128]{2,1,0:T(8,128)(2,1)S(1)}, u32[]{:S(2)}, u32[]{:S(2)}) collective-permute-start(bf16[9,128,128]{2,1,0:T(8,128)(2,1)S(1)} %slice_bitcast_fusion), channel_id=1, source_target_pairs={{0,192},{64,0},{128,64},{192,128},{1,193},{65,1},{129,65},{193,129... | collective-permute-start | bytes 884744 | tf_op jit(solution)/shard_map/ppermute | solution.py:236
  78.2 20.7 %collective-permute-start.13 = (bf16[2,9,128,128]{3,2,1,0:T(8,128)(2,1)S(1)}, bf16[2,9,128,128]{3,2,1,0:T(8,128)(2,1)S(1)}, u32[]{:S(2)}, u32[]{:S(2)}) collective-permute-start(bf16[2,9,128,128]{3,2,1,0:T(8,128)(2,1)S(1)} %collective-permute-done.11.near), channel_id=1, source_target_pairs={{0,64},{64,128},{128,192},{192,0},{1,65},{65,129},{129,193},{193,1... | collective-permute-start | bytes 1769480 | tf_op jit(solution)/shard_map/ppermute | solution.py:236
  86.3 14.3 %collective-permute-start.12 = (bf16[2,9,128,128]{3,2,1,0:T(8,128)(2,1)S(1)}, bf16[2,9,128,128]{3,2,1,0:T(8,128)(2,1)S(1)}, u32[]{:S(2)}, u32[]{:S(2)}) collective-permute-start(bf16[2,9,128,128]{3,2,1,0:T(8,128)(2,1)S(1)} %collective-permute-done.11.near), channel_id=1, source_target_pairs={{0,192},{64,0},{128,64},{192,128},{1,193},{65,1},{129,65},{193,129... | collective-permute-start | bytes 1769480 | tf_op jit(solution)/shard_map/ppermute | solution.py:236
  88.0 17.3 %collective-permute-start.22 = (bf16[9,128,128]{2,1,0:T(8,128)(2,1)S(1)}, bf16[9,128,128]{2,1,0:T(8,128)(2,1)S(1)}, u32[]{:S(2)}, u32[]{:S(2)}) collective-permute-start(bf16[9,128,128]{2,1,0:T(8,128)(2,1)S(1)} %slice_bitcast_fusion.3), channel_id=1, source_target_pairs={{0,64},{64,128},{128,192},{192,0},{1,65},{65,129},{129,193},{193,1... | collective-permute-start | bytes 884744 | tf_op jit(solution)/shard_map/ppermute | solution.py:236
  98.9 13.5 %collective-permute-start.23 = (bf16[9,128,128]{2,1,0:T(8,128)(2,1)S(1)}, bf16[9,128,128]{2,1,0:T(8,128)(2,1)S(1)}, u32[]{:S(2)}, u32[]{:S(2)}) collective-permute-start(bf16[9,128,128]{2,1,0:T(8,128)(2,1)S(1)} %slice_bitcast_fusion.2), channel_id=1, source_target_pairs={{0,192},{64,0},{128,64},{192,128},{1,193},{65,1},{129,65},{193,129... | collective-permute-start | bytes 884744 | tf_op jit(solution)/shard_map/ppermute | solution.py:236
  100.6 15.6 %collective-permute-start.18 = (bf16[9,128,128]{2,1,0:T(8,128)(2,1)S(1)}, bf16[9,128,128]{2,1,0:T(8,128)(2,1)S(1)}, u32[]{:S(2)}, u32[]{:S(2)}) collective-permute-start(bf16[9,128,128]{2,1,0:T(8,128)(2,1)S(1)} %slice_bitcast_fusion.5), channel_id=1, source_target_pairs={{0,64},{64,128},{128,192},{192,0},{1,65},{65,129},{129,193},{193,1... | collective-permute-start | bytes 884744 | tf_op jit(solution)/shard_map/ppermute | solution.py:236
  101.1 15.1 %collective-permute-start.19 = (bf16[9,128,128]{2,1,0:T(8,128)(2,1)S(1)}, bf16[9,128,128]{2,1,0:T(8,128)(2,1)S(1)}, u32[]{:S(2)}, u32[]{:S(2)}) collective-permute-start(bf16[9,128,128]{2,1,0:T(8,128)(2,1)S(1)} %slice_bitcast_fusion.4), channel_id=1, source_target_pairs={{0,192},{64,0},{128,64},{192,128},{1,193},{65,1},{129,65},{193,129... | collective-permute-start | bytes 884744 | tf_op jit(solution)/shard_map/ppermute | solution.py:236
  102.8 17.2 %collective-permute-start.14 = (bf16[9,128,128]{2,1,0:T(8,128)(2,1)S(1)}, bf16[9,128,128]{2,1,0:T(8,128)(2,1)S(1)}, u32[]{:S(2)}, u32[]{:S(2)}) collective-permute-start(bf16[9,128,128]{2,1,0:T(8,128)(2,1)S(1)} %slice_bitcast_fusion.7), channel_id=1, source_target_pairs={{0,64},{64,128},{128,192},{192,0},{1,65},{65,129},{129,193},{193,1... | collective-permute-start | bytes 884744 | tf_op jit(solution)/shard_map/ppermute | solution.py:236
  105.2 14.8 %collective-permute-start.15 = (bf16[9,128,128]{2,1,0:T(8,128)(2,1)S(1)}, bf16[9,128,128]{2,1,0:T(8,128)(2,1)S(1)}, u32[]{:S(2)}, u32[]{:S(2)}) collective-permute-start(bf16[9,128,128]{2,1,0:T(8,128)(2,1)S(1)} %slice_bitcast_fusion.6), channel_id=1, source_target_pairs={{0,192},{64,0},{128,64},{192,128},{1,193},{65,1},{129,65},{193,129... | collective-permute-start | bytes 884744 | tf_op jit(solution)/shard_map/ppermute | solution.py:236
  132.1 7.4 %collective-permute-start.29 = (bf16[256,512]{1,0:T(8,128)(2,1)S(1)}, bf16[256,512]{1,0:T(8,128)(2,1)S(1)}, u32[]{:S(2)}, u32[]{:S(2)}) collective-permute-start(bf16[256,512]{1,0:T(8,128)(2,1)S(1)} %conv.7), channel_id=1, source_target_pairs={{0,8},{1,9},{2,10},{3,11},{4,12},{5,13},{6,14},{7,15},{64,72},{65,... | collective-permute-start | bytes 786440 | tf_op jit(solution)/shard_map/ppermute | solution.py:230
  140.2 2.0 collective-permute-start.30
  144.2 13.4 %collective-permute-start.31 = (bf16[256,512]{1,0:T(8,128)(2,1)S(1)}, bf16[256,512]{1,0:T(8,128)(2,1)S(1)}, u32[]{:S(2)}, u32[]{:S(2)}) collective-permute-start(bf16[256,512]{1,0:T(8,128)(2,1)S(1)} %conv.8), channel_id=1, source_target_pairs={{8,16},{9,17},{10,18},{11,19},{12,20},{13,21},{14,22},{15,23},{72,... | collective-permute-start | bytes 786440 | tf_op jit(solution)/shard_map/ppermute | solution.py:230
  158.2 1.6 collective-permute-start.33
  163.1 1.6 collective-permute-start.35
  168.0 1.6 collective-permute-start.37
  168.3 4.1 collective-permute-start.39
  173.1 1.6 collective-permute-start.40
  173.3 4.1 collective-permute-start.42
  178.3 13.3 %collective-permute-start.45 = (bf16[256,512]{1,0:T(8,128)(2,1)S(1)}, bf16[256,512]{1,0:T(8,128)(2,1)S(1)}, u32[]{:S(2)}, u32[]{:S(2)}) collective-permute-start(bf16[256,512]{1,0:T(8,128)(2,1)S(1)} %conv.7), channel_id=1, source_target_pairs={{0,62},{1,63},{2,60},{3,61},{4,58},{5,59},{6,56},{7,57},{64,126},{... | collective-permute-start | bytes 786440 | tf_op jit(solution)/shard_map/ppermute | solution.py:230
  182.4 9.2 %collective-permute-start.44 = (bf16[256,512]{1,0:T(8,128)(2,1)}, bf16[256,512]{1,0:T(8,128)(2,1)S(1)}, u32[]{:S(2)}, u32[]{:S(2)}) collective-permute-start(bf16[256,512]{1,0:T(8,128)(2,1)} %conv.13), channel_id=1, source_target_pairs={{48,56},{49,57},{50,58},{51,59},{52,60},{53,61},{54,62},{55,63},{1... | collective-permute-start | bytes 786440 | tf_op jit(solution)/shard_map/ppermute | solution.py:230
  185.3 7.2 %collective-permute-start.32 = (bf16[256,512]{1,0:T(8,128)(2,1)S(1)}, bf16[256,512]{1,0:T(8,128)(2,1)S(1)}, u32[]{:S(2)}, u32[]{:S(2)}) collective-permute-start(bf16[256,512]{1,0:T(8,128)(2,1)S(1)} %get-tuple-element.102), channel_id=1, source_target_pairs={{0,1},{1,0},{2,3},{3,2},{4,5},{5,4},{6,7},{7,6},{8,9},{9,8},{10,11... | collective-permute-start | bytes 786440 | tf_op jit(solution)/shard_map/ppermute | solution.py:233
  207.8 11.2 %collective-permute-start.52 = (bf16[256,512]{1,0:T(8,128)(2,1)S(1)}, bf16[256,512]{1,0:T(8,128)(2,1)S(1)}, u32[]{:S(2)}, u32[]{:S(2)}) collective-permute-start(bf16[256,512]{1,0:T(8,128)(2,1)S(1)} %get-tuple-element.121), channel_id=1, source_target_pairs={{0,2},{1,3},{2,4},{3,5},{4,6},{5,7},{6,0},{7,1},{8,10},{9,11},{10,... | collective-permute-start | bytes 786440 | tf_op jit(solution)/shard_map/ppermute | solution.py:239
  207.9 21.4 %collective-permute-start.53 = (bf16[256,512]{1,0:T(8,128)(2,1)S(1)}, bf16[256,512]{1,0:T(8,128)(2,1)S(1)}, u32[]{:S(2)}, u32[]{:S(2)}) collective-permute-start(bf16[256,512]{1,0:T(8,128)(2,1)S(1)} %get-tuple-element.121), channel_id=1, source_target_pairs={{0,4},{1,5},{2,6},{3,7},{4,0},{5,1},{6,2},{7,3},{8,12},{9,13},{10,... | collective-permute-start | bytes 786440 | tf_op jit(solution)/shard_map/ppermute | solution.py:239
  209.8 19.5 %collective-permute-start.54 = (bf16[256,512]{1,0:T(8,128)(2,1)S(1)}, bf16[256,512]{1,0:T(8,128)(2,1)S(1)}, u32[]{:S(2)}, u32[]{:S(2)}) collective-permute-start(bf16[256,512]{1,0:T(8,128)(2,1)S(1)} %get-tuple-element.121), channel_id=1, source_target_pairs={{0,6},{1,7},{2,0},{3,1},{4,2},{5,3},{6,4},{7,5},{8,14},{9,15},{10,... | collective-permute-start | bytes 786440 | tf_op jit(solution)/shard_map/ppermute | solution.py:239
  229.5 46.1 %collective-permute-start.55 = (bf16[4,256,512]{2,1,0:T(8,128)(2,1)S(1)}, bf16[4,256,512]{2,1,0:T(8,128)(2,1)S(1)}, u32[]{:S(2)}, u32[]{:S(2)}) collective-permute-start(bf16[4,256,512]{2,1,0:T(8,128)(2,1)S(1)} %pad_maximum_fusion), channel_id=1, source_target_pairs={{0,192},{64,0},{128,64},{192,128},{1,193},{65,1},{129,65},{193,129... | collective-permute-start | bytes 3145736 | tf_op jit(solution)/shard_map/ppermute | solution.py:236
  231.8 43.9 %collective-permute-start.56 = (bf16[4,256,512]{2,1,0:T(8,128)(2,1)S(1)}, bf16[4,256,512]{2,1,0:T(8,128)(2,1)S(1)}, u32[]{:S(2)}, u32[]{:S(2)}) collective-permute-start(bf16[4,256,512]{2,1,0:T(8,128)(2,1)S(1)} %pad_maximum_fusion), channel_id=1, source_target_pairs={{0,128},{64,192},{128,0},{192,64},{1,129},{65,193},{129,1},{193,65... | collective-permute-start | bytes 3145736 | tf_op jit(solution)/shard_map/ppermute | solution.py:236
  232.0 45.6 %collective-permute-start.57 = (bf16[4,256,512]{2,1,0:T(8,128)(2,1)S(1)}, bf16[4,256,512]{2,1,0:T(8,128)(2,1)S(1)}, u32[]{:S(2)}, u32[]{:S(2)}) collective-permute-start(bf16[4,256,512]{2,1,0:T(8,128)(2,1)S(1)} %pad_maximum_fusion), channel_id=1, source_target_pairs={{0,64},{64,128},{128,192},{192,0},{1,65},{65,129},{129,193},{193,1... | collective-permute-start | bytes 3145736 | tf_op jit(solution)/shard_map/ppermute | solution.py:236
  277.7 7.4 %collective-permute-start.58 = (bf16[16,256,512]{2,1,0:T(8,128)(2,1)S(1)}, bf16[16,256,512]{2,1,0:T(8,128)(2,1)}, u32[]{:S(2)}, u32[]{:S(2)}) collective-permute-start(bf16[16,256,512]{2,1,0:T(8,128)(2,1)S(1)} %constant_dynamic-update-slice_fusion), channel_id=1, source_target_pairs={{0,1},{1,0},{2,3},{3,2},{4,5},{5,4},{6,7},{7,6},{8,9},{9,8},{10,11... | collective-permute-start | bytes 12582920 | tf_op jit(solution)/shard_map/ppermute | solution.py:233
  287.3 2.6 collective-permute-start.62
  292.3 2.6 collective-permute-start.65
  297.3 85.7 %collective-permute-start.68 = (bf16[256,512]{1,0:T(8,128)(2,1)S(1)}, bf16[256,512]{1,0:T(8,128)(2,1)}, u32[]{:S(2)}, u32[]{:S(2)}) collective-permute-start(bf16[256,512]{1,0:T(8,128)(2,1)S(1)} %get-tuple-element.108), channel_id=1, source_target_pairs={{56,6},{57,7},{58,4},{59,5},{60,2},{61,3},{62,0},{63,1},{120,70},{... | collective-permute-start | bytes 786440 | tf_op jit(solution)/shard_map/ppermute | solution.py:230
  300.0 146.5 %collective-permute-start.67 = (bf16[256,512]{1,0:T(8,128)(2,1)}, bf16[256,512]{1,0:T(8,128)(2,1)}, u32[]{:S(2)}, u32[]{:S(2)}) collective-permute-start(bf16[256,512]{1,0:T(8,128)(2,1)} %get-tuple-element.135), channel_id=1, source_target_pairs={{8,0},{9,1},{10,2},{11,3},{12,4},{13,5},{14,6},{15,7},{72,64},{73,... | collective-permute-start | bytes 786440 | tf_op jit(solution)/shard_map/ppermute | solution.py:230
  447.8 6.8 %collective-permute-start.69 = (bf16[256,128]{1,0:T(8,128)(2,1)S(1)}, bf16[256,128]{1,0:T(8,128)(2,1)S(1)}, u32[]{:S(2)}, u32[]{:S(2)}) collective-permute-start(bf16[256,128]{1,0:T(8,128)(2,1)S(1)} %get-tuple-element.160), channel_id=1, source_target_pairs={{0,2},{1,3},{2,4},{3,5},{4,6},{5,7},{6,0},{7,1},{8,10},{9,11},{10,... | collective-permute-start | bytes 196616 | tf_op jit(solution)/shard_map/ppermute | solution.py:239
  447.9 8.3 %collective-permute-start.70 = (bf16[256,128]{1,0:T(8,128)(2,1)S(1)}, bf16[256,128]{1,0:T(8,128)(2,1)S(1)}, u32[]{:S(2)}, u32[]{:S(2)}) collective-permute-start(bf16[256,128]{1,0:T(8,128)(2,1)S(1)} %get-tuple-element.159), channel_id=1, source_target_pairs={{0,4},{1,5},{2,6},{3,7},{4,0},{5,1},{6,2},{7,3},{8,12},{9,13},{10,... | collective-permute-start | bytes 196616 | tf_op jit(solution)/shard_map/ppermute | solution.py:239
  448.0 8.2 %collective-permute-start.71 = (bf16[256,128]{1,0:T(8,128)(2,1)S(1)}, bf16[256,128]{1,0:T(8,128)(2,1)S(1)}, u32[]{:S(2)}, u32[]{:S(2)}) collective-permute-start(bf16[256,128]{1,0:T(8,128)(2,1)S(1)} %get-tuple-element.158), channel_id=1, source_target_pairs={{0,6},{1,7},{2,0},{3,1},{4,2},{5,3},{6,4},{7,5},{8,14},{9,15},{10,... | collective-permute-start | bytes 196616 | tf_op jit(solution)/shard_map/ppermute | solution.py:239
  462.3 5.1 %collective-permute-start.72 = (bf16[256,512]{1,0:T(8,128)(2,1)S(1)}, bf16[256,512]{1,0:T(8,128)(2,1)S(1)}, u32[]{:S(2)}, u32[]{:S(2)}) collective-permute-start(bf16[256,512]{1,0:T(8,128)(2,1)S(1)} %get-tuple-element.138), channel_id=1, source_target_pairs={{0,1},{1,0},{2,3},{3,2},{4,5},{5,4},{6,7},{7,6},{8,9},{9,8},{10,11... | collective-permute-start | bytes 786440 | tf_op jit(solution)/shard_map/ppermute | solution.py:233
  463.1 8.7 %collective-permute-start.76 = (bf16[4,256,128]{2,1,0:T(8,128)(2,1)S(1)}, bf16[4,256,128]{2,1,0:T(8,128)(2,1)S(1)}, u32[]{:S(2)}, u32[]{:S(2)}) collective-permute-start(bf16[4,256,128]{2,1,0:T(8,128)(2,1)S(1)} %pad_maximum_fusion.2), channel_id=1, source_target_pairs={{0,192},{64,0},{128,64},{192,128},{1,193},{65,1},{129,65},{193,129... | collective-permute-start | bytes 786440 | tf_op jit(solution)/shard_map/ppermute | solution.py:236
  465.0 13.2 %collective-permute-start.77 = (bf16[4,256,128]{2,1,0:T(8,128)(2,1)S(1)}, bf16[4,256,128]{2,1,0:T(8,128)(2,1)S(1)}, u32[]{:S(2)}, u32[]{:S(2)}) collective-permute-start(bf16[4,256,128]{2,1,0:T(8,128)(2,1)S(1)} %pad_maximum_fusion.2), channel_id=1, source_target_pairs={{0,128},{64,192},{128,0},{192,64},{1,129},{65,193},{129,1},{193,65... | collective-permute-start | bytes 786440 | tf_op jit(solution)/shard_map/ppermute | solution.py:236
  466.0 13.4 %collective-permute-start.78 = (bf16[4,256,128]{2,1,0:T(8,128)(2,1)S(1)}, bf16[4,256,128]{2,1,0:T(8,128)(2,1)}, u32[]{:S(2)}, u32[]{:S(2)}) collective-permute-start(bf16[4,256,128]{2,1,0:T(8,128)(2,1)S(1)} %pad_maximum_fusion.2), channel_id=1, source_target_pairs={{0,64},{64,128},{128,192},{192,0},{1,65},{65,129},{129,193},{193,1... | collective-permute-start | bytes 786440 | tf_op jit(solution)/shard_map/ppermute | solution.py:236
  468.7 30.7 %collective-permute-start.73 = (f32[2,128]{1,0:T(2,128)S(1)}, f32[2,128]{1,0:T(2,128)S(1)}, u32[]{:S(2)}, u32[]{:S(2)}) collective-permute-start(f32[2,128]{1,0:T(2,128)S(1)} %bitcast.109), channel_id=1, source_target_pairs={{0,2},{1,3},{2,4},{3,5},{4,6},{5,7},{6,0},{7,1},{8,10},{9,11},{10,... | collective-permute-start | bytes 3080 | tf_op jit(solution)/shard_map/ppermute | solution.py:239
  470.2 29.3 %collective-permute-start.74 = (f32[2,128]{1,0:T(2,128)S(1)}, f32[2,128]{1,0:T(2,128)S(1)}, u32[]{:S(2)}, u32[]{:S(2)}) collective-permute-start(f32[2,128]{1,0:T(2,128)S(1)} %bitcast.108), channel_id=1, source_target_pairs={{0,4},{1,5},{2,6},{3,7},{4,0},{5,1},{6,2},{7,3},{8,12},{9,13},{10,... | collective-permute-start | bytes 3080 | tf_op jit(solution)/shard_map/ppermute | solution.py:239
  471.8 27.7 %collective-permute-start.75 = (f32[2,128]{1,0:T(2,128)S(1)}, f32[2,128]{1,0:T(2,128)S(1)}, u32[]{:S(2)}, u32[]{:S(2)}) collective-permute-start(f32[2,128]{1,0:T(2,128)S(1)} %bitcast.107), channel_id=1, source_target_pairs={{0,6},{1,7},{2,0},{3,1},{4,2},{5,3},{6,4},{7,5},{8,14},{9,15},{10,... | collective-permute-start | bytes 3080 | tf_op jit(solution)/shard_map/ppermute | solution.py:239
  499.5 4.4 collective-permute-start.79
  501.0 5.1 collective-permute-start.80
  503.9 3.6 collective-permute-start.81
  (23 other events, 106.1 us)
